TPU v7x, 32 devices: a whole 2x2x4 slice. The times are simulated.
32 devices in a mesh: uv: 8 (over y, x, core), tm: 4 (over z).
Axes of the slice: x: 2, y: 2, z: 4, core: 2. Of those that a mesh axis runs over, the one named last changes fastest.
Arguments:
- visibilities: bfloat16 [8, 128, 16384], P(None, 'uv', 'tm'), may hold values from -0.75 to 0.75
- positions: float32 [2, 128, 16384], P(None, 'uv', 'tm'), may hold values from 4 to 60
- owner: int32 [128, 1], P('uv'), may hold values from 0 to 7; in each aligned block of 16 rows (0 to 15, 16 to 31, ...) at most 4 rows name the same one
- w_plane: int32 [128], P('uv'), may hold values from 0 to 7
- row_offset: int32 [128], P('uv'), may hold values from 0 to 127
- col_offset: int32 [128], P('uv'), may hold values from 0 to 1984
Outputs:
- grid: float32 [8, 8, 1024, 2048], P('tm', None, 'uv')
Inputs may be any that keep to these rules, and one draw needn't show every extreme that they name: `owner`: among the 16 subgrids of one index of uv (aligned blocks of rows), no tile is named by more than 4 of them.
All inputs are finite; a program needn't handle non-finite values.
Results may differ from a plain program's by a relative error of at most 0.0037.
Values may be sent and summed in bfloat16 or wider, within the bound.
No kernel may reach another device: no remote copies, remote signals or barrier semaphores. Data moves between devices by JAX's collectives and lax.ppermute only.
A program may use at most 128 MiB of HBM per device.

v0:
```python
import functools

import jax
import jax.numpy as jnp
from jax import lax
from jax.experimental import pallas as pl
from jax.experimental.pallas import tpu as pltpu
from jax.sharding import PartitionSpec as P

W = 8
SUB = 64
TAPS = 8
TU = 128
NV = 2048
LANES = 128
SUBLANES = 8
BLOCKS = NV // LANES
META = 16
STEP = 4

VMEM = pl.BlockSpec(memory_space=pltpu.VMEM)
SMEM = pl.BlockSpec(memory_space=pltpu.SMEM)
ANY = pl.BlockSpec(memory_space=pl.ANY)


def taper(scaled):
    inner = jnp.maximum(0.0, 1.0 - scaled * scaled)
    return inner * inner


def grid_kernel(me_ref, values_ref, places_ref, *rest, peers, blanks, orders):
    parts_refs, rest = rest[orders : orders + peers], rest[orders + peers :]
    zero_copies = []
    if blanks:
        out_ref, values_wide, sums, blank, sem, values, places, in_sem = rest
        _, sub_count, row_count = values.shape
        in_copies = [
            pltpu.make_async_copy(values_ref.at[:, pl.ds(0, sub_count), :], values, in_sem.at[0]),
            pltpu.make_async_copy(places_ref.at[:, pl.ds(0, sub_count), :], places, in_sem.at[1]),
        ]
        for copy in in_copies:
            copy.start()
        blank[...] = jnp.zeros(blank.shape, jnp.float32)
        zero_copies = [pltpu.make_async_copy(blank, out_ref.at[:, plane], sem.at[plane]) for plane in range(W)]
        for copy in in_copies:
            copy.wait()
        values_ref, places_ref = values, places
    else:
        values_wide, sums = rest
    for copy in zero_copies:
        copy.start()
    comp_count, sub_count, row_count = values_ref.shape
    kept = comp_count // peers * SUB
    for comp in range(comp_count):
        values_wide[comp * sub_count : (comp + 1) * sub_count, :] = values_ref[comp].astype(jnp.float32)
    cells = lax.broadcasted_iota(jnp.int32, (SUB, row_count), 0).astype(jnp.float32) * (2.0 / TAPS)

    def one_sub(sub):
        row_taps = taper(cells - places_ref[0, pl.ds(sub, 1), :] * (2.0 / TAPS)).astype(jnp.bfloat16)
        col_taps = taper(cells - places_ref[1, pl.ds(sub, 1), :] * (2.0 / TAPS))
        weighted = jnp.concatenate(
            [
                (values_wide[pl.ds(comp * sub_count + sub, 1), :] * col_taps).astype(jnp.bfloat16)
                for comp in range(comp_count)
            ],
            axis=0,
        )
        return lax.dot_general(
            weighted, row_taps, (((1,), (1,)), ((), ())), preferred_element_type=jnp.float32
        )

    def some_subs(turn, carry):
        for pair in range(STEP // 2):
            sub = turn * STEP + pair * 2
            sums[pair] = jnp.concatenate([one_sub(sub), one_sub(sub + 1)], axis=1).astype(jnp.bfloat16)
        for pair in range(STEP // 2):
            for mask, parts_ref in enumerate(parts_refs):
                rows = pl.ds(pl.multiple_of((me_ref[0] ^ mask) * kept, kept), kept)
                parts_ref[turn * (STEP // 2) + pair] = sums[pair, rows, :]
        return carry

    lax.fori_loop(0, sub_count // STEP, some_subs, 0)
    for copy in zero_copies:
        copy.wait()


def grid_parts(values, places, peers, chunk, sub_count, blanks, *order):
    comp_count, _, row_count = values.shape
    kept = comp_count // peers * SUB
    me = lax.axis_index("tm").astype(jnp.int32).reshape(1)
    parts_shape = (sub_count // 2, kept, LANES)
    values_block, places_block = (comp_count, sub_count, row_count), (2, sub_count, row_count)
    if blanks:
        in_specs = [ANY] * 2
    else:
        in_specs = [pl.BlockSpec(block, lambda i: (0, chunk, 0)) for block in (values_block, places_block)]
    scratch = [
        pltpu.VMEM((comp_count * sub_count, row_count), jnp.float32),
        pltpu.VMEM((STEP // 2, comp_count * SUB, LANES), jnp.bfloat16),
    ]
    if blanks:
        scratch += [
            pltpu.VMEM((kept // SUB, TU, NV), jnp.float32),
            pltpu.SemaphoreType.DMA((W,)),
            pltpu.VMEM(values_block, values.dtype),
            pltpu.VMEM(places_block, places.dtype),
            pltpu.SemaphoreType.DMA((2,)),
        ]
    return pl.pallas_call(
        functools.partial(grid_kernel, peers=peers, blanks=blanks, orders=len(order)),
        grid=(1,),
        out_shape=[jax.ShapeDtypeStruct(parts_shape, jnp.bfloat16)] * peers
        + [jax.ShapeDtypeStruct((kept // SUB, W, TU, NV), jnp.float32)] * blanks,
        in_specs=[SMEM] + in_specs + [ANY] * len(order),
        out_specs=[pl.BlockSpec(parts_shape, lambda i: (0, 0, 0))] * peers + [ANY] * blanks,
        scratch_shapes=scratch,
        compiler_params=pltpu.CompilerParams(vmem_limit_bytes=(60 if blanks else 48) << 20),
        cost_estimate=pl.CostEstimate(
            flops=8 * sub_count * row_count * SUB * SUB * comp_count,
            bytes_accessed=2 << 20,
            transcendentals=0,
        ),
    )(me, values, places, *order)


def sum_kernel(*refs, peers, hops, orders):
    parts_refs, hops_refs, rest = refs[:peers], refs[peers : peers + hops], refs[peers + hops + orders :]
    pairs = parts_refs[0].shape[0]
    out_ref = rest[0] if hops else rest[1]
    for pair in range(pairs):
        total = parts_refs[0][pair].astype(jnp.float32)
        for parts_ref in parts_refs[1:]:
            total = total + parts_ref[pair].astype(jnp.float32)
        out_ref[pair * 2 * SUB : (pair + 1) * 2 * SUB, :] = total.T.astype(jnp.bfloat16)
    if hops:
        for at, hop_ref in enumerate(hops_refs):
            rest[1][at] = hop_ref[: rest[1].shape[1], :]
    else:
        out_ref[pairs * 2 * SUB :, :] = rest[0][...].astype(jnp.bfloat16)


def sum_parts(parts, hops, order, *numbers):
    pairs, kept, _ = parts[0].shape
    rows = pairs * 2 * SUB + META * len(numbers)
    return pl.pallas_call(
        functools.partial(sum_kernel, peers=len(parts), hops=len(hops), orders=len(order)),
        out_shape=[jax.ShapeDtypeStruct((rows, kept), jnp.bfloat16)]
        + [jax.ShapeDtypeStruct((len(hops), rows, kept), jnp.bfloat16)] * len(hops[:1]),
        in_specs=[VMEM] * (len(parts) + len(hops)) + [ANY] * len(order) + [VMEM] * len(numbers),
        out_specs=[VMEM] * (1 + len(hops[:1])),
        compiler_params=pltpu.CompilerParams(vmem_limit_bytes=8 << 20),
        cost_estimate=pl.CostEstimate(flops=1 << 20, bytes_accessed=2 << 20, transcendentals=0),
    )(*parts, *hops, *order, *numbers)


def exchange(parts, axis):
    size = lax.axis_size(axis)
    far_first = [
        lax.ppermute(parts[mask], axis, [(i, i ^ mask) for i in range(size)]) for mask in range(size - 1, 0, -1)
    ]
    return [parts[0]] + far_first


def across(array, axis):
    size = lax.axis_size(axis)
    return [array] + [lax.ppermute(array, axis, [(i, i ^ mask) for i in range(size)]) for mask in range(2, size, 2)]


def beside(array, axis):
    size = lax.axis_size(axis)
    return lax.ppermute(array, axis, [(i, i ^ 1) for i in range(size)])


def touch_plan(starts, planes, cols, spots, others):
    total = starts.shape[0]
    ids = jnp.arange(total, dtype=jnp.int32)
    taken = starts >= 0
    keys = jnp.where(taken, planes, W) * total + ids
    left = jnp.where(taken, planes * BLOCKS + cols // LANES, -1)
    right = jnp.where(taken & (cols % LANES > LANES - SUB), left + 1, -2)
    before = keys[None, :] < keys[:, None]
    after = keys[None, :] > keys[:, None]
    rank = jnp.sum(before.astype(jnp.int32), axis=1)

    def edges(units):
        same = (left[None, :] == units[:, None]) | (right[None, :] == units[:, None])
        first = ~jnp.any(same & before, axis=1)
        last = ~jnp.any(same & after, axis=1)
        return first.astype(jnp.int32) + 2 * last.astype(jnp.int32)

    flags = edges(left) + jnp.where(right >= 0, 4 * edges(right), 0) + 16 * others
    fields = jnp.stack([starts, cols, planes, spots, flags], axis=0)
    moved = jnp.where(rank[None, None, :] == ids[None, :, None], fields[:, None, :], 0)
    table = jnp.sum(moved, axis=2)
    number = jnp.sum(taken.astype(jnp.int32))
    return jnp.concatenate([table, jnp.full((1, total), number, jnp.int32)], axis=0)


def place_kernel(table_ref, near_ref, other_ref, _, out_ref, canvas, sem):
    comp_count = canvas.shape[1]
    number = table_ref[5, 0]
    lane = lax.broadcasted_iota(jnp.int32, (SUB + SUBLANES, LANES), 1)

    def lanes_of(block):
        return pl.ds(pl.multiple_of(block * LANES, LANES), LANES)

    def out_copy(plane, block):
        return pltpu.make_async_copy(
            canvas.at[plane, :, pl.ds(SUB, TU), lanes_of(block)],
            out_ref.at[:, plane, :, lanes_of(block)],
            sem.at[plane, block],
        )

    def clear(plane, block):
        canvas[plane, :, pl.ds(SUB, TU), lanes_of(block)] = jnp.zeros((comp_count, TU, LANES), jnp.float32)

    def when_set(flags, bit, act):
        @pl.when((flags & bit) != 0)
        def _():
            act()

    def turn(index):
        start = table_ref[0, index]
        col = table_ref[1, index]
        block = table_ref[3, index] // (1 << 16)
        at = pl.ds(pl.multiple_of(table_ref[3, index] % (1 << 16), SUB), SUB)
        shift = col % LANES
        patch = jnp.where((table_ref[4, index] & 16) != 0, other_ref[block, at, :], near_ref[block, at, :])
        patch = patch.astype(jnp.float32)
        if patch.shape[1] < LANES:
            patch = jnp.concatenate([patch] * (LANES // patch.shape[1]), axis=1)
        patch = jnp.concatenate([patch, jnp.zeros((SUBLANES, patch.shape[1]), jnp.float32)], axis=0)
        patch = pltpu.roll(patch, start % SUBLANES, 0)
        return [
            pltpu.roll(
                patch[:, comp // 2 * LANES : (comp // 2 + 1) * LANES], (shift + comp % 2 * SUB) % LANES, 1
            )
            for comp in range(comp_count)
        ]

    def add_patch(index, turned):
        start = table_ref[0, index]
        col = table_ref[1, index]
        plane = table_ref[2, index]
        flags = table_ref[4, index]
        block = col // LANES
        shift = col % LANES
        rows = pl.ds(pl.multiple_of(start // SUBLANES * SUBLANES, SUBLANES), SUB + SUBLANES)
        when_set(flags, 1, lambda: clear(plane, block))
        here = (lane >= shift) & (lane < shift + SUB)
        for comp in range(comp_count):
            canvas[plane, comp, rows, lanes_of(block)] += jnp.where(here, turned[comp], 0.0)
        when_set(flags, 2, lambda: out_copy(plane, block).start())

        @pl.when(shift > LANES - SUB)
        def _():
            when_set(flags, 4, lambda: clear(plane, block + 1))
            for comp in range(comp_count):
                canvas[plane, comp, rows, lanes_of(block + 1)] += jnp.where(
                    lane < shift + SUB - LANES, turned[comp], 0.0
                )
            when_set(flags, 8, lambda: out_copy(plane, block + 1).start())

    def add_two(turn_index, carry):
        index = turn_index * 2
        first, second = turn(index), turn(index + 1)
        add_patch(index, first)

        @pl.when(index + 1 < number)
        def _():
            add_patch(index + 1, second)

        return carry

    def finish(index, carry):
        block = table_ref[1, index] // LANES
        plane = table_ref[2, index]
        flags = table_ref[4, index]
        when_set(flags, 2, lambda: out_copy(plane, block).wait())
        when_set(flags, 8, lambda: out_copy(plane, block + 1).wait())
        return carry

    lax.fori_loop(0, (number + 1) // 2, add_two, 0)
    lax.fori_loop(0, number, finish, 0)


def place_all(near, other, table, tile_grid):
    comp_count = tile_grid.shape[0]
    return pl.pallas_call(
        place_kernel,
        out_shape=jax.ShapeDtypeStruct(tile_grid.shape, jnp.float32),
        in_specs=[SMEM, VMEM, VMEM, ANY],
        out_specs=ANY,
        scratch_shapes=[
            pltpu.VMEM((W, comp_count, TU + 2 * SUB, NV), jnp.float32),
            pltpu.SemaphoreType.DMA((W, BLOCKS)),
        ],
        input_output_aliases={3: 0},
        compiler_params=pltpu.CompilerParams(vmem_limit_bytes=44 << 20),
        cost_estimate=pl.CostEstimate(flops=0, bytes_accessed=16 << 20, transcendentals=0),
    )(table, near, other, tile_grid)


def body(visibilities, positions, owner, w_plane, row_offset, col_offset):
    peers = lax.axis_size("tm")
    tiles = lax.axis_size("uv")
    sub_count = visibilities.shape[1]
    comp_count = visibilities.shape[0] // peers
    kept = comp_count * SUB
    tile = lax.axis_index("uv")
    half = sub_count // 2

    numbers = jnp.stack(
        [owner[:, 0], row_offset, w_plane, col_offset // LANES, col_offset % LANES], axis=0
    ).astype(jnp.bfloat16)
    numbers = jnp.concatenate([numbers, beside(numbers, "uv")], axis=1).astype(jnp.float32)
    numbers = jnp.pad(numbers, ((0, META - 5), (0, kept - 2 * sub_count)))

    *sent_a, tile_grid = grid_parts(visibilities, positions, peers, 0, half, True)
    parts_a = exchange(sent_a, "tm")
    sent_b = grid_parts(visibilities, positions, peers, 1, half, False, sent_a[0])
    parts_b = exchange(sent_b, "tm")
    (sum_a,) = sum_parts(parts_a, [], sent_b[:1], numbers)
    hops_a = across(sum_a, "uv")
    sum_b, near_a = sum_parts(parts_b, hops_a, [])
    near = jnp.concatenate([near_a, jnp.stack(across(sum_b, "uv"), axis=0)], axis=0)
    other = beside(near, "uv")

    told = jnp.stack([hop[half * SUB :, : 2 * sub_count] for hop in hops_a], axis=1).astype(jnp.float32).astype(jnp.int32)
    chips = told.shape[1]
    told = told.reshape(META, -1)
    entry = jnp.arange(told.shape[1], dtype=jnp.int32)
    chip, sub = entry // (2 * sub_count), entry % sub_count
    others = entry // sub_count % 2
    spots = ((sub // half * chips + chip) << 16) + sub % half * SUB
    ahead = (told[0] - tile) % tiles
    starts = jnp.where(ahead == 0, told[1] + SUB, jnp.where(ahead == tiles - 1, told[1] + SUB - TU, -1))
    table = touch_plan(starts, told[2], told[3] * LANES + told[4], spots, others)
    return place_all(near, other, table, tile_grid)


def solution(mesh):
    placed = (P(None, "uv", "tm"), P(None, "uv", "tm"), P("uv", None), P("uv"), P("uv"), P("uv"))
    return jax.shard_map(
        body, mesh=mesh, in_specs=placed, out_specs=P("tm", None, "uv", None), check_vma=False
    )
```

profile of v0, /device:TPU:17, one launch (start us, length us, event | category | flops | bytes accessed | tf_op | source)
XLA Modules:
  0.0 66.5 jit_solution(12042754529057412995)
XLA Ops:
  0.0 0.8 %convert_bitcast_fusion.3 = bf16[1,16]{1,0:T(2,128)(2,1)S(1)} fusion(s32[16,1]{0,1:T(1,128)} %param.8), kind=kLoop, calls=%fused_computation.121 | loop fusion | flops 16 | bytes 96 | tf_op jit(solution)/shard_map/stack;squeeze | solution.py:313
  0.8 0.7 convert_bitcast_fusion.2
  1.4 0.7 %fusion.22 = (bf16[1,16]{1,0:T(2,128)(2,1)S(1)}, bf16[1,16]{1,0:T(2,128)(2,1)S(1)}, bf16[1,16]{1,0:T(2,128)(2,1)S(1)}) fusion(s32[16]{0:T(128)} %param.11, s32[16]{0:T(128)} %param.9), kind=kLoop, calls=%fused_computation.103 | loop fusion | flops 352 | bytes 224 | tf_op jit(solution)/shard_map/stack | solution.py:313
  2.2 0.7 %collective-permute-start.3 = (bf16[5,16]{1,0:T(8,128)(2,1)S(1)}, bf16[5,16]{1,0:T(8,128)(2,1)S(1)}, u32[]{:S(2)}, u32[]{:S(2)}) collective-permute-start(bf16[5,16]{1,0:T(8,128)(2,1)S(1)} %stack.58), channel_id=1, source_target_pairs={{0,4},{4,0},{8,12},{12,8},{16,20},{20,16},{24,28},{28,24},{1,5},{5... | collective-permute-start | bytes 488 | tf_op jit(solution)/shard_map/ppermute | solution.py:171
  2.9 11.6 %shard_map.64 = (bf16[4,128,128]{2,1,0:T(8,128)(2,1)}, bf16[4,128,128]{2,1,0:T(8,128)(2,1)}, bf16[4,128,128]{2,1,0:T(8,128)(2,1)}, bf16[4,128,128]{2,1,0:T(8,128)(2,1)}, f32[2,8,128,2048]{3,2,1,0:T(8,128)}) custom-call(s32[1]{0:T(128)} %bitcast.me_ref, bf16[8,16,4096]{2,1,0:T(8,128)(2,1)} %values_ref.3, f32[2,16,4096]{2,1,0:T(8,128)} %places_ref.3), custom_call_target="tpu_custom_call" | custom-call | flops 8589934592 | bytes 2097152 | tf_op jit(solution)/shard_map/pallas_call | solution.py:109
  14.8 3.2 %collective-permute-start.1 = (bf16[4,128,128]{2,1,0:T(8,128)(2,1)}, bf16[4,128,128]{2,1,0:T(8,128)(2,1)S(1)}, u32[]{:S(2)}, u32[]{:S(2)}) collective-permute-start(bf16[4,128,128]{2,1,0:T(8,128)(2,1)} %get-tuple-element.18), channel_id=1, source_target_pairs={{0,2},{1,3},{2,0},{3,1},{4,6},{5,7},{6,4},{7,5},{8,10},{9,11},{10,... | collective-permute-start | bytes 393224 | tf_op jit(solution)/shard_map/ppermute | solution.py:159
  18.0 0.9 %copy-done = bf16[4,128,128]{2,1,0:T(8,128)(2,1)S(1)} copy-done((bf16[4,128,128]{2,1,0:T(8,128)(2,1)S(1)}, bf16[4,128,128]{2,1,0:T(8,128)(2,1)}, u32[]{:S(2)}) %copy-start) | copy-done | bytes 131096
  18.9 9.6 %shard_map.65 = (bf16[4,128,128]{2,1,0:T(8,128)(2,1)S(1)}, bf16[4,128,128]{2,1,0:T(8,128)(2,1)S(1)}, bf16[4,128,128]{2,1,0:T(8,128)(2,1)S(1)}, bf16[4,128,128]{2,1,0:T(8,128)(2,1)S(1)}) custom-call(s32[1]{0:T(128)} %bitcast.me_ref, bf16[8,16,4096]{2,1,0:T(8,128)(2,1)S(1)} %copy-done.2, f32[2,16,4096]{2,1,0:T(8,128)S(1)} %copy-done.3, ...), custom_call_target="tpu_custom_call" | custom-call | flops 8589934592 | bytes 2097152 | tf_op jit(solution)/shard_map/pallas_call | solution.py:109
  28.9 3.3 %collective-permute-start.8 = (bf16[4,128,128]{2,1,0:T(8,128)(2,1)S(1)}, bf16[4,128,128]{2,1,0:T(8,128)(2,1)S(1)}, u32[]{:S(2)}, u32[]{:S(2)}) collective-permute-start(bf16[4,128,128]{2,1,0:T(8,128)(2,1)S(1)} %get-tuple-element.22), channel_id=1, source_target_pairs={{0,2},{1,3},{2,0},{3,1},{4,6},{5,7},{6,4},{7,5},{8,10},{9,11},{10,... | collective-permute-start | bytes 393224 | tf_op jit(solution)/shard_map/ppermute | solution.py:159
  32.5 2.2 %collective-permute-start.6 = (bf16[528,128]{1,0:T(8,128)(2,1)S(1)}, bf16[528,128]{1,0:T(8,128)(2,1)S(1)}, u32[]{:S(2)}, u32[]{:S(2)}) collective-permute-start(bf16[528,128]{1,0:T(8,128)(2,1)S(1)} %shard_map.66.refs_4_), channel_id=1, source_target_pairs={{0,24},{4,28},{8,16},{12,20},{16,8},{20,12},{24,0},{28,4},{1,25},{... | collective-permute-start | bytes 405512 | tf_op jit(solution)/shard_map/ppermute | solution.py:166
  34.9 1.1 %collective-permute-done.7.refs_1_ = bf16[4,128,128]{2,1,0:T(8,128)(2,1)S(1)} collective-permute-done((bf16[4,128,128]{2,1,0:T(8,128)(2,1)S(1)}, bf16[4,128,128]{2,1,0:T(8,128)(2,1)S(1)}, u32[]{:S(2)}, u32[]{:S(2)}) %collective-permute-start.7) | collective-permute-done | bytes 131104 | tf_op jit(solution)/shard_map/ppermute | solution.py:159
  36.0 1.1 %collective-permute-start.4 = (bf16[528,128]{1,0:T(8,128)(2,1)S(1)}, bf16[528,128]{1,0:T(8,128)(2,1)S(1)}, u32[]{:S(2)}, u32[]{:S(2)}) collective-permute-start(bf16[528,128]{1,0:T(8,128)(2,1)S(1)} %shard_map.66.refs_4_), channel_id=1, source_target_pairs={{0,8},{4,12},{8,0},{12,4},{16,24},{20,28},{24,16},{28,20},{1,9},{5... | collective-permute-start | bytes 405512 | tf_op jit(solution)/shard_map/ppermute | solution.py:166
  37.0 2.5 %collective-permute-done.8.refs_2_ = bf16[4,128,128]{2,1,0:T(8,128)(2,1)S(1)} collective-permute-done((bf16[4,128,128]{2,1,0:T(8,128)(2,1)S(1)}, bf16[4,128,128]{2,1,0:T(8,128)(2,1)S(1)}, u32[]{:S(2)}, u32[]{:S(2)}) %collective-permute-start.8) | collective-permute-done | bytes 131104 | tf_op jit(solution)/shard_map/ppermute | solution.py:159
  39.6 1.8 %collective-permute-done.5.refs_6_ = bf16[528,128]{1,0:T(8,128)(2,1)S(1)} collective-permute-done((bf16[528,128]{1,0:T(8,128)(2,1)S(1)}, bf16[528,128]{1,0:T(8,128)(2,1)S(1)}, u32[]{:S(2)}, u32[]{:S(2)}) %collective-permute-start.5) | collective-permute-done | bytes 135200 | tf_op jit(solution)/shard_map/ppermute | solution.py:166
  41.5 1.1 %collective-permute-start.12 = (bf16[512,128]{1,0:T(8,128)(2,1)S(1)}, bf16[512,128]{1,0:T(8,128)(2,1)S(1)}, u32[]{:S(2)}, u32[]{:S(2)}) collective-permute-start(bf16[512,128]{1,0:T(8,128)(2,1)S(1)} %get-tuple-element.25), channel_id=1, source_target_pairs={{0,24},{4,28},{8,16},{12,20},{16,8},{20,12},{24,0},{28,4},{1,25},{... | collective-permute-start | bytes 393224 | tf_op jit(solution)/shard_map/ppermute | solution.py:166
  42.6 1.4 %collective-permute-start.11 = (bf16[512,128]{1,0:T(8,128)(2,1)S(1)}, bf16[512,128]{1,0:T(8,128)(2,1)S(1)}, u32[]{:S(2)}, u32[]{:S(2)}) collective-permute-start(bf16[512,128]{1,0:T(8,128)(2,1)S(1)} %get-tuple-element.25), channel_id=1, source_target_pairs={{0,16},{4,20},{8,24},{12,28},{16,0},{20,4},{24,8},{28,12},{1,17},{... | collective-permute-start | bytes 393224 | tf_op jit(solution)/shard_map/ppermute | solution.py:166
  44.2 0.6 broadcast.1180
  44.8 0.7 %fusion.39 = (s32[4,32]{1,0:T(4,128)S(1)}, s32[1,4,32]{2,0,1:T(1,128)S(1)}, s32[4,32]{1,0:T(4,128)S(1)}, s32[1,4,32]{2,0,1:T(1,128)S(1)}) fusion(s32[]{:T(128)} %broadcast.1180, bf16[16,1,32]{2,0,1:T(8,128)(2,1)S(1)} %slice_bitcast_fusion, bf16[16,1,32]{2,0,1:T(8,128)(2,1)S(1)} %slice_bitcast_fusion.1, bf16[16,1,32]{2,0,1:T(8,128)(2,1)S(1)} %slice_bitcast_fusion.2, ...), kind=kLoop, calls=%fused_computation.125 | loop fusion | flops 3712 | bytes 6148 | tf_op jit(solution)/shard_map/add | solution.py:338
  45.5 1.4 %fusion.16 = (s32[]{:T(128)}, s32[4,32]{1,0:T(4,128)S(1)}, s32[4,32]{1,0:T(4,128)S(1)}, s32[4,32]{1,0:T(4,128)S(1)}, s32[1,4,32]{2,0,1:T(1,128)S(1)}, /*index=5*/bf16[1,4,32]{2,0,1:T(2,128)(2,1)S(1)}) fusion(s32[]{:T(128)} %broadcast.1180, s32[]{:T(128)S(6)} %axis_index.29, bf16[16,1,32]{2,0,1:T(8,128)(2,1)S(1)} %slice_bitcast_fusion, ...), kind=kLoop, calls=%fused_computation.80 | loop fusion | flops 5119 | bytes 6412 | tf_op jit(solution)/shard_map/reduce_sum | solution.py:195
  47.4 0.9 %collective-permute-done.10 = bf16[512,128]{1,0:T(8,128)(2,1)S(1)} collective-permute-done((bf16[512,128]{1,0:T(8,128)(2,1)S(1)}, bf16[512,128]{1,0:T(8,128)(2,1)S(1)}, u32[]{:S(2)}, u32[]{:S(2)}) %collective-permute-start.10) | collective-permute-done | bytes 131104 | tf_op jit(solution)/shard_map/ppermute | solution.py:166
  48.4 7.5 %collective-permute-start.13 = (bf16[8,512,128]{2,1,0:T(8,128)(2,1)S(1)}, bf16[8,512,128]{2,1,0:T(8,128)(2,1)S(1)}, u32[]{:S(2)}, u32[]{:S(2)}) collective-permute-start(bf16[8,512,128]{2,1,0:T(8,128)(2,1)S(1)} %bitcast_dynamic-update-slice_fusion.near_ref), channel_id=1, source_target_pairs={{0,4},{4,0},{8,12},{12,8},{16,20},{20,16},{24,28},{28,24},{1,5},{5... | collective-permute-start | bytes 3145736 | tf_op jit(solution)/shard_map/ppermute | solution.py:171
  57.1 0.7 %concatenate.10.table_ref = s32[6,128]{1,0:T(8,128)S(1)} pad(s32[5,128]{1,0:T(8,128)S(1)} %select_reduce_fusion, s32[]{:T(128)} %get-tuple-element.27), padding=0_1x0_0 | pad | bytes 5636 | tf_op jit(solution)/shard_map/concatenate | solution.py:196
  57.8 0.4 collective-permute-done.13.other_ref
  58.2 8.3 %shard_map.68 = f32[2,8,128,2048]{3,2,1,0:T(8,128)} custom-call(s32[6,128]{1,0:T(8,128)S(1)} %concatenate.10.table_ref, bf16[8,512,128]{2,1,0:T(8,128)(2,1)S(1)} %bitcast_dynamic-update-slice_fusion.near_ref, bf16[8,512,128]{2,1,0:T(8,128)(2,1)S(1)} %collective-permute-done.13.other_ref, ...), custom_call_target="tpu_custom_call", output_to_operand_aliasing={{}: (3, {})} | custom-call | bytes 16777216 | tf_op jit(solution)/shard_map/pallas_call | solution.py:289
  (55 shorter events, 3.1 us)
Async XLA Ops:
  0.0 18.0 %copy-start.3 = (f32[2,16,4096]{2,1,0:T(8,128)S(1)}, f32[2,16,4096]{2,1,0:T(8,128)}, u32[]{:S(2)}) copy-start(f32[2,16,4096]{2,1,0:T(8,128)} %places_ref.3) | copy-start | bytes 1572868
  0.0 18.0 %copy-start.2 = (bf16[8,16,4096]{2,1,0:T(8,128)(2,1)S(1)}, bf16[8,16,4096]{2,1,0:T(8,128)(2,1)}, u32[]{:S(2)}) copy-start(bf16[8,16,4096]{2,1,0:T(8,128)(2,1)} %values_ref.3) | copy-start | bytes 3145732
  2.2 26.7 %collective-permute-start.3 = (bf16[5,16]{1,0:T(8,128)(2,1)S(1)}, bf16[5,16]{1,0:T(8,128)(2,1)S(1)}, u32[]{:S(2)}, u32[]{:S(2)}) collective-permute-start(bf16[5,16]{1,0:T(8,128)(2,1)S(1)} %stack.58), channel_id=1, source_target_pairs={{0,4},{4,0},{8,12},{12,8},{16,20},{20,16},{24,28},{28,24},{1,5},{5... | collective-permute-start | bytes 488 | tf_op jit(solution)/shard_map/ppermute | solution.py:171
  14.5 17.7 %collective-permute-start = (bf16[4,128,128]{2,1,0:T(8,128)(2,1)}, bf16[4,128,128]{2,1,0:T(8,128)(2,1)S(1)}, u32[]{:S(2)}, u32[]{:S(2)}) collective-permute-start(bf16[4,128,128]{2,1,0:T(8,128)(2,1)} %get-tuple-element.17), channel_id=1, source_target_pairs={{0,3},{1,2},{2,1},{3,0},{4,7},{5,6},{6,5},{7,4},{8,11},{9,10},{10,... | collective-permute-start | bytes 393224 | tf_op jit(solution)/shard_map/ppermute | solution.py:159
  14.8 17.5 %collective-permute-start.1 = (bf16[4,128,128]{2,1,0:T(8,128)(2,1)}, bf16[4,128,128]{2,1,0:T(8,128)(2,1)S(1)}, u32[]{:S(2)}, u32[]{:S(2)}) collective-permute-start(bf16[4,128,128]{2,1,0:T(8,128)(2,1)} %get-tuple-element.18), channel_id=1, source_target_pairs={{0,2},{1,3},{2,0},{3,1},{4,6},{5,7},{6,4},{7,5},{8,10},{9,11},{10,... | collective-permute-start | bytes 393224 | tf_op jit(solution)/shard_map/ppermute | solution.py:159
  18.0 14.3 %collective-permute-start.2 = (bf16[4,128,128]{2,1,0:T(8,128)(2,1)}, bf16[4,128,128]{2,1,0:T(8,128)(2,1)S(1)}, u32[]{:S(2)}, u32[]{:S(2)}) collective-permute-start(bf16[4,128,128]{2,1,0:T(8,128)(2,1)} %get-tuple-element.19), channel_id=1, source_target_pairs={{0,1},{1,0},{2,3},{3,2},{4,5},{5,4},{6,7},{7,6},{8,9},{9,8},{10,11... | collective-permute-start | bytes 393224 | tf_op jit(solution)/shard_map/ppermute | solution.py:159
  18.0 0.9 %copy-start = (bf16[4,128,128]{2,1,0:T(8,128)(2,1)S(1)}, bf16[4,128,128]{2,1,0:T(8,128)(2,1)}, u32[]{:S(2)}) copy-start(bf16[4,128,128]{2,1,0:T(8,128)(2,1)} %get-tuple-element.16.rest_0_.refs_0_) | copy-start | bytes 393220
  18.9 13.4 %copy-start.1 = (bf16[4,128,128]{2,1,0:T(8,128)(2,1)S(1)}, bf16[4,128,128]{2,1,0:T(8,128)(2,1)}, u32[]{:S(2)}) copy-start(bf16[4,128,128]{2,1,0:T(8,128)(2,1)} %get-tuple-element.16.rest_0_.refs_0_) | copy-start | bytes 393220
  28.5 7.5 %collective-permute-start.7 = (bf16[4,128,128]{2,1,0:T(8,128)(2,1)S(1)}, bf16[4,128,128]{2,1,0:T(8,128)(2,1)S(1)}, u32[]{:S(2)}, u32[]{:S(2)}) collective-permute-start(bf16[4,128,128]{2,1,0:T(8,128)(2,1)S(1)} %get-tuple-element.21), channel_id=1, source_target_pairs={{0,3},{1,2},{2,1},{3,0},{4,7},{5,6},{6,5},{7,4},{8,11},{9,10},{10,... | collective-permute-start | bytes 393224 | tf_op jit(solution)/shard_map/ppermute | solution.py:159
  28.9 10.7 %collective-permute-start.8 = (bf16[4,128,128]{2,1,0:T(8,128)(2,1)S(1)}, bf16[4,128,128]{2,1,0:T(8,128)(2,1)S(1)}, u32[]{:S(2)}, u32[]{:S(2)}) collective-permute-start(bf16[4,128,128]{2,1,0:T(8,128)(2,1)S(1)} %get-tuple-element.22), channel_id=1, source_target_pairs={{0,2},{1,3},{2,0},{3,1},{4,6},{5,7},{6,4},{7,5},{8,10},{9,11},{10,... | collective-permute-start | bytes 393224 | tf_op jit(solution)/shard_map/ppermute | solution.py:159
  32.3 7.3 %collective-permute-start.9 = (bf16[4,128,128]{2,1,0:T(8,128)(2,1)S(1)}, bf16[4,128,128]{2,1,0:T(8,128)(2,1)S(1)}, u32[]{:S(2)}, u32[]{:S(2)}) collective-permute-start(bf16[4,128,128]{2,1,0:T(8,128)(2,1)S(1)} %get-tuple-element.23), channel_id=1, source_target_pairs={{0,1},{1,0},{2,3},{3,2},{4,5},{5,4},{6,7},{7,6},{8,9},{9,8},{10,11... | collective-permute-start | bytes 393224 | tf_op jit(solution)/shard_map/ppermute | solution.py:159
  32.5 7.1 %collective-permute-start.6 = (bf16[528,128]{1,0:T(8,128)(2,1)S(1)}, bf16[528,128]{1,0:T(8,128)(2,1)S(1)}, u32[]{:S(2)}, u32[]{:S(2)}) collective-permute-start(bf16[528,128]{1,0:T(8,128)(2,1)S(1)} %shard_map.66.refs_4_), channel_id=1, source_target_pairs={{0,24},{4,28},{8,16},{12,20},{16,8},{20,12},{24,0},{28,4},{1,25},{... | collective-permute-start | bytes 405512 | tf_op jit(solution)/shard_map/ppermute | solution.py:166
  34.7 6.6 %collective-permute-start.5 = (bf16[528,128]{1,0:T(8,128)(2,1)S(1)}, bf16[528,128]{1,0:T(8,128)(2,1)S(1)}, u32[]{:S(2)}, u32[]{:S(2)}) collective-permute-start(bf16[528,128]{1,0:T(8,128)(2,1)S(1)} %shard_map.66.refs_4_), channel_id=1, source_target_pairs={{0,16},{4,20},{8,24},{12,28},{16,0},{20,4},{24,8},{28,12},{1,17},{... | collective-permute-start | bytes 405512 | tf_op jit(solution)/shard_map/ppermute | solution.py:166
  36.0 5.3 %collective-permute-start.4 = (bf16[528,128]{1,0:T(8,128)(2,1)S(1)}, bf16[528,128]{1,0:T(8,128)(2,1)S(1)}, u32[]{:S(2)}, u32[]{:S(2)}) collective-permute-start(bf16[528,128]{1,0:T(8,128)(2,1)S(1)} %shard_map.66.refs_4_), channel_id=1, source_target_pairs={{0,8},{4,12},{8,0},{12,4},{16,24},{20,28},{24,16},{28,20},{1,9},{5... | collective-permute-start | bytes 405512 | tf_op jit(solution)/shard_map/ppermute | solution.py:166
  41.5 6.8 %collective-permute-start.12 = (bf16[512,128]{1,0:T(8,128)(2,1)S(1)}, bf16[512,128]{1,0:T(8,128)(2,1)S(1)}, u32[]{:S(2)}, u32[]{:S(2)}) collective-permute-start(bf16[512,128]{1,0:T(8,128)(2,1)S(1)} %get-tuple-element.25), channel_id=1, source_target_pairs={{0,24},{4,28},{8,16},{12,20},{16,8},{20,12},{24,0},{28,4},{1,25},{... | collective-permute-start | bytes 393224 | tf_op jit(solution)/shard_map/ppermute | solution.py:166
  42.6 5.7 %collective-permute-start.11 = (bf16[512,128]{1,0:T(8,128)(2,1)S(1)}, bf16[512,128]{1,0:T(8,128)(2,1)S(1)}, u32[]{:S(2)}, u32[]{:S(2)}) collective-permute-start(bf16[512,128]{1,0:T(8,128)(2,1)S(1)} %get-tuple-element.25), channel_id=1, source_target_pairs={{0,16},{4,20},{8,24},{12,28},{16,0},{20,4},{24,8},{28,12},{1,17},{... | collective-permute-start | bytes 393224 | tf_op jit(solution)/shard_map/ppermute | solution.py:166
  44.0 4.3 %collective-permute-start.10 = (bf16[512,128]{1,0:T(8,128)(2,1)S(1)}, bf16[512,128]{1,0:T(8,128)(2,1)S(1)}, u32[]{:S(2)}, u32[]{:S(2)}) collective-permute-start(bf16[512,128]{1,0:T(8,128)(2,1)S(1)} %get-tuple-element.25), channel_id=1, source_target_pairs={{0,8},{4,12},{8,0},{12,4},{16,24},{20,28},{24,16},{28,20},{1,9},{5... | collective-permute-start | bytes 393224 | tf_op jit(solution)/shard_map/ppermute | solution.py:166
  48.4 9.8 %collective-permute-start.13 = (bf16[8,512,128]{2,1,0:T(8,128)(2,1)S(1)}, bf16[8,512,128]{2,1,0:T(8,128)(2,1)S(1)}, u32[]{:S(2)}, u32[]{:S(2)}) collective-permute-start(bf16[8,512,128]{2,1,0:T(8,128)(2,1)S(1)} %bitcast_dynamic-update-slice_fusion.near_ref), channel_id=1, source_target_pairs={{0,4},{4,0},{8,12},{12,8},{16,20},{20,16},{24,28},{28,24},{1,5},{5... | collective-permute-start | bytes 3145736 | tf_op jit(solution)/shard_map/ppermute | solution.py:171
where the time goes:
time: 66.5 us
  Pallas kernels  29.8 us (45%)
  starting transfers between devices  21.6 us (32%)
  waiting for transfers between devices  6.66 us (10%)
  other arithmetic  5.01 us (8%)
  local copies, waits for them, and re-layouts  3.19 us (5%)
    pallas_call x2, Pallas kernels, grid_parts(): pl.pallas_call(functools.partial(grid_kernel, peers=peers, blanks=blanks,...  21.2 us
    pallas_call x1, Pallas kernels, place_all(): pl.pallas_call(place_kernel, out_shape=jax.ShapeDtypeStruct(tile_grid.sha...  8.3 us
    ppermute x2, starting transfers between devices, beside(): return lax.ppermute(array, axis, [(i, i ^ 1) for i in range(size)])  8.25 us
    ppermute x6, starting transfers between devices, exchange(): lax.ppermute(parts[mask], axis, [(i, i ^ mask) for i in range(size)])  7.13 us
    ppermute x6, starting transfers between devices, across(): lax.ppermute(array, axis, [(i, i ^ mask) for i in range(size)])  6.22 us
    ppermute x6, waiting for transfers between devices, exchange(): lax.ppermute(parts[mask], axis, [(i, i ^ mask) for i in range(size)])  3.58 us
    ppermute x6, waiting for transfers between devices, across(): lax.ppermute(array, axis, [(i, i ^ mask) for i in range(size)])  2.7 us
    another operation x3, other arithmetic, body(): jnp.stack([owner[:, 0], row_offset, w_plane, col_offset // LANES, col_off...  2.12 us
  transfers between devices with their start and end apart: 14, of which 5 were waited for; matrix products, arithmetic and copies ran while one was open for 8% of the time, Pallas kernels for 32%

commit v1 on v0

--- a/solution.py
+++ b/solution.py
@@ -28,11 +28,15 @@
     return inner * inner
 
 
-def grid_kernel(me_ref, values_ref, places_ref, *rest, peers, blanks, orders):
-    parts_refs, rest = rest[orders : orders + peers], rest[orders + peers :]
-    zero_copies = []
-    if blanks:
-        out_ref, values_wide, sums, blank, sem, values, places, in_sem = rest
+def number_rows(owner, row_offset, w_plane, col_offset):
+    rows = [owner, row_offset, w_plane, col_offset // LANES, col_offset % LANES]
+    blank = jnp.zeros((META - len(rows), owner.shape[1]), jnp.int32)
+    return jnp.concatenate(rows + [blank], axis=0).astype(jnp.float32).astype(jnp.bfloat16)
+
+
+def grid_kernel(me_ref, values_ref, places_ref, *rest, peers, first):
+    if first:
+        kept_ref, sent_ref, out_ref, values_wide, sums, blank, sem, values, places, in_sem = rest
         _, sub_count, row_count = values.shape
         in_copies = [
             pltpu.make_async_copy(values_ref.at[:, pl.ds(0, sub_count), :], values, in_sem.at[0]),
@@ -44,13 +48,14 @@
         zero_copies = [pltpu.make_async_copy(blank, out_ref.at[:, plane], sem.at[plane]) for plane in range(W)]
         for copy in in_copies:
             copy.wait()
+        for copy in zero_copies:
+            copy.start()
         values_ref, places_ref = values, places
     else:
-        values_wide, sums = rest
-    for copy in zero_copies:
-        copy.start()
+        _, owner_ref, row_ref, plane_ref, col_ref, kept_ref, sent_ref, numbers_ref, values_wide, sums = rest
+        numbers_ref[...] = number_rows(owner_ref[...], row_ref[...], plane_ref[...], col_ref[...])
     comp_count, sub_count, row_count = values_ref.shape
-    kept = comp_count // peers * SUB
+    rows_each = comp_count // peers * SUB
     for comp in range(comp_count):
         values_wide[comp * sub_count : (comp + 1) * sub_count, :] = values_ref[comp].astype(jnp.float32)
     cells = lax.broadcasted_iota(jnp.int32, (SUB, row_count), 0).astype(jnp.float32) * (2.0 / TAPS)
@@ -74,101 +79,136 @@
             sub = turn * STEP + pair * 2
             sums[pair] = jnp.concatenate([one_sub(sub), one_sub(sub + 1)], axis=1).astype(jnp.bfloat16)
         for pair in range(STEP // 2):
-            for mask, parts_ref in enumerate(parts_refs):
-                rows = pl.ds(pl.multiple_of((me_ref[0] ^ mask) * kept, kept), kept)
-                parts_ref[turn * (STEP // 2) + pair] = sums[pair, rows, :]
+            for mask in range(peers):
+                rows = pl.ds(pl.multiple_of((me_ref[0] ^ mask) * rows_each, rows_each), rows_each)
+                target = sent_ref if mask % 2 else kept_ref
+                target[mask // 2, turn * (STEP // 2) + pair] = sums[pair, rows, :]
         return carry
 
     lax.fori_loop(0, sub_count // STEP, some_subs, 0)
-    for copy in zero_copies:
-        copy.wait()
-
-
-def grid_parts(values, places, peers, chunk, sub_count, blanks, *order):
-    comp_count, _, row_count = values.shape
-    kept = comp_count // peers * SUB
+    if first:
+        for copy in zero_copies:
+            copy.wait()
+
+
+def grid_parts(values, places, peers, chunk, sub_count, order=None, numbers=()):
+    comp_count, all_subs, row_count = values.shape
+    rows_each = comp_count // peers * SUB
+    first = order is None
     me = lax.axis_index("tm").astype(jnp.int32).reshape(1)
-    parts_shape = (sub_count // 2, kept, LANES)
+    parts_shape = (peers // 2, sub_count // 2, rows_each, LANES)
     values_block, places_block = (comp_count, sub_count, row_count), (2, sub_count, row_count)
-    if blanks:
-        in_specs = [ANY] * 2
-    else:
-        in_specs = [pl.BlockSpec(block, lambda i: (0, chunk, 0)) for block in (values_block, places_block)]
+    out_shape = [jax.ShapeDtypeStruct(parts_shape, jnp.bfloat16)] * 2
+    out_specs = [pl.BlockSpec(parts_shape, lambda i: (0, 0, 0, 0))] * 2
     scratch = [
         pltpu.VMEM((comp_count * sub_count, row_count), jnp.float32),
         pltpu.VMEM((STEP // 2, comp_count * SUB, LANES), jnp.bfloat16),
     ]
-    if blanks:
+    if first:
+        in_specs = [ANY] * 2
+        out_shape.append(jax.ShapeDtypeStruct((rows_each // SUB, W, TU, NV), jnp.float32))
+        out_specs.append(ANY)
         scratch += [
-            pltpu.VMEM((kept // SUB, TU, NV), jnp.float32),
+            pltpu.VMEM((rows_each // SUB, TU, NV), jnp.float32),
             pltpu.SemaphoreType.DMA((W,)),
             pltpu.VMEM(values_block, values.dtype),
             pltpu.VMEM(places_block, places.dtype),
             pltpu.SemaphoreType.DMA((2,)),
         ]
+        more = []
+    else:
+        whole = pl.BlockSpec((1, all_subs), lambda i: (0, 0))
+        in_specs = [pl.BlockSpec(block, lambda i: (0, chunk, 0)) for block in (values_block, places_block)]
+        in_specs += [ANY] + [whole] * len(numbers)
+        out_shape.append(jax.ShapeDtypeStruct((META, all_subs), jnp.bfloat16))
+        out_specs.append(pl.BlockSpec((META, all_subs), lambda i: (0, 0)))
+        more = [order, *numbers]
     return pl.pallas_call(
-        functools.partial(grid_kernel, peers=peers, blanks=blanks, orders=len(order)),
+        functools.partial(grid_kernel, peers=peers, first=first),
         grid=(1,),
-        out_shape=[jax.ShapeDtypeStruct(parts_shape, jnp.bfloat16)] * peers
-        + [jax.ShapeDtypeStruct((kept // SUB, W, TU, NV), jnp.float32)] * blanks,
-        in_specs=[SMEM] + in_specs + [ANY] * len(order),
-        out_specs=[pl.BlockSpec(parts_shape, lambda i: (0, 0, 0))] * peers + [ANY] * blanks,
+        out_shape=out_shape,
+        in_specs=[SMEM] + in_specs,
+        out_specs=out_specs,
         scratch_shapes=scratch,
-        compiler_params=pltpu.CompilerParams(vmem_limit_bytes=(60 if blanks else 48) << 20),
+        compiler_params=pltpu.CompilerParams(vmem_limit_bytes=(60 if first else 48) << 20),
         cost_estimate=pl.CostEstimate(
             flops=8 * sub_count * row_count * SUB * SUB * comp_count,
             bytes_accessed=2 << 20,
             transcendentals=0,
         ),
-    )(me, values, places, *order)
-
-
-def sum_kernel(*refs, peers, hops, orders):
-    parts_refs, hops_refs, rest = refs[:peers], refs[peers : peers + hops], refs[peers + hops + orders :]
-    pairs = parts_refs[0].shape[0]
-    out_ref = rest[0] if hops else rest[1]
+    )(me, values, places, *more)
+
+
+def halve_kernel(kept_ref, arrived_ref, *rest):
+    next_kept_ref, next_sent_ref = rest[-2:]
+    for at in range(kept_ref.shape[0]):
+        total = kept_ref[at].astype(jnp.float32) + arrived_ref[at].astype(jnp.float32)
+        if at % 2:
+            next_sent_ref[at // 2] = total.astype(jnp.bfloat16)
+        else:
+            next_kept_ref[at // 2] = total
+
+
+def halve(kept, arrived, order):
+    shape = (kept.shape[0] // 2,) + kept.shape[1:]
+    return pl.pallas_call(
+        halve_kernel,
+        out_shape=[jax.ShapeDtypeStruct(shape, jnp.float32), jax.ShapeDtypeStruct(shape, jnp.bfloat16)],
+        in_specs=[VMEM] * 2 + [ANY] * len(order),
+        out_specs=[VMEM] * 2,
+        compiler_params=pltpu.CompilerParams(vmem_limit_bytes=8 << 20),
+        cost_estimate=pl.CostEstimate(flops=1 << 18, bytes_accessed=1 << 20, transcendentals=0),
+    )(kept, arrived, *order)
+
+
+def paired(array, axis, mask):
+    return lax.ppermute(array, axis, [(i, i ^ mask) for i in range(lax.axis_size(axis))])
+
+
+def reduce_over(kept, sent, axis, order):
+    mask = 1
+    arrived = paired(sent, axis, mask)
+    while kept.shape[0] > 1:
+        kept, sent = halve(kept, arrived, order)
+        mask *= 2
+        arrived = paired(sent, axis, mask)
+    return kept, arrived
+
+
+def sum_kernel(kept_ref, arrived_ref, *rest, hops):
+    pairs = kept_ref.shape[1]
+    out_ref = rest[hops or 2]
     for pair in range(pairs):
-        total = parts_refs[0][pair].astype(jnp.float32)
-        for parts_ref in parts_refs[1:]:
-            total = total + parts_ref[pair].astype(jnp.float32)
+        total = kept_ref[0, pair].astype(jnp.float32) + arrived_ref[0, pair].astype(jnp.float32)
         out_ref[pair * 2 * SUB : (pair + 1) * 2 * SUB, :] = total.T.astype(jnp.bfloat16)
     if hops:
-        for at, hop_ref in enumerate(hops_refs):
-            rest[1][at] = hop_ref[: rest[1].shape[1], :]
+        near_ref = rest[hops + 1]
+        for at in range(hops):
+            near_ref[at] = rest[at][: near_ref.shape[1], :]
     else:
-        out_ref[pairs * 2 * SUB :, :] = rest[0][...].astype(jnp.bfloat16)
-
-
-def sum_parts(parts, hops, order, *numbers):
-    pairs, kept, _ = parts[0].shape
-    rows = pairs * 2 * SUB + META * len(numbers)
+        numbers = [ref[...].astype(jnp.float32) for ref in rest[:2]]
+        blank = jnp.zeros((META, out_ref.shape[1] - 2 * numbers[0].shape[1]), jnp.float32)
+        out_ref[pairs * 2 * SUB :, :] = jnp.concatenate(numbers + [blank], axis=1).astype(jnp.bfloat16)
+
+
+def sum_parts(kept, arrived, hops, numbers):
+    _, pairs, lanes, _ = kept.shape
+    rows = pairs * 2 * SUB
+    out_shape = [jax.ShapeDtypeStruct((rows if hops else rows + META, lanes), jnp.bfloat16)]
+    if hops:
+        out_shape.append(jax.ShapeDtypeStruct((len(hops), rows, lanes), jnp.bfloat16))
     return pl.pallas_call(
-        functools.partial(sum_kernel, peers=len(parts), hops=len(hops), orders=len(order)),
-        out_shape=[jax.ShapeDtypeStruct((rows, kept), jnp.bfloat16)]
-        + [jax.ShapeDtypeStruct((len(hops), rows, kept), jnp.bfloat16)] * len(hops[:1]),
-        in_specs=[VMEM] * (len(parts) + len(hops)) + [ANY] * len(order) + [VMEM] * len(numbers),
-        out_specs=[VMEM] * (1 + len(hops[:1])),
+        functools.partial(sum_kernel, hops=len(hops)),
+        out_shape=out_shape,
+        in_specs=[VMEM] * (2 + len(hops) + len(numbers)),
+        out_specs=[VMEM] * len(out_shape),
         compiler_params=pltpu.CompilerParams(vmem_limit_bytes=8 << 20),
         cost_estimate=pl.CostEstimate(flops=1 << 20, bytes_accessed=2 << 20, transcendentals=0),
-    )(*parts, *hops, *order, *numbers)
-
-
-def exchange(parts, axis):
-    size = lax.axis_size(axis)
-    far_first = [
-        lax.ppermute(parts[mask], axis, [(i, i ^ mask) for i in range(size)]) for mask in range(size - 1, 0, -1)
-    ]
-    return [parts[0]] + far_first
+    )(kept, arrived, *hops, *numbers)
 
 
 def across(array, axis):
-    size = lax.axis_size(axis)
-    return [array] + [lax.ppermute(array, axis, [(i, i ^ mask) for i in range(size)]) for mask in range(2, size, 2)]
-
-
-def beside(array, axis):
-    size = lax.axis_size(axis)
-    return lax.ppermute(array, axis, [(i, i ^ 1) for i in range(size)])
+    return [array] + [paired(array, axis, mask) for mask in range(2, lax.axis_size(axis), 2)]
 
 
 def touch_plan(starts, planes, cols, spots, others):
@@ -306,25 +346,27 @@
     tiles = lax.axis_size("uv")
     sub_count = visibilities.shape[1]
     comp_count = visibilities.shape[0] // peers
-    kept = comp_count * SUB
     tile = lax.axis_index("uv")
     half = sub_count // 2
 
-    numbers = jnp.stack(
-        [owner[:, 0], row_offset, w_plane, col_offset // LANES, col_offset % LANES], axis=0
-    ).astype(jnp.bfloat16)
-    numbers = jnp.concatenate([numbers, beside(numbers, "uv")], axis=1).astype(jnp.float32)
-    numbers = jnp.pad(numbers, ((0, META - 5), (0, kept - 2 * sub_count)))
-
-    *sent_a, tile_grid = grid_parts(visibilities, positions, peers, 0, half, True)
-    parts_a = exchange(sent_a, "tm")
-    sent_b = grid_parts(visibilities, positions, peers, 1, half, False, sent_a[0])
-    parts_b = exchange(sent_b, "tm")
-    (sum_a,) = sum_parts(parts_a, [], sent_b[:1], numbers)
+    *parts_a, tile_grid = grid_parts(visibilities, positions, peers, 0, half)
+    *parts_b, own_numbers = grid_parts(
+        visibilities,
+        positions,
+        peers,
+        1,
+        half,
+        tile_grid,
+        (owner.T, row_offset[None], w_plane[None], col_offset[None]),
+    )
+    reduced_a = reduce_over(*parts_a, "tm", parts_b[:1])
+    reduced_b = reduce_over(*parts_b, "tm", [])
+    numbers = (own_numbers, paired(own_numbers, "uv", 1))
+    (sum_a,) = sum_parts(*reduced_a, [], numbers)
     hops_a = across(sum_a, "uv")
-    sum_b, near_a = sum_parts(parts_b, hops_a, [])
+    sum_b, near_a = sum_parts(*reduced_b, hops_a, ())
     near = jnp.concatenate([near_a, jnp.stack(across(sum_b, "uv"), axis=0)], axis=0)
-    other = beside(near, "uv")
+    other = paired(near, "uv", 1)
 
     told = jnp.stack([hop[half * SUB :, : 2 * sub_count] for hop in hops_a], axis=1).astype(jnp.float32).astype(jnp.int32)
     chips = told.shape[1]

time: 66.5 us -> 62.7 us (0.943)
  the two profiles are of different devices: /device:TPU:17 before, /device:TPU:1 now
where the time goes in v1:
time: 62.7 us; the launch traced here: 62.6 us
  Pallas kernels  29.5 us (47%)
  starting transfers between devices  16.1 us (26%)
  waiting for transfers between devices  11.7 us (19%)
  other arithmetic  2.81 us (4%)
  local copies, waits for them, and re-layouts  2.28 us (4%)
    pallas_call x2, Pallas kernels, grid_parts(): pl.pallas_call(functools.partial(grid_kernel, peers=peers, first=first),...  21.3 us
    ppermute x12, starting transfers between devices, paired(): lax.ppermute(array, axis, [(i, i ^ mask) for i in range(lax.axis_size(axi...  16.1 us
    ppermute x12, waiting for transfers between devices, paired(): lax.ppermute(array, axis, [(i, i ^ mask) for i in range(lax.axis_size(axi...  11.7 us
    pallas_call x1, Pallas kernels, place_all(): pl.pallas_call(place_kernel, out_shape=jax.ShapeDtypeStruct(tile_grid.sha...  7.83 us
    reduce_sum x1, other arithmetic, touch_plan(): number = jnp.sum(taken.astype(jnp.int32))  1.42 us
  transfers between devices with their start and end apart: 12, of which 4 were waited for; matrix products, arithmetic and copies ran while one was open for 8% of the time, Pallas kernels for 16%

profile of v1, /device:TPU:1, one launch (start us, length us, event | category | flops | bytes accessed | tf_op | source)
XLA Modules:
  0.0 62.6 jit_solution(11217275567491405962)
XLA Ops:
  0.0 11.7 %shard_map.64 = (bf16[2,4,128,128]{3,2,1,0:T(8,128)(2,1)}, bf16[2,4,128,128]{3,2,1,0:T(8,128)(2,1)}, f32[2,8,128,2048]{3,2,1,0:T(8,128)}) custom-call(s32[1]{0:T(128)} %bitcast.me_ref, bf16[8,16,4096]{2,1,0:T(8,128)(2,1)} %values_ref.3, f32[2,16,4096]{2,1,0:T(8,128)} %places_ref.3), custom_call_target="tpu_custom_call" | custom-call | flops 8589934592 | bytes 2097152 | tf_op jit(solution)/shard_map/pallas_call | solution.py:126
  11.7 2.2 %collective-permute-start = (bf16[2,4,128,128]{3,2,1,0:T(8,128)(2,1)}, bf16[2,4,128,128]{3,2,1,0:T(8,128)(2,1)S(1)}, u32[]{:S(2)}, u32[]{:S(2)}) collective-permute-start(bf16[2,4,128,128]{3,2,1,0:T(8,128)(2,1)} %get-tuple-element.18), channel_id=1, source_target_pairs={{0,1},{1,0},{2,3},{3,2},{4,5},{5,4},{6,7},{7,6},{8,9},{9,8},{10,11... | collective-permute-start | bytes 786440 | tf_op jit(solution)/shard_map/ppermute | solution.py:165
  14.0 9.6 %shard_map.65 = (bf16[2,4,128,128]{3,2,1,0:T(8,128)(2,1)S(1)}, bf16[2,4,128,128]{3,2,1,0:T(8,128)(2,1)S(1)}, bf16[16,16]{1,0:T(8,128)(2,1)S(1)}) custom-call(s32[1]{0:T(128)} %bitcast.me_ref, bf16[8,16,4096]{2,1,0:T(8,128)(2,1)S(1)} %copy-done.1, f32[2,16,4096]{2,1,0:T(8,128)S(1)} %copy-done.2, f32[2,8,128,2048]{3,2,1,0:T(8,128)} %get-tuple-element.19.rest_0_._, ...), custom_call_target="tpu_custom_call" | custom-call | flops 8589934592 | bytes 2097152 | tf_op jit(solution)/shard_map/pallas_call | solution.py:126
  23.7 2.5 %collective-permute-start.1 = (bf16[1,4,128,128]{3,2,1,0:T(8,128)(2,1)S(1)}, bf16[1,4,128,128]{3,2,1,0:T(8,128)(2,1)S(1)}, u32[]{:S(2)}, u32[]{:S(2)}) collective-permute-start(bf16[1,4,128,128]{3,2,1,0:T(8,128)(2,1)S(1)} %get-tuple-element.22), channel_id=1, source_target_pairs={{0,2},{1,3},{2,0},{3,1},{4,6},{5,7},{6,4},{7,5},{8,10},{9,11},{10,... | collective-permute-start | bytes 393224 | tf_op jit(solution)/shard_map/ppermute | solution.py:165
  26.2 1.5 %collective-permute-start.2 = (bf16[16,16]{1,0:T(8,128)(2,1)S(1)}, bf16[16,16]{1,0:T(8,128)(2,1)S(1)}, u32[]{:S(2)}, u32[]{:S(2)}) collective-permute-start(bf16[16,16]{1,0:T(8,128)(2,1)S(1)} %get-tuple-element.23.rest_0_), channel_id=1, source_target_pairs={{0,4},{4,0},{8,12},{12,8},{16,20},{20,16},{24,28},{28,24},{1,5},{5... | collective-permute-start | bytes 1544 | tf_op jit(solution)/shard_map/ppermute | solution.py:165
  27.8 5.7 %collective-permute-done.6.arrived_ref = bf16[2,4,128,128]{3,2,1,0:T(8,128)(2,1)S(1)} collective-permute-done((bf16[2,4,128,128]{3,2,1,0:T(8,128)(2,1)S(1)}, bf16[2,4,128,128]{3,2,1,0:T(8,128)(2,1)S(1)}, u32[]{:S(2)}, u32[]{:S(2)}) %collective-permute-start.6) | collective-permute-done | bytes 262176 | tf_op jit(solution)/shard_map/ppermute | solution.py:165
  33.6 0.1 shard_map.67.rest_0_
  33.7 2.2 %collective-permute-start.5 = (bf16[528,128]{1,0:T(8,128)(2,1)S(1)}, bf16[528,128]{1,0:T(8,128)(2,1)S(1)}, u32[]{:S(2)}, u32[]{:S(2)}) collective-permute-start(bf16[528,128]{1,0:T(8,128)(2,1)S(1)} %shard_map.67.rest_0_), channel_id=1, source_target_pairs={{0,24},{4,28},{8,16},{12,20},{16,8},{20,12},{24,0},{28,4},{1,25},{... | collective-permute-start | bytes 405512 | tf_op jit(solution)/shard_map/ppermute | solution.py:165
  35.9 0.2 collective-permute-start.4
  36.1 0.3 collective-permute-start.3
  36.4 5.1 %collective-permute-done.7.arrived_ref = bf16[1,4,128,128]{3,2,1,0:T(8,128)(2,1)S(1)} collective-permute-done((bf16[1,4,128,128]{3,2,1,0:T(8,128)(2,1)S(1)}, bf16[1,4,128,128]{3,2,1,0:T(8,128)(2,1)S(1)}, u32[]{:S(2)}, u32[]{:S(2)}) %collective-permute-start.7) | collective-permute-done | bytes 131104 | tf_op jit(solution)/shard_map/ppermute | solution.py:165
  41.7 2.4 %collective-permute-start.10 = (bf16[512,128]{1,0:T(8,128)(2,1)S(1)}, bf16[512,128]{1,0:T(8,128)(2,1)S(1)}, u32[]{:S(2)}, u32[]{:S(2)}) collective-permute-start(bf16[512,128]{1,0:T(8,128)(2,1)S(1)} %get-tuple-element.28), channel_id=1, source_target_pairs={{0,24},{4,28},{8,16},{12,20},{16,8},{20,12},{24,0},{28,4},{1,25},{... | collective-permute-start | bytes 393224 | tf_op jit(solution)/shard_map/ppermute | solution.py:165
  44.0 0.3 collective-permute-start.9
  44.4 0.6 broadcast.1135
  45.0 0.7 %fusion.30 = (s32[4,32]{1,0:T(4,128)S(1)}, s32[1,4,32]{2,0,1:T(1,128)S(1)}, s32[4,32]{1,0:T(4,128)S(1)}, s32[1,4,32]{2,0,1:T(1,128)S(1)}) fusion(s32[]{:T(128)} %broadcast.1135, bf16[16,1,32]{2,0,1:T(8,128)(2,1)S(1)} %slice_bitcast_fusion, bf16[16,1,32]{2,0,1:T(8,128)(2,1)S(1)} %slice_bitcast_fusion.1, bf16[16,1,32]{2,0,1:T(8,128)(2,1)S(1)} %slice_bitcast_fusion.2, ...), kind=kLoop, calls=%fused_computation.105 | loop fusion | flops 3712 | bytes 6148 | tf_op jit(solution)/shard_map/add | solution.py:380
  45.7 1.4 %fusion.9 = (s32[]{:T(128)}, s32[4,32]{1,0:T(4,128)S(1)}, s32[4,32]{1,0:T(4,128)S(1)}, s32[4,32]{1,0:T(4,128)S(1)}, s32[1,4,32]{2,0,1:T(1,128)S(1)}, /*index=5*/bf16[1,4,32]{2,0,1:T(2,128)(2,1)S(1)}) fusion(s32[]{:T(128)} %broadcast.1135, s32[]{:T(128)S(6)} %axis_index.29, bf16[16,1,32]{2,0,1:T(8,128)(2,1)S(1)} %slice_bitcast_fusion, ...), kind=kLoop, calls=%fused_computation.69 | loop fusion | flops 5119 | bytes 6412 | tf_op jit(solution)/shard_map/reduce_sum | solution.py:235
  47.5 0.6 collective-permute-done.8
  48.2 4.3 %collective-permute-start.11 = (bf16[8,512,128]{2,1,0:T(8,128)(2,1)S(1)}, bf16[8,512,128]{2,1,0:T(8,128)(2,1)S(1)}, u32[]{:S(2)}, u32[]{:S(2)}) collective-permute-start(bf16[8,512,128]{2,1,0:T(8,128)(2,1)S(1)} %bitcast_dynamic-update-slice_fusion.near_ref), channel_id=1, source_target_pairs={{0,4},{4,0},{8,12},{12,8},{16,20},{20,16},{24,28},{28,24},{1,5},{5... | collective-permute-start | bytes 3145736 | tf_op jit(solution)/shard_map/ppermute | solution.py:165
  53.0 0.2 fusion.3
  53.3 0.2 fusion
  53.5 0.2 select_reduce_fusion
  53.7 0.7 %concatenate.6.table_ref = s32[6,128]{1,0:T(8,128)S(1)} pad(s32[5,128]{1,0:T(8,128)S(1)} %select_reduce_fusion, s32[]{:T(128)} %get-tuple-element.29), padding=0_1x0_0 | pad | bytes 5636 | tf_op jit(solution)/shard_map/concatenate | solution.py:236
  54.4 0.4 collective-permute-done.11.other_ref
  54.8 7.8 %shard_map.70 = f32[2,8,128,2048]{3,2,1,0:T(8,128)} custom-call(s32[6,128]{1,0:T(8,128)S(1)} %concatenate.6.table_ref, bf16[8,512,128]{2,1,0:T(8,128)(2,1)S(1)} %bitcast_dynamic-update-slice_fusion.near_ref, bf16[8,512,128]{2,1,0:T(8,128)(2,1)S(1)} %collective-permute-done.11.other_ref, ...), custom_call_target="tpu_custom_call", output_to_operand_aliasing={{}: (3, {})} | custom-call | bytes 16777216 | tf_op jit(solution)/shard_map/pallas_call | solution.py:329
  (53 shorter events, 1.6 us)
Async XLA Ops:
  0.0 13.9 %copy-start.2 = (f32[2,16,4096]{2,1,0:T(8,128)S(1)}, f32[2,16,4096]{2,1,0:T(8,128)}, u32[]{:S(2)}) copy-start(f32[2,16,4096]{2,1,0:T(8,128)} %places_ref.3) | copy-start | bytes 1572868
  0.0 13.9 %copy-start.1 = (bf16[8,16,4096]{2,1,0:T(8,128)(2,1)S(1)}, bf16[8,16,4096]{2,1,0:T(8,128)(2,1)}, u32[]{:S(2)}) copy-start(bf16[8,16,4096]{2,1,0:T(8,128)(2,1)} %values_ref.3) | copy-start | bytes 3145732
  0.0 13.9 %copy-start.6 = (s32[16]{0:T(128)S(1)}, s32[16]{0:T(128)}, u32[]{:S(2)}) copy-start(s32[16]{0:T(128)} %param.11) | copy-start | bytes 196
  0.0 13.9 %copy-start.4 = (s32[16]{0:T(128)S(1)}, s32[16]{0:T(128)}, u32[]{:S(2)}) copy-start(s32[16]{0:T(128)} %param.10) | copy-start | bytes 196
  0.0 13.9 %copy-start.5 = (s32[16]{0:T(128)S(1)}, s32[16]{0:T(128)}, u32[]{:S(2)}) copy-start(s32[16]{0:T(128)} %param.9) | copy-start | bytes 196
  0.0 13.9 %copy-start.3 = (s32[16,1]{0,1:T(1,128)S(1)}, s32[16,1]{0,1:T(1,128)}, u32[]{:S(2)}) copy-start(s32[16,1]{0,1:T(1,128)} %param.8) | copy-start | bytes 196
  11.7 11.9 %copy-start = (bf16[2,4,128,128]{3,2,1,0:T(8,128)(2,1)S(1)}, bf16[2,4,128,128]{3,2,1,0:T(8,128)(2,1)}, u32[]{:S(2)}) copy-start(bf16[2,4,128,128]{3,2,1,0:T(8,128)(2,1)} %get-tuple-element.17.kept_ref) | copy-start | bytes 786436
  11.7 11.9 %collective-permute-start = (bf16[2,4,128,128]{3,2,1,0:T(8,128)(2,1)}, bf16[2,4,128,128]{3,2,1,0:T(8,128)(2,1)S(1)}, u32[]{:S(2)}, u32[]{:S(2)}) collective-permute-start(bf16[2,4,128,128]{3,2,1,0:T(8,128)(2,1)} %get-tuple-element.18), channel_id=1, source_target_pairs={{0,1},{1,0},{2,3},{3,2},{4,5},{5,4},{6,7},{7,6},{8,9},{9,8},{10,11... | collective-permute-start | bytes 786440 | tf_op jit(solution)/shard_map/ppermute | solution.py:165
  23.6 9.9 %collective-permute-start.6 = (bf16[2,4,128,128]{3,2,1,0:T(8,128)(2,1)S(1)}, bf16[2,4,128,128]{3,2,1,0:T(8,128)(2,1)S(1)}, u32[]{:S(2)}, u32[]{:S(2)}) collective-permute-start(bf16[2,4,128,128]{3,2,1,0:T(8,128)(2,1)S(1)} %get-tuple-element.24), channel_id=1, source_target_pairs={{0,1},{1,0},{2,3},{3,2},{4,5},{5,4},{6,7},{7,6},{8,9},{9,8},{10,11... | collective-permute-start | bytes 786440 | tf_op jit(solution)/shard_map/ppermute | solution.py:165
  23.7 9.8 %collective-permute-start.1 = (bf16[1,4,128,128]{3,2,1,0:T(8,128)(2,1)S(1)}, bf16[1,4,128,128]{3,2,1,0:T(8,128)(2,1)S(1)}, u32[]{:S(2)}, u32[]{:S(2)}) collective-permute-start(bf16[1,4,128,128]{3,2,1,0:T(8,128)(2,1)S(1)} %get-tuple-element.22), channel_id=1, source_target_pairs={{0,2},{1,3},{2,0},{3,1},{4,6},{5,7},{6,4},{7,5},{8,10},{9,11},{10,... | collective-permute-start | bytes 393224 | tf_op jit(solution)/shard_map/ppermute | solution.py:165
  26.2 7.3 %collective-permute-start.2 = (bf16[16,16]{1,0:T(8,128)(2,1)S(1)}, bf16[16,16]{1,0:T(8,128)(2,1)S(1)}, u32[]{:S(2)}, u32[]{:S(2)}) collective-permute-start(bf16[16,16]{1,0:T(8,128)(2,1)S(1)} %get-tuple-element.23.rest_0_), channel_id=1, source_target_pairs={{0,4},{4,0},{8,12},{12,8},{16,20},{20,16},{24,28},{28,24},{1,5},{5... | collective-permute-start | bytes 1544 | tf_op jit(solution)/shard_map/ppermute | solution.py:165
  33.5 8.0 %collective-permute-start.7 = (bf16[1,4,128,128]{3,2,1,0:T(8,128)(2,1)S(1)}, bf16[1,4,128,128]{3,2,1,0:T(8,128)(2,1)S(1)}, u32[]{:S(2)}, u32[]{:S(2)}) collective-permute-start(bf16[1,4,128,128]{3,2,1,0:T(8,128)(2,1)S(1)} %get-tuple-element.26), channel_id=1, source_target_pairs={{0,2},{1,3},{2,0},{3,1},{4,6},{5,7},{6,4},{7,5},{8,10},{9,11},{10,... | collective-permute-start | bytes 393224 | tf_op jit(solution)/shard_map/ppermute | solution.py:165
  33.7 7.8 %collective-permute-start.5 = (bf16[528,128]{1,0:T(8,128)(2,1)S(1)}, bf16[528,128]{1,0:T(8,128)(2,1)S(1)}, u32[]{:S(2)}, u32[]{:S(2)}) collective-permute-start(bf16[528,128]{1,0:T(8,128)(2,1)S(1)} %shard_map.67.rest_0_), channel_id=1, source_target_pairs={{0,24},{4,28},{8,16},{12,20},{16,8},{20,12},{24,0},{28,4},{1,25},{... | collective-permute-start | bytes 405512 | tf_op jit(solution)/shard_map/ppermute | solution.py:165
  35.9 5.6 %collective-permute-start.4 = (bf16[528,128]{1,0:T(8,128)(2,1)S(1)}, bf16[528,128]{1,0:T(8,128)(2,1)S(1)}, u32[]{:S(2)}, u32[]{:S(2)}) collective-permute-start(bf16[528,128]{1,0:T(8,128)(2,1)S(1)} %shard_map.67.rest_0_), channel_id=1, source_target_pairs={{0,16},{4,20},{8,24},{12,28},{16,0},{20,4},{24,8},{28,12},{1,17},{... | collective-permute-start | bytes 405512 | tf_op jit(solution)/shard_map/ppermute | solution.py:165
  36.1 5.4 %collective-permute-start.3 = (bf16[528,128]{1,0:T(8,128)(2,1)S(1)}, bf16[528,128]{1,0:T(8,128)(2,1)S(1)}, u32[]{:S(2)}, u32[]{:S(2)}) collective-permute-start(bf16[528,128]{1,0:T(8,128)(2,1)S(1)} %shard_map.67.rest_0_), channel_id=1, source_target_pairs={{0,8},{4,12},{8,0},{12,4},{16,24},{20,28},{24,16},{28,20},{1,9},{5... | collective-permute-start | bytes 405512 | tf_op jit(solution)/shard_map/ppermute | solution.py:165
  41.7 6.5 %collective-permute-start.10 = (bf16[512,128]{1,0:T(8,128)(2,1)S(1)}, bf16[512,128]{1,0:T(8,128)(2,1)S(1)}, u32[]{:S(2)}, u32[]{:S(2)}) collective-permute-start(bf16[512,128]{1,0:T(8,128)(2,1)S(1)} %get-tuple-element.28), channel_id=1, source_target_pairs={{0,24},{4,28},{8,16},{12,20},{16,8},{20,12},{24,0},{28,4},{1,25},{... | collective-permute-start | bytes 393224 | tf_op jit(solution)/shard_map/ppermute | solution.py:165
  44.0 4.1 %collective-permute-start.9 = (bf16[512,128]{1,0:T(8,128)(2,1)S(1)}, bf16[512,128]{1,0:T(8,128)(2,1)S(1)}, u32[]{:S(2)}, u32[]{:S(2)}) collective-permute-start(bf16[512,128]{1,0:T(8,128)(2,1)S(1)} %get-tuple-element.28), channel_id=1, source_target_pairs={{0,16},{4,20},{8,24},{12,28},{16,0},{20,4},{24,8},{28,12},{1,17},{... | collective-permute-start | bytes 393224 | tf_op jit(solution)/shard_map/ppermute | solution.py:165
  44.3 3.8 %collective-permute-start.8 = (bf16[512,128]{1,0:T(8,128)(2,1)S(1)}, bf16[512,128]{1,0:T(8,128)(2,1)S(1)}, u32[]{:S(2)}, u32[]{:S(2)}) collective-permute-start(bf16[512,128]{1,0:T(8,128)(2,1)S(1)} %get-tuple-element.28), channel_id=1, source_target_pairs={{0,8},{4,12},{8,0},{12,4},{16,24},{20,28},{24,16},{28,20},{1,9},{5... | collective-permute-start | bytes 393224 | tf_op jit(solution)/shard_map/ppermute | solution.py:165
  48.2 6.6 %collective-permute-start.11 = (bf16[8,512,128]{2,1,0:T(8,128)(2,1)S(1)}, bf16[8,512,128]{2,1,0:T(8,128)(2,1)S(1)}, u32[]{:S(2)}, u32[]{:S(2)}) collective-permute-start(bf16[8,512,128]{2,1,0:T(8,128)(2,1)S(1)} %bitcast_dynamic-update-slice_fusion.near_ref), channel_id=1, source_target_pairs={{0,4},{4,0},{8,12},{12,8},{16,20},{20,16},{24,28},{28,24},{1,5},{5... | collective-permute-start | bytes 3145736 | tf_op jit(solution)/shard_map/ppermute | solution.py:165

commit v2 on v1

--- a/solution.py
+++ b/solution.py
@@ -175,36 +175,65 @@
     return kept, arrived
 
 
-def sum_kernel(kept_ref, arrived_ref, *rest, hops):
-    pairs = kept_ref.shape[1]
-    out_ref = rest[hops or 2]
+def turning(chunk_numbers, sub, lanes):
+    row_offsets = chunk_numbers[1:2, sub : sub + 2]
+    col_shifts = chunk_numbers[4:5, sub : sub + 2]
+    to = lax.broadcasted_iota(jnp.int32, (2 * SUB, 2 * SUB), 0)
+    of = lax.broadcasted_iota(jnp.int32, (2 * SUB, 2 * SUB), 1)
+    turned = jnp.where(of < SUB, row_offsets[:, 0:1], row_offsets[:, 1:2]) & (SUBLANES - 1)
+    rows = (to == (of & SUB) + ((of + turned) & (SUB - 1))).astype(jnp.bfloat16)
+    to = lax.broadcasted_iota(jnp.int32, (lanes, LANES), 1)
+    of = lax.broadcasted_iota(jnp.int32, (lanes, LANES), 0)
+    cols = [
+        (to == ((of + col_shifts[:, which : which + 1]) & (LANES - 1))).astype(jnp.bfloat16) for which in range(2)
+    ]
+    return rows, cols
+
+
+def sum_kernel(kept_ref, arrived_ref, numbers_ref, *rest, hops, first_sub):
+    pairs, lanes = kept_ref.shape[1:3]
+    group = min(lanes, LANES)
+    out_ref = rest[hops or 1]
+    numbers = numbers_ref[...].astype(jnp.float32).astype(jnp.int32)
     for pair in range(pairs):
         total = kept_ref[0, pair].astype(jnp.float32) + arrived_ref[0, pair].astype(jnp.float32)
-        out_ref[pair * 2 * SUB : (pair + 1) * 2 * SUB, :] = total.T.astype(jnp.bfloat16)
+        rows, cols = turning(numbers, first_sub + 2 * pair, group)
+        total = lax.dot_general(
+            rows, total.astype(jnp.bfloat16), (((1,), (1,)), ((), ())), preferred_element_type=jnp.float32
+        ).astype(jnp.bfloat16)
+        for which in range(2):
+            at = (pair * 2 + which) * SUB
+            for left in range(0, lanes, group):
+                out_ref[at : at + SUB, left : left + LANES] = jnp.dot(
+                    total[which * SUB : (which + 1) * SUB, left : left + group],
+                    cols[which],
+                    preferred_element_type=jnp.float32,
+                ).astype(jnp.bfloat16)
     if hops:
         near_ref = rest[hops + 1]
         for at in range(hops):
             near_ref[at] = rest[at][: near_ref.shape[1], :]
     else:
-        numbers = [ref[...].astype(jnp.float32) for ref in rest[:2]]
-        blank = jnp.zeros((META, out_ref.shape[1] - 2 * numbers[0].shape[1]), jnp.float32)
-        out_ref[pairs * 2 * SUB :, :] = jnp.concatenate(numbers + [blank], axis=1).astype(jnp.bfloat16)
-
-
-def sum_parts(kept, arrived, hops, numbers):
+        both = [ref[...].astype(jnp.float32) for ref in (numbers_ref, rest[0])]
+        blank = jnp.zeros((META, out_ref.shape[1] - 2 * both[0].shape[1]), jnp.float32)
+        out_ref[pairs * 2 * SUB :, :] = jnp.concatenate(both + [blank], axis=1).astype(jnp.bfloat16)
+
+
+def sum_parts(kept, arrived, first_sub, own_numbers, hops, other_numbers):
     _, pairs, lanes, _ = kept.shape
     rows = pairs * 2 * SUB
+    lanes = max(lanes, LANES)
     out_shape = [jax.ShapeDtypeStruct((rows if hops else rows + META, lanes), jnp.bfloat16)]
     if hops:
         out_shape.append(jax.ShapeDtypeStruct((len(hops), rows, lanes), jnp.bfloat16))
     return pl.pallas_call(
-        functools.partial(sum_kernel, hops=len(hops)),
+        functools.partial(sum_kernel, hops=len(hops), first_sub=first_sub),
         out_shape=out_shape,
-        in_specs=[VMEM] * (2 + len(hops) + len(numbers)),
+        in_specs=[VMEM] * (3 + len(hops) + len(other_numbers)),
         out_specs=[VMEM] * len(out_shape),
         compiler_params=pltpu.CompilerParams(vmem_limit_bytes=8 << 20),
         cost_estimate=pl.CostEstimate(flops=1 << 20, bytes_accessed=2 << 20, transcendentals=0),
-    )(kept, arrived, *hops, *numbers)
+    )(kept, arrived, own_numbers, *hops, *other_numbers)
 
 
 def across(array, axis):
@@ -239,6 +268,7 @@
 def place_kernel(table_ref, near_ref, other_ref, _, out_ref, canvas, sem):
     comp_count = canvas.shape[1]
     number = table_ref[5, 0]
+    row = lax.broadcasted_iota(jnp.int32, (SUB + SUBLANES, LANES), 0)
     lane = lax.broadcasted_iota(jnp.int32, (SUB + SUBLANES, LANES), 1)
 
     def lanes_of(block):
@@ -259,51 +289,47 @@
         def _():
             act()
 
-    def turn(index):
-        start = table_ref[0, index]
-        col = table_ref[1, index]
-        block = table_ref[3, index] // (1 << 16)
-        at = pl.ds(pl.multiple_of(table_ref[3, index] % (1 << 16), SUB), SUB)
-        shift = col % LANES
+    def patch_of(index):
+        spot = table_ref[3, index]
+        block = spot >> 16
+        at = pl.ds(pl.multiple_of(spot & 0xFFFF, SUB), SUB)
         patch = jnp.where((table_ref[4, index] & 16) != 0, other_ref[block, at, :], near_ref[block, at, :])
         patch = patch.astype(jnp.float32)
-        if patch.shape[1] < LANES:
-            patch = jnp.concatenate([patch] * (LANES // patch.shape[1]), axis=1)
-        patch = jnp.concatenate([patch, jnp.zeros((SUBLANES, patch.shape[1]), jnp.float32)], axis=0)
-        patch = pltpu.roll(patch, start % SUBLANES, 0)
-        return [
-            pltpu.roll(
-                patch[:, comp // 2 * LANES : (comp // 2 + 1) * LANES], (shift + comp % 2 * SUB) % LANES, 1
-            )
-            for comp in range(comp_count)
-        ]
-
-    def add_patch(index, turned):
+        patches = []
+        for comp in range(comp_count):
+            values = patch[:, comp // 2 * LANES : (comp // 2 + 1) * LANES]
+            if comp % 2:
+                values = pltpu.roll(values, SUB, 1)
+            patches.append(jnp.concatenate([values, values[:SUBLANES]], axis=0))
+        return patches
+
+    def add_patch(index, patches):
         start = table_ref[0, index]
         col = table_ref[1, index]
         plane = table_ref[2, index]
         flags = table_ref[4, index]
-        block = col // LANES
-        shift = col % LANES
-        rows = pl.ds(pl.multiple_of(start // SUBLANES * SUBLANES, SUBLANES), SUB + SUBLANES)
+        block = col >> 7
+        shift = col & (LANES - 1)
+        skip = start & (SUBLANES - 1)
+        rows = pl.ds(pl.multiple_of(start - skip, SUBLANES), SUB + SUBLANES)
+        inside = (row >= skip) & (row < skip + SUB)
         when_set(flags, 1, lambda: clear(plane, block))
-        here = (lane >= shift) & (lane < shift + SUB)
+        here = inside & (lane >= shift) & (lane < shift + SUB)
         for comp in range(comp_count):
-            canvas[plane, comp, rows, lanes_of(block)] += jnp.where(here, turned[comp], 0.0)
+            canvas[plane, comp, rows, lanes_of(block)] += jnp.where(here, patches[comp], 0.0)
         when_set(flags, 2, lambda: out_copy(plane, block).start())
 
         @pl.when(shift > LANES - SUB)
         def _():
             when_set(flags, 4, lambda: clear(plane, block + 1))
+            there = inside & (lane < shift + SUB - LANES)
             for comp in range(comp_count):
-                canvas[plane, comp, rows, lanes_of(block + 1)] += jnp.where(
-                    lane < shift + SUB - LANES, turned[comp], 0.0
-                )
+                canvas[plane, comp, rows, lanes_of(block + 1)] += jnp.where(there, patches[comp], 0.0)
             when_set(flags, 8, lambda: out_copy(plane, block + 1).start())
 
     def add_two(turn_index, carry):
         index = turn_index * 2
-        first, second = turn(index), turn(index + 1)
+        first, second = patch_of(index), patch_of(index + 1)
         add_patch(index, first)
 
         @pl.when(index + 1 < number)
@@ -313,7 +339,7 @@
         return carry
 
     def finish(index, carry):
-        block = table_ref[1, index] // LANES
+        block = table_ref[1, index] >> 7
         plane = table_ref[2, index]
         flags = table_ref[4, index]
         when_set(flags, 2, lambda: out_copy(plane, block).wait())
@@ -361,10 +387,9 @@
     )
     reduced_a = reduce_over(*parts_a, "tm", parts_b[:1])
     reduced_b = reduce_over(*parts_b, "tm", [])
-    numbers = (own_numbers, paired(own_numbers, "uv", 1))
-    (sum_a,) = sum_parts(*reduced_a, [], numbers)
+    (sum_a,) = sum_parts(*reduced_a, 0, own_numbers, [], [paired(own_numbers, "uv", 1)])
     hops_a = across(sum_a, "uv")
-    sum_b, near_a = sum_parts(*reduced_b, hops_a, ())
+    sum_b, near_a = sum_parts(*reduced_b, half, own_numbers, hops_a, [])
     near = jnp.concatenate([near_a, jnp.stack(across(sum_b, "uv"), axis=0)], axis=0)
     other = paired(near, "uv", 1)
 

time: 62.7 us -> 60.8 us (0.970)
  the two profiles are of different devices: /device:TPU:1 before, /device:TPU:0 now
where the time goes in v2:
time: 60.8 us; the launch traced here: 60.7 us
  Pallas kernels  27.2 us (45%)
  starting transfers between devices  14.7 us (24%)
  waiting for transfers between devices  13.4 us (22%)
  other arithmetic  2.81 us (5%)
  local copies, waits for them, and re-layouts  2.28 us (4%)
    pallas_call x2, Pallas kernels, grid_parts(): pl.pallas_call(functools.partial(grid_kernel, peers=peers, first=first),...  21.4 us
    ppermute x12, starting transfers between devices, paired(): lax.ppermute(array, axis, [(i, i ^ mask) for i in range(lax.axis_size(axi...  14.7 us
    ppermute x12, waiting for transfers between devices, paired(): lax.ppermute(array, axis, [(i, i ^ mask) for i in range(lax.axis_size(axi...  13.4 us
    pallas_call x1, Pallas kernels, place_all(): pl.pallas_call(place_kernel, out_shape=jax.ShapeDtypeStruct(tile_grid.sha...  4.65 us
    reduce_sum x1, other arithmetic, touch_plan(): number = jnp.sum(taken.astype(jnp.int32))  1.42 us
  transfers between devices with their start and end apart: 12, of which 7 were waited for; matrix products, arithmetic and copies ran while one was open for 8% of the time, Pallas kernels for 17%

profile of v2, /device:TPU:0, one launch (start us, length us, event | category | flops | bytes accessed | tf_op | source)
XLA Modules:
  0.0 60.7 jit_solution(16262216422531864054)
XLA Ops:
  0.0 11.7 %shard_map.64 = (bf16[2,4,128,128]{3,2,1,0:T(8,128)(2,1)}, bf16[2,4,128,128]{3,2,1,0:T(8,128)(2,1)}, f32[2,8,128,2048]{3,2,1,0:T(8,128)}) custom-call(s32[1]{0:T(128)} %bitcast.me_ref, bf16[8,16,4096]{2,1,0:T(8,128)(2,1)} %values_ref.3, f32[2,16,4096]{2,1,0:T(8,128)} %places_ref.3), custom_call_target="tpu_custom_call" | custom-call | flops 8589934592 | bytes 2097152 | tf_op jit(solution)/shard_map/pallas_call | solution.py:126
  11.7 3.1 %collective-permute-start = (bf16[2,4,128,128]{3,2,1,0:T(8,128)(2,1)}, bf16[2,4,128,128]{3,2,1,0:T(8,128)(2,1)S(1)}, u32[]{:S(2)}, u32[]{:S(2)}) collective-permute-start(bf16[2,4,128,128]{3,2,1,0:T(8,128)(2,1)} %get-tuple-element.18), channel_id=1, source_target_pairs={{0,1},{1,0},{2,3},{3,2},{4,5},{5,4},{6,7},{7,6},{8,9},{9,8},{10,11... | collective-permute-start | bytes 786440 | tf_op jit(solution)/shard_map/ppermute | solution.py:165
  14.9 9.8 %shard_map.65 = (bf16[2,4,128,128]{3,2,1,0:T(8,128)(2,1)S(1)}, bf16[2,4,128,128]{3,2,1,0:T(8,128)(2,1)S(1)}, bf16[16,16]{1,0:T(8,128)(2,1)S(1)}) custom-call(s32[1]{0:T(128)} %bitcast.me_ref, bf16[8,16,4096]{2,1,0:T(8,128)(2,1)S(1)} %copy-done.1, f32[2,16,4096]{2,1,0:T(8,128)S(1)} %copy-done.2, f32[2,8,128,2048]{3,2,1,0:T(8,128)} %get-tuple-element.19.rest_0_._, ...), custom_call_target="tpu_custom_call" | custom-call | flops 8589934592 | bytes 2097152 | tf_op jit(solution)/shard_map/pallas_call | solution.py:126
  24.8 3.1 %collective-permute-start.1 = (bf16[1,4,128,128]{3,2,1,0:T(8,128)(2,1)S(1)}, bf16[1,4,128,128]{3,2,1,0:T(8,128)(2,1)S(1)}, u32[]{:S(2)}, u32[]{:S(2)}) collective-permute-start(bf16[1,4,128,128]{3,2,1,0:T(8,128)(2,1)S(1)} %get-tuple-element.22), channel_id=1, source_target_pairs={{0,2},{1,3},{2,0},{3,1},{4,6},{5,7},{6,4},{7,5},{8,10},{9,11},{10,... | collective-permute-start | bytes 393224 | tf_op jit(solution)/shard_map/ppermute | solution.py:165
  27.9 7.4 %collective-permute-done.6.arrived_ref = bf16[2,4,128,128]{3,2,1,0:T(8,128)(2,1)S(1)} collective-permute-done((bf16[2,4,128,128]{3,2,1,0:T(8,128)(2,1)S(1)}, bf16[2,4,128,128]{3,2,1,0:T(8,128)(2,1)S(1)}, u32[]{:S(2)}, u32[]{:S(2)}) %collective-permute-start.6) | collective-permute-done | bytes 262176 | tf_op jit(solution)/shard_map/ppermute | solution.py:165
  35.3 1.3 %collective-permute-start.7 = (bf16[1,4,128,128]{3,2,1,0:T(8,128)(2,1)S(1)}, bf16[1,4,128,128]{3,2,1,0:T(8,128)(2,1)S(1)}, u32[]{:S(2)}, u32[]{:S(2)}) collective-permute-start(bf16[1,4,128,128]{3,2,1,0:T(8,128)(2,1)S(1)} %get-tuple-element.26), channel_id=1, source_target_pairs={{0,2},{1,3},{2,0},{3,1},{4,6},{5,7},{6,4},{7,5},{8,10},{9,11},{10,... | collective-permute-start | bytes 393224 | tf_op jit(solution)/shard_map/ppermute | solution.py:165
  36.6 0.5 shard_map.67.rest_0_
  37.1 2.5 %collective-permute-start.5 = (bf16[528,128]{1,0:T(8,128)(2,1)S(1)}, bf16[528,128]{1,0:T(8,128)(2,1)S(1)}, u32[]{:S(2)}, u32[]{:S(2)}) collective-permute-start(bf16[528,128]{1,0:T(8,128)(2,1)S(1)} %shard_map.67.rest_0_), channel_id=1, source_target_pairs={{0,24},{4,28},{8,16},{12,20},{16,8},{20,12},{24,0},{28,4},{1,25},{... | collective-permute-start | bytes 405512 | tf_op jit(solution)/shard_map/ppermute | solution.py:165
  39.6 0.5 collective-permute-start.4
  40.1 0.5 collective-permute-start.3
  40.6 2.3 %collective-permute-done.7.arrived_ref = bf16[1,4,128,128]{3,2,1,0:T(8,128)(2,1)S(1)} collective-permute-done((bf16[1,4,128,128]{3,2,1,0:T(8,128)(2,1)S(1)}, bf16[1,4,128,128]{3,2,1,0:T(8,128)(2,1)S(1)}, u32[]{:S(2)}, u32[]{:S(2)}) %collective-permute-start.7) | collective-permute-done | bytes 131104 | tf_op jit(solution)/shard_map/ppermute | solution.py:165
  42.9 0.7 %collective-permute-done.5.rest_3_ = bf16[528,128]{1,0:T(8,128)(2,1)S(1)} collective-permute-done((bf16[528,128]{1,0:T(8,128)(2,1)S(1)}, bf16[528,128]{1,0:T(8,128)(2,1)S(1)}, u32[]{:S(2)}, u32[]{:S(2)}) %collective-permute-start.5) | collective-permute-done | bytes 135200 | tf_op jit(solution)/shard_map/ppermute | solution.py:165
  43.6 1.4 %collective-permute-done.4.rest_2_ = bf16[528,128]{1,0:T(8,128)(2,1)S(1)} collective-permute-done((bf16[528,128]{1,0:T(8,128)(2,1)S(1)}, bf16[528,128]{1,0:T(8,128)(2,1)S(1)}, u32[]{:S(2)}, u32[]{:S(2)}) %collective-permute-start.4) | collective-permute-done | bytes 135200 | tf_op jit(solution)/shard_map/ppermute | solution.py:165
  45.1 0.5 shard_map.69
  45.6 1.6 %collective-permute-start.10 = (bf16[512,128]{1,0:T(8,128)(2,1)S(1)}, bf16[512,128]{1,0:T(8,128)(2,1)S(1)}, u32[]{:S(2)}, u32[]{:S(2)}) collective-permute-start(bf16[512,128]{1,0:T(8,128)(2,1)S(1)} %get-tuple-element.28), channel_id=1, source_target_pairs={{0,24},{4,28},{8,16},{12,20},{16,8},{20,12},{24,0},{28,4},{1,25},{... | collective-permute-start | bytes 393224 | tf_op jit(solution)/shard_map/ppermute | solution.py:165
  47.1 1.0 %collective-permute-start.9 = (bf16[512,128]{1,0:T(8,128)(2,1)S(1)}, bf16[512,128]{1,0:T(8,128)(2,1)S(1)}, u32[]{:S(2)}, u32[]{:S(2)}) collective-permute-start(bf16[512,128]{1,0:T(8,128)(2,1)S(1)} %get-tuple-element.28), channel_id=1, source_target_pairs={{0,16},{4,20},{8,24},{12,28},{16,0},{20,4},{24,8},{28,12},{1,17},{... | collective-permute-start | bytes 393224 | tf_op jit(solution)/shard_map/ppermute | solution.py:165
  48.1 1.0 %collective-permute-start.8 = (bf16[512,128]{1,0:T(8,128)(2,1)S(1)}, bf16[512,128]{1,0:T(8,128)(2,1)S(1)}, u32[]{:S(2)}, u32[]{:S(2)}) collective-permute-start(bf16[512,128]{1,0:T(8,128)(2,1)S(1)} %get-tuple-element.28), channel_id=1, source_target_pairs={{0,8},{4,12},{8,0},{12,4},{16,24},{20,28},{24,16},{28,20},{1,9},{5... | collective-permute-start | bytes 393224 | tf_op jit(solution)/shard_map/ppermute | solution.py:165
  49.1 0.6 broadcast.1135
  49.7 0.7 %fusion.30 = (s32[4,32]{1,0:T(4,128)S(1)}, s32[1,4,32]{2,0,1:T(1,128)S(1)}, s32[4,32]{1,0:T(4,128)S(1)}, s32[1,4,32]{2,0,1:T(1,128)S(1)}) fusion(s32[]{:T(128)} %broadcast.1135, bf16[16,1,32]{2,0,1:T(8,128)(2,1)S(1)} %slice_bitcast_fusion, bf16[16,1,32]{2,0,1:T(8,128)(2,1)S(1)} %slice_bitcast_fusion.1, bf16[16,1,32]{2,0,1:T(8,128)(2,1)S(1)} %slice_bitcast_fusion.2, ...), kind=kLoop, calls=%fused_computation.105 | loop fusion | flops 3712 | bytes 6148 | tf_op jit(solution)/shard_map/add | solution.py:405
  50.5 1.4 %fusion.9 = (s32[]{:T(128)}, s32[4,32]{1,0:T(4,128)S(1)}, s32[4,32]{1,0:T(4,128)S(1)}, s32[4,32]{1,0:T(4,128)S(1)}, s32[1,4,32]{2,0,1:T(1,128)S(1)}, /*index=5*/bf16[1,4,32]{2,0,1:T(2,128)(2,1)S(1)}) fusion(s32[]{:T(128)} %broadcast.1135, s32[]{:T(128)S(6)} %axis_index.29, bf16[16,1,32]{2,0,1:T(8,128)(2,1)S(1)} %slice_bitcast_fusion, ...), kind=kLoop, calls=%fused_computation.69 | loop fusion | flops 5119 | bytes 6412 | tf_op jit(solution)/shard_map/reduce_sum | solution.py:264
  52.3 0.8 %collective-permute-done.8 = bf16[512,128]{1,0:T(8,128)(2,1)S(1)} collective-permute-done((bf16[512,128]{1,0:T(8,128)(2,1)S(1)}, bf16[512,128]{1,0:T(8,128)(2,1)S(1)}, u32[]{:S(2)}, u32[]{:S(2)}) %collective-permute-start.8) | collective-permute-done | bytes 131104 | tf_op jit(solution)/shard_map/ppermute | solution.py:165
  54.5 0.7 %concatenate.6.table_ref = s32[6,128]{1,0:T(8,128)S(1)} pad(s32[5,128]{1,0:T(8,128)S(1)} %select_reduce_fusion, s32[]{:T(128)} %get-tuple-element.29), padding=0_1x0_0 | pad | bytes 5636 | tf_op jit(solution)/shard_map/concatenate | solution.py:265
  55.2 0.7 %collective-permute-done.11.other_ref = bf16[8,512,128]{2,1,0:T(8,128)(2,1)S(1)} collective-permute-done((bf16[8,512,128]{2,1,0:T(8,128)(2,1)S(1)}, bf16[8,512,128]{2,1,0:T(8,128)(2,1)S(1)}, u32[]{:S(2)}, u32[]{:S(2)}) %collective-permute-start.11) | collective-permute-done | bytes 1048608 | tf_op jit(solution)/shard_map/ppermute | solution.py:165
  55.9 4.7 %shard_map.70 = f32[2,8,128,2048]{3,2,1,0:T(8,128)} custom-call(s32[6,128]{1,0:T(8,128)S(1)} %concatenate.6.table_ref, bf16[8,512,128]{2,1,0:T(8,128)(2,1)S(1)} %bitcast_dynamic-update-slice_fusion.near_ref, bf16[8,512,128]{2,1,0:T(8,128)(2,1)S(1)} %collective-permute-done.11.other_ref, ...), custom_call_target="tpu_custom_call", output_to_operand_aliasing={{}: (3, {})} | custom-call | bytes 16777216 | tf_op jit(solution)/shard_map/pallas_call | solution.py:355
  (53 shorter events, 2.1 us)
Async XLA Ops:
  0.0 14.8 %copy-start.2 = (f32[2,16,4096]{2,1,0:T(8,128)S(1)}, f32[2,16,4096]{2,1,0:T(8,128)}, u32[]{:S(2)}) copy-start(f32[2,16,4096]{2,1,0:T(8,128)} %places_ref.3) | copy-start | bytes 1572868
  0.0 14.8 %copy-start.1 = (bf16[8,16,4096]{2,1,0:T(8,128)(2,1)S(1)}, bf16[8,16,4096]{2,1,0:T(8,128)(2,1)}, u32[]{:S(2)}) copy-start(bf16[8,16,4096]{2,1,0:T(8,128)(2,1)} %values_ref.3) | copy-start | bytes 3145732
  0.0 14.8 %copy-start.6 = (s32[16]{0:T(128)S(1)}, s32[16]{0:T(128)}, u32[]{:S(2)}) copy-start(s32[16]{0:T(128)} %param.11) | copy-start | bytes 196
  0.0 14.8 %copy-start.4 = (s32[16]{0:T(128)S(1)}, s32[16]{0:T(128)}, u32[]{:S(2)}) copy-start(s32[16]{0:T(128)} %param.10) | copy-start | bytes 196
  0.0 14.8 %copy-start.5 = (s32[16]{0:T(128)S(1)}, s32[16]{0:T(128)}, u32[]{:S(2)}) copy-start(s32[16]{0:T(128)} %param.9) | copy-start | bytes 196
  0.0 14.8 %copy-start.3 = (s32[16,1]{0,1:T(1,128)S(1)}, s32[16,1]{0,1:T(1,128)}, u32[]{:S(2)}) copy-start(s32[16,1]{0,1:T(1,128)} %param.8) | copy-start | bytes 196
  11.7 13.0 %copy-start = (bf16[2,4,128,128]{3,2,1,0:T(8,128)(2,1)S(1)}, bf16[2,4,128,128]{3,2,1,0:T(8,128)(2,1)}, u32[]{:S(2)}) copy-start(bf16[2,4,128,128]{3,2,1,0:T(8,128)(2,1)} %get-tuple-element.17.kept_ref) | copy-start | bytes 786436
  11.7 13.0 %collective-permute-start = (bf16[2,4,128,128]{3,2,1,0:T(8,128)(2,1)}, bf16[2,4,128,128]{3,2,1,0:T(8,128)(2,1)S(1)}, u32[]{:S(2)}, u32[]{:S(2)}) collective-permute-start(bf16[2,4,128,128]{3,2,1,0:T(8,128)(2,1)} %get-tuple-element.18), channel_id=1, source_target_pairs={{0,1},{1,0},{2,3},{3,2},{4,5},{5,4},{6,7},{7,6},{8,9},{9,8},{10,11... | collective-permute-start | bytes 786440 | tf_op jit(solution)/shard_map/ppermute | solution.py:165
  24.6 10.6 %collective-permute-start.6 = (bf16[2,4,128,128]{3,2,1,0:T(8,128)(2,1)S(1)}, bf16[2,4,128,128]{3,2,1,0:T(8,128)(2,1)S(1)}, u32[]{:S(2)}, u32[]{:S(2)}) collective-permute-start(bf16[2,4,128,128]{3,2,1,0:T(8,128)(2,1)S(1)} %get-tuple-element.24), channel_id=1, source_target_pairs={{0,1},{1,0},{2,3},{3,2},{4,5},{5,4},{6,7},{7,6},{8,9},{9,8},{10,11... | collective-permute-start | bytes 786440 | tf_op jit(solution)/shard_map/ppermute | solution.py:165
  24.8 11.8 %collective-permute-start.1 = (bf16[1,4,128,128]{3,2,1,0:T(8,128)(2,1)S(1)}, bf16[1,4,128,128]{3,2,1,0:T(8,128)(2,1)S(1)}, u32[]{:S(2)}, u32[]{:S(2)}) collective-permute-start(bf16[1,4,128,128]{3,2,1,0:T(8,128)(2,1)S(1)} %get-tuple-element.22), channel_id=1, source_target_pairs={{0,2},{1,3},{2,0},{3,1},{4,6},{5,7},{6,4},{7,5},{8,10},{9,11},{10,... | collective-permute-start | bytes 393224 | tf_op jit(solution)/shard_map/ppermute | solution.py:165
  27.9 8.7 %collective-permute-start.2 = (bf16[16,16]{1,0:T(8,128)(2,1)S(1)}, bf16[16,16]{1,0:T(8,128)(2,1)S(1)}, u32[]{:S(2)}, u32[]{:S(2)}) collective-permute-start(bf16[16,16]{1,0:T(8,128)(2,1)S(1)} %get-tuple-element.23.numbers_ref), channel_id=1, source_target_pairs={{0,4},{4,0},{8,12},{12,8},{16,20},{20,16},{24,28},{28,24},{1,5},{5... | collective-permute-start | bytes 1544 | tf_op jit(solution)/shard_map/ppermute | solution.py:165
  35.3 7.6 %collective-permute-start.7 = (bf16[1,4,128,128]{3,2,1,0:T(8,128)(2,1)S(1)}, bf16[1,4,128,128]{3,2,1,0:T(8,128)(2,1)S(1)}, u32[]{:S(2)}, u32[]{:S(2)}) collective-permute-start(bf16[1,4,128,128]{3,2,1,0:T(8,128)(2,1)S(1)} %get-tuple-element.26), channel_id=1, source_target_pairs={{0,2},{1,3},{2,0},{3,1},{4,6},{5,7},{6,4},{7,5},{8,10},{9,11},{10,... | collective-permute-start | bytes 393224 | tf_op jit(solution)/shard_map/ppermute | solution.py:165
  37.1 6.5 %collective-permute-start.5 = (bf16[528,128]{1,0:T(8,128)(2,1)S(1)}, bf16[528,128]{1,0:T(8,128)(2,1)S(1)}, u32[]{:S(2)}, u32[]{:S(2)}) collective-permute-start(bf16[528,128]{1,0:T(8,128)(2,1)S(1)} %shard_map.67.rest_0_), channel_id=1, source_target_pairs={{0,24},{4,28},{8,16},{12,20},{16,8},{20,12},{24,0},{28,4},{1,25},{... | collective-permute-start | bytes 405512 | tf_op jit(solution)/shard_map/ppermute | solution.py:165
  39.6 5.4 %collective-permute-start.4 = (bf16[528,128]{1,0:T(8,128)(2,1)S(1)}, bf16[528,128]{1,0:T(8,128)(2,1)S(1)}, u32[]{:S(2)}, u32[]{:S(2)}) collective-permute-start(bf16[528,128]{1,0:T(8,128)(2,1)S(1)} %shard_map.67.rest_0_), channel_id=1, source_target_pairs={{0,16},{4,20},{8,24},{12,28},{16,0},{20,4},{24,8},{28,12},{1,17},{... | collective-permute-start | bytes 405512 | tf_op jit(solution)/shard_map/ppermute | solution.py:165
  40.1 5.0 %collective-permute-start.3 = (bf16[528,128]{1,0:T(8,128)(2,1)S(1)}, bf16[528,128]{1,0:T(8,128)(2,1)S(1)}, u32[]{:S(2)}, u32[]{:S(2)}) collective-permute-start(bf16[528,128]{1,0:T(8,128)(2,1)S(1)} %shard_map.67.rest_0_), channel_id=1, source_target_pairs={{0,8},{4,12},{8,0},{12,4},{16,24},{20,28},{24,16},{28,20},{1,9},{5... | collective-permute-start | bytes 405512 | tf_op jit(solution)/shard_map/ppermute | solution.py:165
  45.6 7.5 %collective-permute-start.10 = (bf16[512,128]{1,0:T(8,128)(2,1)S(1)}, bf16[512,128]{1,0:T(8,128)(2,1)S(1)}, u32[]{:S(2)}, u32[]{:S(2)}) collective-permute-start(bf16[512,128]{1,0:T(8,128)(2,1)S(1)} %get-tuple-element.28), channel_id=1, source_target_pairs={{0,24},{4,28},{8,16},{12,20},{16,8},{20,12},{24,0},{28,4},{1,25},{... | collective-permute-start | bytes 393224 | tf_op jit(solution)/shard_map/ppermute | solution.py:165
  47.1 5.9 %collective-permute-start.9 = (bf16[512,128]{1,0:T(8,128)(2,1)S(1)}, bf16[512,128]{1,0:T(8,128)(2,1)S(1)}, u32[]{:S(2)}, u32[]{:S(2)}) collective-permute-start(bf16[512,128]{1,0:T(8,128)(2,1)S(1)} %get-tuple-element.28), channel_id=1, source_target_pairs={{0,16},{4,20},{8,24},{12,28},{16,0},{20,4},{24,8},{28,12},{1,17},{... | collective-permute-start | bytes 393224 | tf_op jit(solution)/shard_map/ppermute | solution.py:165
  48.1 5.0 %collective-permute-start.8 = (bf16[512,128]{1,0:T(8,128)(2,1)S(1)}, bf16[512,128]{1,0:T(8,128)(2,1)S(1)}, u32[]{:S(2)}, u32[]{:S(2)}) collective-permute-start(bf16[512,128]{1,0:T(8,128)(2,1)S(1)} %get-tuple-element.28), channel_id=1, source_target_pairs={{0,8},{4,12},{8,0},{12,4},{16,24},{20,28},{24,16},{28,20},{1,9},{5... | collective-permute-start | bytes 393224 | tf_op jit(solution)/shard_map/ppermute | solution.py:165
  53.2 2.7 %collective-permute-start.11 = (bf16[8,512,128]{2,1,0:T(8,128)(2,1)S(1)}, bf16[8,512,128]{2,1,0:T(8,128)(2,1)S(1)}, u32[]{:S(2)}, u32[]{:S(2)}) collective-permute-start(bf16[8,512,128]{2,1,0:T(8,128)(2,1)S(1)} %bitcast_dynamic-update-slice_fusion.near_ref), channel_id=1, source_target_pairs={{0,4},{4,0},{8,12},{12,8},{16,20},{20,16},{24,28},{28,24},{1,5},{5... | collective-permute-start | bytes 3145736 | tf_op jit(solution)/shard_map/ppermute | solution.py:165

commit v3 on v2

--- a/solution.py
+++ b/solution.py
@@ -34,7 +34,7 @@
     return jnp.concatenate(rows + [blank], axis=0).astype(jnp.float32).astype(jnp.bfloat16)
 
 
-def grid_kernel(me_ref, values_ref, places_ref, *rest, peers, first):
+def grid_kernel(me_ref, values_ref, places_ref, *rest, peers, first, turns, earlier):
     if first:
         kept_ref, sent_ref, out_ref, values_wide, sums, blank, sem, values, places, in_sem = rest
         _, sub_count, row_count = values.shape
@@ -52,8 +52,15 @@
             copy.start()
         values_ref, places_ref = values, places
     else:
-        _, owner_ref, row_ref, plane_ref, col_ref, kept_ref, sent_ref, numbers_ref, values_wide, sums = rest
-        numbers_ref[...] = number_rows(owner_ref[...], row_ref[...], plane_ref[...], col_ref[...])
+        rest = rest[1:]
+        if earlier:
+            earlier_kept, earlier_sent, kept_ref, sent_ref, values_wide, sums = rest
+            done = earlier_kept.shape[1]
+            kept_ref[:, :done] = earlier_kept[...]
+            sent_ref[:, :done] = earlier_sent[...]
+        else:
+            owner_ref, row_ref, plane_ref, col_ref, kept_ref, sent_ref, numbers_ref, values_wide, sums = rest
+            numbers_ref[...] = number_rows(owner_ref[...], row_ref[...], plane_ref[...], col_ref[...])
     comp_count, sub_count, row_count = values_ref.shape
     rows_each = comp_count // peers * SUB
     for comp in range(comp_count):
@@ -85,18 +92,19 @@
                 target[mask // 2, turn * (STEP // 2) + pair] = sums[pair, rows, :]
         return carry
 
-    lax.fori_loop(0, sub_count // STEP, some_subs, 0)
+    lax.fori_loop(*turns, some_subs, 0)
     if first:
         for copy in zero_copies:
             copy.wait()
 
 
-def grid_parts(values, places, peers, chunk, sub_count, order=None, numbers=()):
+def grid_parts(values, places, peers, chunk, turns, order=None, numbers=(), earlier=()):
     comp_count, all_subs, row_count = values.shape
+    sub_count = all_subs // 2
     rows_each = comp_count // peers * SUB
     first = order is None
     me = lax.axis_index("tm").astype(jnp.int32).reshape(1)
-    parts_shape = (peers // 2, sub_count // 2, rows_each, LANES)
+    parts_shape = (peers // 2, turns[1] * STEP // 2, rows_each, LANES)
     values_block, places_block = (comp_count, sub_count, row_count), (2, sub_count, row_count)
     out_shape = [jax.ShapeDtypeStruct(parts_shape, jnp.bfloat16)] * 2
     out_specs = [pl.BlockSpec(parts_shape, lambda i: (0, 0, 0, 0))] * 2
@@ -117,14 +125,15 @@
         ]
         more = []
     else:
-        whole = pl.BlockSpec((1, all_subs), lambda i: (0, 0))
         in_specs = [pl.BlockSpec(block, lambda i: (0, chunk, 0)) for block in (values_block, places_block)]
-        in_specs += [ANY] + [whole] * len(numbers)
-        out_shape.append(jax.ShapeDtypeStruct((META, all_subs), jnp.bfloat16))
-        out_specs.append(pl.BlockSpec((META, all_subs), lambda i: (0, 0)))
-        more = [order, *numbers]
+        in_specs += [ANY] + [pl.BlockSpec((1, all_subs), lambda i: (0, 0))] * len(numbers)
+        in_specs += [pl.BlockSpec(array.shape, lambda i: (0, 0, 0, 0)) for array in earlier]
+        more = [order, *numbers, *earlier]
+        if numbers:
+            out_shape.append(jax.ShapeDtypeStruct((META, all_subs), jnp.bfloat16))
+            out_specs.append(pl.BlockSpec((META, all_subs), lambda i: (0, 0)))
     return pl.pallas_call(
-        functools.partial(grid_kernel, peers=peers, first=first),
+        functools.partial(grid_kernel, peers=peers, first=first, turns=turns, earlier=bool(earlier)),
         grid=(1,),
         out_shape=out_shape,
         in_specs=[SMEM] + in_specs,
@@ -132,7 +141,7 @@
         scratch_shapes=scratch,
         compiler_params=pltpu.CompilerParams(vmem_limit_bytes=(60 if first else 48) << 20),
         cost_estimate=pl.CostEstimate(
-            flops=8 * sub_count * row_count * SUB * SUB * comp_count,
+            flops=8 * (turns[1] - turns[0]) * STEP * row_count * SUB * SUB * comp_count,
             bytes_accessed=2 << 20,
             transcendentals=0,
         ),
@@ -165,14 +174,12 @@
     return lax.ppermute(array, axis, [(i, i ^ mask) for i in range(lax.axis_size(axis))])
 
 
-def reduce_over(kept, sent, axis, order):
+def halve_all(kept, sent, axis, order):
     mask = 1
-    arrived = paired(sent, axis, mask)
     while kept.shape[0] > 1:
-        kept, sent = halve(kept, arrived, order)
+        kept, sent = halve(kept, paired(sent, axis, mask), order)
         mask *= 2
-        arrived = paired(sent, axis, mask)
-    return kept, arrived
+    return kept, sent
 
 
 def turning(chunk_numbers, sub, lanes):
@@ -375,21 +382,24 @@
     tile = lax.axis_index("uv")
     half = sub_count // 2
 
-    *parts_a, tile_grid = grid_parts(visibilities, positions, peers, 0, half)
+    split = half // STEP // 2
+    *parts_a, tile_grid = grid_parts(visibilities, positions, peers, 0, (0, half // STEP))
     *parts_b, own_numbers = grid_parts(
         visibilities,
         positions,
         peers,
         1,
-        half,
-        tile_grid,
-        (owner.T, row_offset[None], w_plane[None], col_offset[None]),
+        (0, split),
+        order=tile_grid,
+        numbers=(owner.T, row_offset[None], w_plane[None], col_offset[None]),
     )
-    reduced_a = reduce_over(*parts_a, "tm", parts_b[:1])
-    reduced_b = reduce_over(*parts_b, "tm", [])
-    (sum_a,) = sum_parts(*reduced_a, 0, own_numbers, [], [paired(own_numbers, "uv", 1)])
+    kept_a, sent_a = halve_all(*parts_a, "tm", parts_b[:1])
+    parts_b = grid_parts(visibilities, positions, peers, 1, (split, half // STEP), order=sent_a, earlier=parts_b)
+    kept_b, sent_b = halve_all(*parts_b, "tm", [])
+    arrived_a, arrived_b = (paired(sent, "tm", peers // 2) for sent in (sent_a, sent_b))
+    (sum_a,) = sum_parts(kept_a, arrived_a, 0, own_numbers, [], [paired(own_numbers, "uv", 1)])
     hops_a = across(sum_a, "uv")
-    sum_b, near_a = sum_parts(*reduced_b, half, own_numbers, hops_a, [])
+    sum_b, near_a = sum_parts(kept_b, arrived_b, half, own_numbers, hops_a, [])
     near = jnp.concatenate([near_a, jnp.stack(across(sum_b, "uv"), axis=0)], axis=0)
     other = paired(near, "uv", 1)
 

time: 60.8 us -> 63.8 us (1.049); the launches traced: 60.7 us -> 64.6 us
  Pallas kernels: 27.2 us -> 29.3 us
  starting transfers between devices: 14.7 us -> 15.7 us
  waiting for transfers between devices: 13.4 us -> 14.2 us
    pallas_call x1, Pallas kernels: 4.65 us -> 6.78 us  [place_all(): pl.pallas_call(place_kernel, out_shape=jax.ShapeDtypeStruct(tile_grid.sha...]
    ppermute x12, starting transfers between devices: 14.7 us -> 15.7 us  [paired(): lax.ppermute(array, axis, [(i, i ^ mask) for i in range(lax.axis_size(axi...]
    ppermute x12, waiting for transfers between devices: 13.4 us -> 14.2 us  [paired(): lax.ppermute(array, axis, [(i, i ^ mask) for i in range(lax.axis_size(axi...]
    pallas_call x2 -> x3, Pallas kernels: 21.4 us -> 21.4 us  [grid_parts(): pl.pallas_call(functools.partial(grid_kernel, peers=peers, first=first, t...]
  transfers between devices with their start and end apart: 12 -> 12, of which waited for: 7 -> 8; matrix products, arithmetic and copies ran while one was open for 8% -> 8% of each run, Pallas kernels for 17% -> 16%
where the time goes in v3:
time: 63.8 us; the launch traced here: 64.6 us
  Pallas kernels  29.3 us (46%)
  starting transfers between devices  15.7 us (25%)
  waiting for transfers between devices  14.2 us (22%)
  other arithmetic  2.81 us (4%)
  local copies, waits for them, and re-layouts  2.28 us (4%)
    pallas_call x3, Pallas kernels, grid_parts(): pl.pallas_call(functools.partial(grid_kernel, peers=peers, first=first, t...  21.4 us
    ppermute x12, starting transfers between devices, paired(): lax.ppermute(array, axis, [(i, i ^ mask) for i in range(lax.axis_size(axi...  15.7 us
    ppermute x12, waiting for transfers between devices, paired(): lax.ppermute(array, axis, [(i, i ^ mask) for i in range(lax.axis_size(axi...  14.2 us
    pallas_call x1, Pallas kernels, place_all(): pl.pallas_call(place_kernel, out_shape=jax.ShapeDtypeStruct(tile_grid.sha...  6.78 us
    reduce_sum x1, other arithmetic, touch_plan(): number = jnp.sum(taken.astype(jnp.int32))  1.42 us
  transfers between devices with their start and end apart: 12, of which 8 were waited for; matrix products, arithmetic and copies ran while one was open for 8% of the time, Pallas kernels for 16%

profile of v3, /device:TPU:0, one launch (start us, length us, event | category | flops | bytes accessed | tf_op | source)
XLA Modules:
  0.0 64.6 jit_solution(4522105900957212633)
XLA Ops:
  0.0 11.9 %shard_map.64 = (bf16[2,4,128,128]{3,2,1,0:T(8,128)(2,1)}, bf16[2,4,128,128]{3,2,1,0:T(8,128)(2,1)}, f32[2,8,128,2048]{3,2,1,0:T(8,128)}) custom-call(s32[1]{0:T(128)} %bitcast.me_ref, bf16[8,16,4096]{2,1,0:T(8,128)(2,1)} %values_ref.5, f32[2,16,4096]{2,1,0:T(8,128)} %places_ref.5), custom_call_target="tpu_custom_call" | custom-call | flops 8589934592 | bytes 2097152 | tf_op jit(solution)/shard_map/pallas_call | solution.py:135
  11.9 3.1 %collective-permute-start = (bf16[2,4,128,128]{3,2,1,0:T(8,128)(2,1)}, bf16[2,4,128,128]{3,2,1,0:T(8,128)(2,1)S(1)}, u32[]{:S(2)}, u32[]{:S(2)}) collective-permute-start(bf16[2,4,128,128]{3,2,1,0:T(8,128)(2,1)} %get-tuple-element.20), channel_id=1, source_target_pairs={{0,1},{1,0},{2,3},{3,2},{4,5},{5,4},{6,7},{7,6},{8,9},{9,8},{10,11... | collective-permute-start | bytes 786440 | tf_op jit(solution)/shard_map/ppermute | solution.py:174
  15.0 4.8 %shard_map.65 = (bf16[2,2,128,128]{3,2,1,0:T(8,128)(2,1)S(1)}, bf16[2,2,128,128]{3,2,1,0:T(8,128)(2,1)S(1)}, bf16[16,16]{1,0:T(8,128)(2,1)S(1)}) custom-call(s32[1]{0:T(128)} %bitcast.me_ref, bf16[8,16,4096]{2,1,0:T(8,128)(2,1)S(1)} %copy-done, f32[2,16,4096]{2,1,0:T(8,128)S(1)} %copy-done.1, f32[2,8,128,2048]{3,2,1,0:T(8,128)} %get-tuple-element.21.rest_0_._, ...), custom_call_target="tpu_custom_call" | custom-call | flops 4294967296 | bytes 2097152 | tf_op jit(solution)/shard_map/pallas_call | solution.py:135
  19.8 1.7 %collective-permute-done.arrived_ref = bf16[2,4,128,128]{3,2,1,0:T(8,128)(2,1)S(1)} collective-permute-done((bf16[2,4,128,128]{3,2,1,0:T(8,128)(2,1)}, bf16[2,4,128,128]{3,2,1,0:T(8,128)(2,1)S(1)}, u32[]{:S(2)}, u32[]{:S(2)}) %collective-permute-start) | collective-permute-done | bytes 262176 | tf_op jit(solution)/shard_map/ppermute | solution.py:174
  21.6 2.8 %collective-permute-start.1 = (bf16[1,4,128,128]{3,2,1,0:T(8,128)(2,1)S(1)}, bf16[1,4,128,128]{3,2,1,0:T(8,128)(2,1)S(1)}, u32[]{:S(2)}, u32[]{:S(2)}) collective-permute-start(bf16[1,4,128,128]{3,2,1,0:T(8,128)(2,1)S(1)} %get-tuple-element.24.rest_0_), channel_id=1, source_target_pairs={{0,2},{1,3},{2,0},{3,1},{4,6},{5,7},{6,4},{7,5},{8,10},{9,11},{10,... | collective-permute-start | bytes 393224 | tf_op jit(solution)/shard_map/ppermute | solution.py:174
  24.4 4.8 %shard_map.68 = (bf16[2,4,128,128]{3,2,1,0:T(8,128)(2,1)S(1)}, bf16[2,4,128,128]{3,2,1,0:T(8,128)(2,1)S(1)}) custom-call(s32[1]{0:T(128)} %bitcast.me_ref, bf16[8,16,4096]{2,1,0:T(8,128)(2,1)S(1)} %copy-done, f32[2,16,4096]{2,1,0:T(8,128)S(1)} %copy-done.1, bf16[1,4,128,128]{3,2,1,0:T(8,128)(2,1)S(1)} %get-tuple-element.24.rest_0_, ...), custom_call_target="tpu_custom_call" | custom-call | flops 4294967296 | bytes 2097152 | tf_op jit(solution)/shard_map/pallas_call | solution.py:135
  29.2 1.6 %collective-permute-start.6 = (bf16[2,4,128,128]{3,2,1,0:T(8,128)(2,1)S(1)}, bf16[2,4,128,128]{3,2,1,0:T(8,128)(2,1)S(1)}, u32[]{:S(2)}, u32[]{:S(2)}) collective-permute-start(bf16[2,4,128,128]{3,2,1,0:T(8,128)(2,1)S(1)} %get-tuple-element.28), channel_id=1, source_target_pairs={{0,1},{1,0},{2,3},{3,2},{4,5},{5,4},{6,7},{7,6},{8,9},{9,8},{10,11... | collective-permute-start | bytes 786440 | tf_op jit(solution)/shard_map/ppermute | solution.py:174
  30.8 1.2 %collective-permute-done.2.rest_0_ = bf16[16,16]{1,0:T(8,128)(2,1)S(1)} collective-permute-done((bf16[16,16]{1,0:T(8,128)(2,1)S(1)}, bf16[16,16]{1,0:T(8,128)(2,1)S(1)}, u32[]{:S(2)}, u32[]{:S(2)}) %collective-permute-start.2) | collective-permute-done | bytes 544 | tf_op jit(solution)/shard_map/ppermute | solution.py:174
  32.5 2.5 %collective-permute-start.5 = (bf16[528,128]{1,0:T(8,128)(2,1)S(1)}, bf16[528,128]{1,0:T(8,128)(2,1)S(1)}, u32[]{:S(2)}, u32[]{:S(2)}) collective-permute-start(bf16[528,128]{1,0:T(8,128)(2,1)S(1)} %shard_map.67.rest_0_), channel_id=1, source_target_pairs={{0,24},{4,28},{8,16},{12,20},{16,8},{20,12},{24,0},{28,4},{1,25},{... | collective-permute-start | bytes 405512 | tf_op jit(solution)/shard_map/ppermute | solution.py:174
  35.0 0.5 collective-permute-start.4
  35.5 0.5 collective-permute-start.3
  36.2 1.0 %collective-permute-start.7 = (bf16[1,4,128,128]{3,2,1,0:T(8,128)(2,1)S(1)}, bf16[1,4,128,128]{3,2,1,0:T(8,128)(2,1)S(1)}, u32[]{:S(2)}, u32[]{:S(2)}) collective-permute-start(bf16[1,4,128,128]{3,2,1,0:T(8,128)(2,1)S(1)} %get-tuple-element.30), channel_id=1, source_target_pairs={{0,2},{1,3},{2,0},{3,1},{4,6},{5,7},{6,4},{7,5},{8,10},{9,11},{10,... | collective-permute-start | bytes 393224 | tf_op jit(solution)/shard_map/ppermute | solution.py:174
  37.2 2.3 %collective-permute-done.5.rest_3_ = bf16[528,128]{1,0:T(8,128)(2,1)S(1)} collective-permute-done((bf16[528,128]{1,0:T(8,128)(2,1)S(1)}, bf16[528,128]{1,0:T(8,128)(2,1)S(1)}, u32[]{:S(2)}, u32[]{:S(2)}) %collective-permute-start.5) | collective-permute-done | bytes 135200 | tf_op jit(solution)/shard_map/ppermute | solution.py:174
  39.5 2.5 %collective-permute-done.4.rest_2_ = bf16[528,128]{1,0:T(8,128)(2,1)S(1)} collective-permute-done((bf16[528,128]{1,0:T(8,128)(2,1)S(1)}, bf16[528,128]{1,0:T(8,128)(2,1)S(1)}, u32[]{:S(2)}, u32[]{:S(2)}) %collective-permute-start.4) | collective-permute-done | bytes 135200 | tf_op jit(solution)/shard_map/ppermute | solution.py:174
  42.1 0.6 broadcast.1135
  42.7 0.7 %fusion.30 = (s32[4,32]{1,0:T(4,128)S(1)}, s32[1,4,32]{2,0,1:T(1,128)S(1)}, s32[4,32]{1,0:T(4,128)S(1)}, s32[1,4,32]{2,0,1:T(1,128)S(1)}) fusion(s32[]{:T(128)} %broadcast.1135, bf16[16,1,32]{2,0,1:T(8,128)(2,1)S(1)} %slice_bitcast_fusion, bf16[16,1,32]{2,0,1:T(8,128)(2,1)S(1)} %slice_bitcast_fusion.1, bf16[16,1,32]{2,0,1:T(8,128)(2,1)S(1)} %slice_bitcast_fusion.2, ...), kind=kLoop, calls=%fused_computation.105 | loop fusion | flops 3712 | bytes 6148 | tf_op jit(solution)/shard_map/add | solution.py:415
  43.4 1.4 %fusion.9 = (s32[]{:T(128)}, s32[4,32]{1,0:T(4,128)S(1)}, s32[4,32]{1,0:T(4,128)S(1)}, s32[4,32]{1,0:T(4,128)S(1)}, s32[1,4,32]{2,0,1:T(1,128)S(1)}, /*index=5*/bf16[1,4,32]{2,0,1:T(2,128)(2,1)S(1)}) fusion(s32[]{:T(128)} %broadcast.1135, s32[]{:T(128)S(6)} %axis_index.33, bf16[16,1,32]{2,0,1:T(8,128)(2,1)S(1)} %slice_bitcast_fusion, ...), kind=kLoop, calls=%fused_computation.69 | loop fusion | flops 5119 | bytes 6412 | tf_op jit(solution)/shard_map/reduce_sum | solution.py:271
  45.7 1.9 %collective-permute-start.10 = (bf16[512,128]{1,0:T(8,128)(2,1)S(1)}, bf16[512,128]{1,0:T(8,128)(2,1)S(1)}, u32[]{:S(2)}, u32[]{:S(2)}) collective-permute-start(bf16[512,128]{1,0:T(8,128)(2,1)S(1)} %get-tuple-element.32), channel_id=1, source_target_pairs={{0,24},{4,28},{8,16},{12,20},{16,8},{20,12},{24,0},{28,4},{1,25},{... | collective-permute-start | bytes 393224 | tf_op jit(solution)/shard_map/ppermute | solution.py:174
  47.6 1.1 %collective-permute-start.9 = (bf16[512,128]{1,0:T(8,128)(2,1)S(1)}, bf16[512,128]{1,0:T(8,128)(2,1)S(1)}, u32[]{:S(2)}, u32[]{:S(2)}) collective-permute-start(bf16[512,128]{1,0:T(8,128)(2,1)S(1)} %get-tuple-element.32), channel_id=1, source_target_pairs={{0,16},{4,20},{8,24},{12,28},{16,0},{20,4},{24,8},{28,12},{1,17},{... | collective-permute-start | bytes 393224 | tf_op jit(solution)/shard_map/ppermute | solution.py:174
  48.7 0.5 collective-permute-start.8
  49.3 5.6 %collective-permute-done.8 = bf16[512,128]{1,0:T(8,128)(2,1)S(1)} collective-permute-done((bf16[512,128]{1,0:T(8,128)(2,1)S(1)}, bf16[512,128]{1,0:T(8,128)(2,1)S(1)}, u32[]{:S(2)}, u32[]{:S(2)}) %collective-permute-start.8) | collective-permute-done | bytes 131104 | tf_op jit(solution)/shard_map/ppermute | solution.py:174
  56.2 0.7 %concatenate.6.table_ref = s32[6,128]{1,0:T(8,128)S(1)} pad(s32[5,128]{1,0:T(8,128)S(1)} %select_reduce_fusion, s32[]{:T(128)} %get-tuple-element.33), padding=0_1x0_0 | pad | bytes 5636 | tf_op jit(solution)/shard_map/concatenate | solution.py:272
  56.9 0.7 %collective-permute-done.11.other_ref = bf16[8,512,128]{2,1,0:T(8,128)(2,1)S(1)} collective-permute-done((bf16[8,512,128]{2,1,0:T(8,128)(2,1)S(1)}, bf16[8,512,128]{2,1,0:T(8,128)(2,1)S(1)}, u32[]{:S(2)}, u32[]{:S(2)}) %collective-permute-start.11) | collective-permute-done | bytes 1048608 | tf_op jit(solution)/shard_map/ppermute | solution.py:174
  57.7 6.8 %shard_map.71 = f32[2,8,128,2048]{3,2,1,0:T(8,128)} custom-call(s32[6,128]{1,0:T(8,128)S(1)} %concatenate.6.table_ref, bf16[8,512,128]{2,1,0:T(8,128)(2,1)S(1)} %bitcast_dynamic-update-slice_fusion.near_ref, bf16[8,512,128]{2,1,0:T(8,128)(2,1)S(1)} %collective-permute-done.11.other_ref, ...), custom_call_target="tpu_custom_call", output_to_operand_aliasing={{}: (3, {})} | custom-call | bytes 16777216 | tf_op jit(solution)/shard_map/pallas_call | solution.py:362
  (54 shorter events, 3.0 us)
Async XLA Ops:
  0.0 15.0 %copy-start.1 = (f32[2,16,4096]{2,1,0:T(8,128)S(1)}, f32[2,16,4096]{2,1,0:T(8,128)}, u32[]{:S(2)}) copy-start(f32[2,16,4096]{2,1,0:T(8,128)} %places_ref.5) | copy-start | bytes 1572868
  0.0 15.0 %copy-start = (bf16[8,16,4096]{2,1,0:T(8,128)(2,1)S(1)}, bf16[8,16,4096]{2,1,0:T(8,128)(2,1)}, u32[]{:S(2)}) copy-start(bf16[8,16,4096]{2,1,0:T(8,128)(2,1)} %values_ref.5) | copy-start | bytes 3145732
  0.0 15.0 %copy-start.6 = (s32[16]{0:T(128)S(1)}, s32[16]{0:T(128)}, u32[]{:S(2)}) copy-start(s32[16]{0:T(128)} %param.11) | copy-start | bytes 196
  0.0 15.0 %copy-start.4 = (s32[16]{0:T(128)S(1)}, s32[16]{0:T(128)}, u32[]{:S(2)}) copy-start(s32[16]{0:T(128)} %param.10) | copy-start | bytes 196
  0.0 15.0 %copy-start.5 = (s32[16]{0:T(128)S(1)}, s32[16]{0:T(128)}, u32[]{:S(2)}) copy-start(s32[16]{0:T(128)} %param.9) | copy-start | bytes 196
  0.0 15.0 %copy-start.3 = (s32[16,1]{0,1:T(1,128)S(1)}, s32[16,1]{0,1:T(1,128)}, u32[]{:S(2)}) copy-start(s32[16,1]{0,1:T(1,128)} %param.8) | copy-start | bytes 196
  11.9 9.6 %copy-start.2 = (bf16[2,4,128,128]{3,2,1,0:T(8,128)(2,1)S(1)}, bf16[2,4,128,128]{3,2,1,0:T(8,128)(2,1)}, u32[]{:S(2)}) copy-start(bf16[2,4,128,128]{3,2,1,0:T(8,128)(2,1)} %get-tuple-element.19.kept_ref) | copy-start | bytes 786436
  11.9 9.6 %collective-permute-start = (bf16[2,4,128,128]{3,2,1,0:T(8,128)(2,1)}, bf16[2,4,128,128]{3,2,1,0:T(8,128)(2,1)S(1)}, u32[]{:S(2)}, u32[]{:S(2)}) collective-permute-start(bf16[2,4,128,128]{3,2,1,0:T(8,128)(2,1)} %get-tuple-element.20), channel_id=1, source_target_pairs={{0,1},{1,0},{2,3},{3,2},{4,5},{5,4},{6,7},{7,6},{8,9},{9,8},{10,11... | collective-permute-start | bytes 786440 | tf_op jit(solution)/shard_map/ppermute | solution.py:174
  21.6 10.4 %collective-permute-start.1 = (bf16[1,4,128,128]{3,2,1,0:T(8,128)(2,1)S(1)}, bf16[1,4,128,128]{3,2,1,0:T(8,128)(2,1)S(1)}, u32[]{:S(2)}, u32[]{:S(2)}) collective-permute-start(bf16[1,4,128,128]{3,2,1,0:T(8,128)(2,1)S(1)} %get-tuple-element.24.rest_0_), channel_id=1, source_target_pairs={{0,2},{1,3},{2,0},{3,1},{4,6},{5,7},{6,4},{7,5},{8,10},{9,11},{10,... | collective-permute-start | bytes 393224 | tf_op jit(solution)/shard_map/ppermute | solution.py:174
  29.2 7.0 %collective-permute-start.6 = (bf16[2,4,128,128]{3,2,1,0:T(8,128)(2,1)S(1)}, bf16[2,4,128,128]{3,2,1,0:T(8,128)(2,1)S(1)}, u32[]{:S(2)}, u32[]{:S(2)}) collective-permute-start(bf16[2,4,128,128]{3,2,1,0:T(8,128)(2,1)S(1)} %get-tuple-element.28), channel_id=1, source_target_pairs={{0,1},{1,0},{2,3},{3,2},{4,5},{5,4},{6,7},{7,6},{8,9},{9,8},{10,11... | collective-permute-start | bytes 786440 | tf_op jit(solution)/shard_map/ppermute | solution.py:174
  30.8 1.2 %collective-permute-start.2 = (bf16[16,16]{1,0:T(8,128)(2,1)S(1)}, bf16[16,16]{1,0:T(8,128)(2,1)S(1)}, u32[]{:S(2)}, u32[]{:S(2)}) collective-permute-start(bf16[16,16]{1,0:T(8,128)(2,1)S(1)} %get-tuple-element.25.numbers_ref), channel_id=1, source_target_pairs={{0,4},{4,0},{8,12},{12,8},{16,20},{20,16},{24,28},{28,24},{1,5},{5... | collective-permute-start | bytes 1544 | tf_op jit(solution)/shard_map/ppermute | solution.py:174
  32.5 7.0 %collective-permute-start.5 = (bf16[528,128]{1,0:T(8,128)(2,1)S(1)}, bf16[528,128]{1,0:T(8,128)(2,1)S(1)}, u32[]{:S(2)}, u32[]{:S(2)}) collective-permute-start(bf16[528,128]{1,0:T(8,128)(2,1)S(1)} %shard_map.67.rest_0_), channel_id=1, source_target_pairs={{0,24},{4,28},{8,16},{12,20},{16,8},{20,12},{24,0},{28,4},{1,25},{... | collective-permute-start | bytes 405512 | tf_op jit(solution)/shard_map/ppermute | solution.py:174
  35.0 7.0 %collective-permute-start.4 = (bf16[528,128]{1,0:T(8,128)(2,1)S(1)}, bf16[528,128]{1,0:T(8,128)(2,1)S(1)}, u32[]{:S(2)}, u32[]{:S(2)}) collective-permute-start(bf16[528,128]{1,0:T(8,128)(2,1)S(1)} %shard_map.67.rest_0_), channel_id=1, source_target_pairs={{0,16},{4,20},{8,24},{12,28},{16,0},{20,4},{24,8},{28,12},{1,17},{... | collective-permute-start | bytes 405512 | tf_op jit(solution)/shard_map/ppermute | solution.py:174
  35.5 6.6 %collective-permute-start.3 = (bf16[528,128]{1,0:T(8,128)(2,1)S(1)}, bf16[528,128]{1,0:T(8,128)(2,1)S(1)}, u32[]{:S(2)}, u32[]{:S(2)}) collective-permute-start(bf16[528,128]{1,0:T(8,128)(2,1)S(1)} %shard_map.67.rest_0_), channel_id=1, source_target_pairs={{0,8},{4,12},{8,0},{12,4},{16,24},{20,28},{24,16},{28,20},{1,9},{5... | collective-permute-start | bytes 405512 | tf_op jit(solution)/shard_map/ppermute | solution.py:174
  36.2 9.0 %collective-permute-start.7 = (bf16[1,4,128,128]{3,2,1,0:T(8,128)(2,1)S(1)}, bf16[1,4,128,128]{3,2,1,0:T(8,128)(2,1)S(1)}, u32[]{:S(2)}, u32[]{:S(2)}) collective-permute-start(bf16[1,4,128,128]{3,2,1,0:T(8,128)(2,1)S(1)} %get-tuple-element.30), channel_id=1, source_target_pairs={{0,2},{1,3},{2,0},{3,1},{4,6},{5,7},{6,4},{7,5},{8,10},{9,11},{10,... | collective-permute-start | bytes 393224 | tf_op jit(solution)/shard_map/ppermute | solution.py:174
  45.7 9.2 %collective-permute-start.10 = (bf16[512,128]{1,0:T(8,128)(2,1)S(1)}, bf16[512,128]{1,0:T(8,128)(2,1)S(1)}, u32[]{:S(2)}, u32[]{:S(2)}) collective-permute-start(bf16[512,128]{1,0:T(8,128)(2,1)S(1)} %get-tuple-element.32), channel_id=1, source_target_pairs={{0,24},{4,28},{8,16},{12,20},{16,8},{20,12},{24,0},{28,4},{1,25},{... | collective-permute-start | bytes 393224 | tf_op jit(solution)/shard_map/ppermute | solution.py:174
  47.6 7.3 %collective-permute-start.9 = (bf16[512,128]{1,0:T(8,128)(2,1)S(1)}, bf16[512,128]{1,0:T(8,128)(2,1)S(1)}, u32[]{:S(2)}, u32[]{:S(2)}) collective-permute-start(bf16[512,128]{1,0:T(8,128)(2,1)S(1)} %get-tuple-element.32), channel_id=1, source_target_pairs={{0,16},{4,20},{8,24},{12,28},{16,0},{20,4},{24,8},{28,12},{1,17},{... | collective-permute-start | bytes 393224 | tf_op jit(solution)/shard_map/ppermute | solution.py:174
  48.7 6.2 %collective-permute-start.8 = (bf16[512,128]{1,0:T(8,128)(2,1)S(1)}, bf16[512,128]{1,0:T(8,128)(2,1)S(1)}, u32[]{:S(2)}, u32[]{:S(2)}) collective-permute-start(bf16[512,128]{1,0:T(8,128)(2,1)S(1)} %get-tuple-element.32), channel_id=1, source_target_pairs={{0,8},{4,12},{8,0},{12,4},{16,24},{20,28},{24,16},{28,20},{1,9},{5... | collective-permute-start | bytes 393224 | tf_op jit(solution)/shard_map/ppermute | solution.py:174
  55.0 2.7 %collective-permute-start.11 = (bf16[8,512,128]{2,1,0:T(8,128)(2,1)S(1)}, bf16[8,512,128]{2,1,0:T(8,128)(2,1)S(1)}, u32[]{:S(2)}, u32[]{:S(2)}) collective-permute-start(bf16[8,512,128]{2,1,0:T(8,128)(2,1)S(1)} %bitcast_dynamic-update-slice_fusion.near_ref), channel_id=1, source_target_pairs={{0,4},{4,0},{8,12},{12,8},{16,20},{20,16},{24,28},{28,24},{1,5},{5... | collective-permute-start | bytes 3145736 | tf_op jit(solution)/shard_map/ppermute | solution.py:174

commit v4 on v2

--- a/solution.py
+++ b/solution.py
@@ -16,7 +16,6 @@
 SUBLANES = 8
 BLOCKS = NV // LANES
 META = 16
-STEP = 4
 
 VMEM = pl.BlockSpec(memory_space=pltpu.VMEM)
 SMEM = pl.BlockSpec(memory_space=pltpu.SMEM)
@@ -34,20 +33,21 @@
     return jnp.concatenate(rows + [blank], axis=0).astype(jnp.float32).astype(jnp.bfloat16)
 
 
-def grid_kernel(me_ref, values_ref, places_ref, *rest, peers, first):
+def grid_kernel(me_ref, values_ref, places_ref, *rest, peers, first, base, turns):
     if first:
         kept_ref, sent_ref, out_ref, values_wide, sums, blank, sem, values, places, in_sem = rest
-        _, sub_count, row_count = values.shape
-        in_copies = [
-            pltpu.make_async_copy(values_ref.at[:, pl.ds(0, sub_count), :], values, in_sem.at[0]),
-            pltpu.make_async_copy(places_ref.at[:, pl.ds(0, sub_count), :], places, in_sem.at[1]),
-        ]
+        all_subs = values.shape[1]
+        in_copies = []
+        for part in range(2):
+            some = pl.ds(part * all_subs // 2, all_subs // 2)
+            in_copies += [
+                pltpu.make_async_copy(places_ref.at[:, some, :], places.at[:, some, :], in_sem.at[part, 0]),
+                pltpu.make_async_copy(values_ref.at[:, some, :], values.at[:, some, :], in_sem.at[part, 1]),
+            ]
         for copy in in_copies:
             copy.start()
         blank[...] = jnp.zeros(blank.shape, jnp.float32)
         zero_copies = [pltpu.make_async_copy(blank, out_ref.at[:, plane], sem.at[plane]) for plane in range(W)]
-        for copy in in_copies:
-            copy.wait()
         for copy in zero_copies:
             copy.start()
         values_ref, places_ref = values, places
@@ -56,9 +56,12 @@
         numbers_ref[...] = number_rows(owner_ref[...], row_ref[...], plane_ref[...], col_ref[...])
     comp_count, sub_count, row_count = values_ref.shape
     rows_each = comp_count // peers * SUB
-    for comp in range(comp_count):
-        values_wide[comp * sub_count : (comp + 1) * sub_count, :] = values_ref[comp].astype(jnp.float32)
     cells = lax.broadcasted_iota(jnp.int32, (SUB, row_count), 0).astype(jnp.float32) * (2.0 / TAPS)
+
+    def widen(low, high):
+        for comp in range(comp_count):
+            at = comp * sub_count
+            values_wide[at + low : at + high, :] = values_ref[comp, low:high, :].astype(jnp.float32)
 
     def one_sub(sub):
         row_taps = taper(cells - places_ref[0, pl.ds(sub, 1), :] * (2.0 / TAPS)).astype(jnp.bfloat16)
@@ -74,38 +77,50 @@
             weighted, row_taps, (((1,), (1,)), ((), ())), preferred_element_type=jnp.float32
         )
 
-    def some_subs(turn, carry):
-        for pair in range(STEP // 2):
-            sub = turn * STEP + pair * 2
-            sums[pair] = jnp.concatenate([one_sub(sub), one_sub(sub + 1)], axis=1).astype(jnp.bfloat16)
-        for pair in range(STEP // 2):
-            for mask in range(peers):
-                rows = pl.ds(pl.multiple_of((me_ref[0] ^ mask) * rows_each, rows_each), rows_each)
-                target = sent_ref if mask % 2 else kept_ref
-                target[mask // 2, turn * (STEP // 2) + pair] = sums[pair, rows, :]
-        return carry
-
-    lax.fori_loop(0, sub_count // STEP, some_subs, 0)
+    def some_subs(low, step):
+        def run(turn, carry):
+            for pair in range(step // 2):
+                sub = low + turn * step + pair * 2
+                sums[pair] = jnp.concatenate([one_sub(sub), one_sub(sub + 1)], axis=1).astype(jnp.bfloat16)
+            for pair in range(step // 2):
+                for mask in range(peers):
+                    rows = pl.ds(pl.multiple_of((me_ref[0] ^ mask) * rows_each, rows_each), rows_each)
+                    target = sent_ref if mask % 2 else kept_ref
+                    target[mask // 2, (low - base) // 2 + turn * (step // 2) + pair] = sums[pair, rows, :]
+            return carry
+
+        return run
+
+    for part, (low, high, step) in enumerate(turns):
+        if first:
+            for copy in in_copies[2 * part : 2 * part + 2]:
+                copy.wait()
+            widen(part * all_subs // 2, (part + 1) * all_subs // 2)
+        else:
+            widen(0, sub_count)
+        lax.fori_loop(0, (high - low) // step, some_subs(low, step), 0)
     if first:
         for copy in zero_copies:
             copy.wait()
 
 
-def grid_parts(values, places, peers, chunk, sub_count, order=None, numbers=()):
+def grid_parts(values, places, peers, base, turns, order=None, numbers=()):
     comp_count, all_subs, row_count = values.shape
     rows_each = comp_count // peers * SUB
     first = order is None
     me = lax.axis_index("tm").astype(jnp.int32).reshape(1)
-    parts_shape = (peers // 2, sub_count // 2, rows_each, LANES)
-    values_block, places_block = (comp_count, sub_count, row_count), (2, sub_count, row_count)
+    parts_shape = (peers // 2, (turns[-1][1] - base) // 2, rows_each, LANES)
+    read = all_subs if first else all_subs // 2
+    values_block, places_block = (comp_count, read, row_count), (2, read, row_count)
     out_shape = [jax.ShapeDtypeStruct(parts_shape, jnp.bfloat16)] * 2
     out_specs = [pl.BlockSpec(parts_shape, lambda i: (0, 0, 0, 0))] * 2
     scratch = [
-        pltpu.VMEM((comp_count * sub_count, row_count), jnp.float32),
-        pltpu.VMEM((STEP // 2, comp_count * SUB, LANES), jnp.bfloat16),
+        pltpu.VMEM((comp_count * read, row_count), jnp.float32),
+        pltpu.VMEM((max(step for _, _, step in turns) // 2, comp_count * SUB, LANES), jnp.bfloat16),
     ]
     if first:
-        in_specs = [ANY] * 2
+        values, places = (pltpu.with_memory_space_constraint(array, pltpu.HBM) for array in (values, places))
+        in_specs = [pl.BlockSpec(memory_space=pltpu.HBM)] * 2
         out_shape.append(jax.ShapeDtypeStruct((rows_each // SUB, W, TU, NV), jnp.float32))
         out_specs.append(ANY)
         scratch += [
@@ -113,26 +128,26 @@
             pltpu.SemaphoreType.DMA((W,)),
             pltpu.VMEM(values_block, values.dtype),
             pltpu.VMEM(places_block, places.dtype),
-            pltpu.SemaphoreType.DMA((2,)),
+            pltpu.SemaphoreType.DMA((2, 2)),
         ]
         more = []
     else:
         whole = pl.BlockSpec((1, all_subs), lambda i: (0, 0))
-        in_specs = [pl.BlockSpec(block, lambda i: (0, chunk, 0)) for block in (values_block, places_block)]
+        in_specs = [pl.BlockSpec(block, lambda i: (0, 1, 0)) for block in (values_block, places_block)]
         in_specs += [ANY] + [whole] * len(numbers)
         out_shape.append(jax.ShapeDtypeStruct((META, all_subs), jnp.bfloat16))
         out_specs.append(pl.BlockSpec((META, all_subs), lambda i: (0, 0)))
         more = [order, *numbers]
     return pl.pallas_call(
-        functools.partial(grid_kernel, peers=peers, first=first),
+        functools.partial(grid_kernel, peers=peers, first=first, base=base, turns=turns),
         grid=(1,),
         out_shape=out_shape,
         in_specs=[SMEM] + in_specs,
         out_specs=out_specs,
         scratch_shapes=scratch,
-        compiler_params=pltpu.CompilerParams(vmem_limit_bytes=(60 if first else 48) << 20),
+        compiler_params=pltpu.CompilerParams(vmem_limit_bytes=48 << 20),
         cost_estimate=pl.CostEstimate(
-            flops=8 * sub_count * row_count * SUB * SUB * comp_count,
+            flops=64 * row_count * SUB * SUB * comp_count,
             bytes_accessed=2 << 20,
             transcendentals=0,
         ),
@@ -225,7 +240,7 @@
     lanes = max(lanes, LANES)
     out_shape = [jax.ShapeDtypeStruct((rows if hops else rows + META, lanes), jnp.bfloat16)]
     if hops:
-        out_shape.append(jax.ShapeDtypeStruct((len(hops), rows, lanes), jnp.bfloat16))
+        out_shape.append(jax.ShapeDtypeStruct((len(hops), hops[0].shape[0] - META, lanes), jnp.bfloat16))
     return pl.pallas_call(
         functools.partial(sum_kernel, hops=len(hops), first_sub=first_sub),
         out_shape=out_shape,
@@ -373,15 +388,18 @@
     sub_count = visibilities.shape[1]
     comp_count = visibilities.shape[0] // peers
     tile = lax.axis_index("uv")
-    half = sub_count // 2
-
-    *parts_a, tile_grid = grid_parts(visibilities, positions, peers, 0, half)
+    half, more = sub_count // 2, sub_count // 8
+    cut = half + more
+
+    *parts_a, tile_grid = grid_parts(
+        visibilities, positions, peers, 0, ((0, half, half // 2), (half, cut, more))
+    )
     *parts_b, own_numbers = grid_parts(
         visibilities,
         positions,
         peers,
-        1,
-        half,
+        more,
+        ((more, half, half - more),),
         tile_grid,
         (owner.T, row_offset[None], w_plane[None], col_offset[None]),
     )
@@ -389,17 +407,15 @@
     reduced_b = reduce_over(*parts_b, "tm", [])
     (sum_a,) = sum_parts(*reduced_a, 0, own_numbers, [], [paired(own_numbers, "uv", 1)])
     hops_a = across(sum_a, "uv")
-    sum_b, near_a = sum_parts(*reduced_b, half, own_numbers, hops_a, [])
-    near = jnp.concatenate([near_a, jnp.stack(across(sum_b, "uv"), axis=0)], axis=0)
+    sum_b, near_a = sum_parts(*reduced_b, cut, own_numbers, hops_a, [])
+    near = jnp.concatenate([near_a, jnp.stack(across(sum_b, "uv"), axis=0)], axis=1)
     other = paired(near, "uv", 1)
 
-    told = jnp.stack([hop[half * SUB :, : 2 * sub_count] for hop in hops_a], axis=1).astype(jnp.float32).astype(jnp.int32)
-    chips = told.shape[1]
+    told = jnp.stack([hop[cut * SUB :, : 2 * sub_count] for hop in hops_a], axis=1).astype(jnp.float32).astype(jnp.int32)
     told = told.reshape(META, -1)
     entry = jnp.arange(told.shape[1], dtype=jnp.int32)
-    chip, sub = entry // (2 * sub_count), entry % sub_count
-    others = entry // sub_count % 2
-    spots = ((sub // half * chips + chip) << 16) + sub % half * SUB
+    chip, others, sub = entry // (2 * sub_count), entry // sub_count % 2, entry % sub_count
+    spots = (chip << 16) + sub * SUB
     ahead = (told[0] - tile) % tiles
     starts = jnp.where(ahead == 0, told[1] + SUB, jnp.where(ahead == tiles - 1, told[1] + SUB - TU, -1))
     table = touch_plan(starts, told[2], told[3] * LANES + told[4], spots, others)

time: 60.8 us -> 66 us (1.086)
  the two profiles are of different devices: /device:TPU:0 before, /device:TPU:25 now
where the time goes in v4:
time: 66 us
  Pallas kernels  29.5 us (45%)
  starting transfers between devices  19.5 us (30%)
  waiting for transfers between devices  11.8 us (18%)
  other arithmetic  2.79 us (4%)
  local copies, waits for them, and re-layouts  2.03 us (3%)
    pallas_call x2, Pallas kernels, grid_parts(): pl.pallas_call(functools.partial(grid_kernel, peers=peers, first=first, b...  21.5 us
    ppermute x12, starting transfers between devices, paired(): lax.ppermute(array, axis, [(i, i ^ mask) for i in range(lax.axis_size(axi...  19.5 us
    ppermute x12, waiting for transfers between devices, paired(): lax.ppermute(array, axis, [(i, i ^ mask) for i in range(lax.axis_size(axi...  11.8 us
    pallas_call x1, Pallas kernels, place_all(): pl.pallas_call(place_kernel, out_shape=jax.ShapeDtypeStruct(tile_grid.sha...  6.89 us
    reduce_sum x1, other arithmetic, touch_plan(): number = jnp.sum(taken.astype(jnp.int32))  1.33 us
  transfers between devices with their start and end apart: 12, of which 8 were waited for; matrix products, arithmetic and copies ran while one was open for 7% of the time, Pallas kernels for 12%

profile of v4, /device:TPU:25, one launch (start us, length us, event | category | flops | bytes accessed | tf_op | source)
XLA Modules:
  0.0 66.0 jit_solution(10120479679602285906)
XLA Ops:
  0.0 14.5 %shard_map.64 = (bf16[2,5,128,128]{3,2,1,0:T(8,128)(2,1)S(1)}, bf16[2,5,128,128]{3,2,1,0:T(8,128)(2,1)S(1)}, f32[2,8,128,2048]{3,2,1,0:T(8,128)}) custom-call(s32[1]{0:T(128)} %bitcast.me_ref, bf16[8,16,4096]{2,1,0:T(8,128)(2,1)} %values_ref.3, f32[2,16,4096]{2,1,0:T(8,128)} %places_ref.3), custom_call_target="tpu_custom_call" | custom-call | flops 8589934592 | bytes 2097152 | tf_op jit(solution)/shard_map/pallas_call | solution.py:141
  14.5 0.2 collective-permute-start
  14.8 7.0 %shard_map.65 = (bf16[2,3,128,128]{3,2,1,0:T(8,128)(2,1)S(1)}, bf16[2,3,128,128]{3,2,1,0:T(8,128)(2,1)S(1)}, bf16[16,16]{1,0:T(8,128)(2,1)S(1)}) custom-call(s32[1]{0:T(128)} %bitcast.me_ref, bf16[8,16,4096]{2,1,0:T(8,128)(2,1)S(1)} %copy-done, f32[2,16,4096]{2,1,0:T(8,128)S(1)} %copy-done.1, f32[2,8,128,2048]{3,2,1,0:T(8,128)} %get-tuple-element.19.rest_0_._, ...), custom_call_target="tpu_custom_call" | custom-call | flops 8589934592 | bytes 2097152 | tf_op jit(solution)/shard_map/pallas_call | solution.py:141
  21.9 1.4 %collective-permute-start.6 = (bf16[2,3,128,128]{3,2,1,0:T(8,128)(2,1)S(1)}, bf16[2,3,128,128]{3,2,1,0:T(8,128)(2,1)S(1)}, u32[]{:S(2)}, u32[]{:S(2)}) collective-permute-start(bf16[2,3,128,128]{3,2,1,0:T(8,128)(2,1)S(1)} %get-tuple-element.24), channel_id=1, source_target_pairs={{0,1},{1,0},{2,3},{3,2},{4,5},{5,4},{6,7},{7,6},{8,9},{9,8},{10,11... | collective-permute-start | bytes 589832 | tf_op jit(solution)/shard_map/ppermute | solution.py:180
  23.4 1.8 %collective-permute-start.2 = (bf16[16,16]{1,0:T(8,128)(2,1)S(1)}, bf16[16,16]{1,0:T(8,128)(2,1)S(1)}, u32[]{:S(2)}, u32[]{:S(2)}) collective-permute-start(bf16[16,16]{1,0:T(8,128)(2,1)S(1)} %get-tuple-element.23.numbers_ref), channel_id=1, source_target_pairs={{0,4},{4,0},{8,12},{12,8},{16,20},{20,16},{24,28},{28,24},{1,5},{5... | collective-permute-start | bytes 1544 | tf_op jit(solution)/shard_map/ppermute | solution.py:180
  25.2 2.9 %collective-permute-done.6.arrived_ref = bf16[2,3,128,128]{3,2,1,0:T(8,128)(2,1)S(1)} collective-permute-done((bf16[2,3,128,128]{3,2,1,0:T(8,128)(2,1)S(1)}, bf16[2,3,128,128]{3,2,1,0:T(8,128)(2,1)S(1)}, u32[]{:S(2)}, u32[]{:S(2)}) %collective-permute-start.6) | collective-permute-done | bytes 196640 | tf_op jit(solution)/shard_map/ppermute | solution.py:180
  28.2 2.0 %collective-permute-start.7 = (bf16[1,3,128,128]{3,2,1,0:T(8,128)(2,1)S(1)}, bf16[1,3,128,128]{3,2,1,0:T(8,128)(2,1)S(1)}, u32[]{:S(2)}, u32[]{:S(2)}) collective-permute-start(bf16[1,3,128,128]{3,2,1,0:T(8,128)(2,1)S(1)} %get-tuple-element.26), channel_id=1, source_target_pairs={{0,2},{1,3},{2,0},{3,1},{4,6},{5,7},{6,4},{7,5},{8,10},{9,11},{10,... | collective-permute-start | bytes 294920 | tf_op jit(solution)/shard_map/ppermute | solution.py:180
  30.2 2.6 %collective-permute-done.1.arrived_ref = bf16[1,5,128,128]{3,2,1,0:T(8,128)(2,1)S(1)} collective-permute-done((bf16[1,5,128,128]{3,2,1,0:T(8,128)(2,1)S(1)}, bf16[1,5,128,128]{3,2,1,0:T(8,128)(2,1)S(1)}, u32[]{:S(2)}, u32[]{:S(2)}) %collective-permute-start.1) | collective-permute-done | bytes 163872 | tf_op jit(solution)/shard_map/ppermute | solution.py:180
  32.8 0.5 shard_map.67.rest_0_
  33.3 2.3 %collective-permute-start.5 = (bf16[656,128]{1,0:T(8,128)(2,1)S(1)}, bf16[656,128]{1,0:T(8,128)(2,1)S(1)}, u32[]{:S(2)}, u32[]{:S(2)}) collective-permute-start(bf16[656,128]{1,0:T(8,128)(2,1)S(1)} %shard_map.67.rest_0_), channel_id=1, source_target_pairs={{0,24},{4,28},{8,16},{12,20},{16,8},{20,12},{24,0},{28,4},{1,25},{... | collective-permute-start | bytes 503816 | tf_op jit(solution)/shard_map/ppermute | solution.py:180
  35.6 0.2 collective-permute-start.4
  36.0 2.5 %collective-permute-done.5.rest_3_ = bf16[656,128]{1,0:T(8,128)(2,1)S(1)} collective-permute-done((bf16[656,128]{1,0:T(8,128)(2,1)S(1)}, bf16[656,128]{1,0:T(8,128)(2,1)S(1)}, u32[]{:S(2)}, u32[]{:S(2)}) %collective-permute-start.5) | collective-permute-done | bytes 167968 | tf_op jit(solution)/shard_map/ppermute | solution.py:180
  38.5 1.8 %collective-permute-done.4.rest_2_ = bf16[656,128]{1,0:T(8,128)(2,1)S(1)} collective-permute-done((bf16[656,128]{1,0:T(8,128)(2,1)S(1)}, bf16[656,128]{1,0:T(8,128)(2,1)S(1)}, u32[]{:S(2)}, u32[]{:S(2)}) %collective-permute-start.4) | collective-permute-done | bytes 167968 | tf_op jit(solution)/shard_map/ppermute | solution.py:180
  40.4 0.4 shard_map.69
  40.9 1.4 %collective-permute-start.10 = (bf16[384,128]{1,0:T(8,128)(2,1)S(1)}, bf16[384,128]{1,0:T(8,128)(2,1)S(1)}, u32[]{:S(2)}, u32[]{:S(2)}) collective-permute-start(bf16[384,128]{1,0:T(8,128)(2,1)S(1)} %get-tuple-element.28), channel_id=1, source_target_pairs={{0,24},{4,28},{8,16},{12,20},{16,8},{20,12},{24,0},{28,4},{1,25},{... | collective-permute-start | bytes 294920 | tf_op jit(solution)/shard_map/ppermute | solution.py:180
  42.2 1.1 %collective-permute-start.9 = (bf16[384,128]{1,0:T(8,128)(2,1)S(1)}, bf16[384,128]{1,0:T(8,128)(2,1)S(1)}, u32[]{:S(2)}, u32[]{:S(2)}) collective-permute-start(bf16[384,128]{1,0:T(8,128)(2,1)S(1)} %get-tuple-element.28), channel_id=1, source_target_pairs={{0,16},{4,20},{8,24},{12,28},{16,0},{20,4},{24,8},{28,12},{1,17},{... | collective-permute-start | bytes 294920 | tf_op jit(solution)/shard_map/ppermute | solution.py:180
  43.6 0.6 broadcast.1054
  44.2 1.3 %fusion.9 = (s32[]{:T(128)}, s32[4,32]{1,0:T(4,128)S(1)}, s32[4,32]{1,0:T(4,128)S(1)}, s32[4,32]{1,0:T(4,128)S(1)}, s32[1,4,32]{2,0,1:T(1,128)S(1)}, /*index=5*/bf16[1,4,32]{2,0,1:T(2,128)(2,1)S(1)}) fusion(s32[]{:T(128)} %broadcast.1054, s32[]{:T(128)S(6)} %axis_index.29, bf16[16,1,32]{2,0,1:T(8,128)(2,1)S(1)} %slice_bitcast_fusion, ...), kind=kLoop, calls=%fused_computation.63 | loop fusion | flops 5119 | bytes 6412 | tf_op jit(solution)/shard_map/reduce_sum | solution.py:279
  45.6 0.7 %fusion.29 = (s32[4,32]{1,0:T(4,128)S(1)}, s32[1,4,32]{2,0,1:T(1,128)S(1)}, s32[4,32]{1,0:T(4,128)S(1)}, s32[1,4,32]{2,0,1:T(1,128)S(1)}) fusion(s32[]{:T(128)} %broadcast.1054, bf16[16,1,32]{2,0,1:T(8,128)(2,1)S(1)} %slice_bitcast_fusion, bf16[16,1,32]{2,0,1:T(8,128)(2,1)S(1)} %slice_bitcast_fusion.1, bf16[16,1,32]{2,0,1:T(8,128)(2,1)S(1)} %slice_bitcast_fusion.2, ...), kind=kLoop, calls=%fused_computation.95 | loop fusion | flops 3712 | bytes 6148 | tf_op jit(solution)/shard_map/add | solution.py:421
  46.6 1.2 %collective-permute-done.9 = bf16[384,128]{1,0:T(8,128)(2,1)S(1)} collective-permute-done((bf16[384,128]{1,0:T(8,128)(2,1)S(1)}, bf16[384,128]{1,0:T(8,128)(2,1)S(1)}, u32[]{:S(2)}, u32[]{:S(2)}) %collective-permute-start.9) | collective-permute-done | bytes 98336 | tf_op jit(solution)/shard_map/ppermute | solution.py:180
  48.0 8.6 %collective-permute-start.11 = (bf16[4,1024,128]{2,1,0:T(8,128)(2,1)S(1)}, bf16[4,1024,128]{2,1,0:T(8,128)(2,1)S(1)}, u32[]{:S(2)}, u32[]{:S(2)}) collective-permute-start(bf16[4,1024,128]{2,1,0:T(8,128)(2,1)S(1)} %maximum_maximum_fusion.near_ref), channel_id=1, source_target_pairs={{0,4},{4,0},{8,12},{12,8},{16,20},{20,16},{24,28},{28,24},{1,5},{5... | collective-permute-start | bytes 3145736 | tf_op jit(solution)/shard_map/ppermute | solution.py:180
  57.8 0.6 concatenate.6.table_ref
  58.4 0.5 collective-permute-done.11.other_ref
  58.9 6.9 %shard_map.70 = f32[2,8,128,2048]{3,2,1,0:T(8,128)} custom-call(s32[6,128]{1,0:T(8,128)S(1)} %concatenate.6.table_ref, bf16[4,1024,128]{2,1,0:T(8,128)(2,1)S(1)} %maximum_maximum_fusion.near_ref, bf16[4,1024,128]{2,1,0:T(8,128)(2,1)S(1)} %collective-permute-done.11.other_ref, ...), custom_call_target="tpu_custom_call", output_to_operand_aliasing={{}: (3, {})} | custom-call | bytes 16777216 | tf_op jit(solution)/shard_map/pallas_call | solution.py:370
  (47 shorter events, 2.5 us)
Async XLA Ops:
  0.0 14.8 %copy-start = (bf16[8,16,4096]{2,1,0:T(8,128)(2,1)S(1)}, bf16[8,16,4096]{2,1,0:T(8,128)(2,1)}, u32[]{:S(2)}) copy-start(bf16[8,16,4096]{2,1,0:T(8,128)(2,1)} %values_ref.3) | copy-start | bytes 3145732
  0.0 14.8 %copy-start.1 = (f32[2,16,4096]{2,1,0:T(8,128)S(1)}, f32[2,16,4096]{2,1,0:T(8,128)}, u32[]{:S(2)}) copy-start(f32[2,16,4096]{2,1,0:T(8,128)} %places_ref.3) | copy-start | bytes 1572868
  0.0 14.8 %copy-start.2 = (s32[16,1]{0,1:T(1,128)S(1)}, s32[16,1]{0,1:T(1,128)}, u32[]{:S(2)}) copy-start(s32[16,1]{0,1:T(1,128)} %param.8) | copy-start | bytes 196
  0.0 14.8 %copy-start.3 = (s32[16]{0:T(128)S(1)}, s32[16]{0:T(128)}, u32[]{:S(2)}) copy-start(s32[16]{0:T(128)} %param.10) | copy-start | bytes 196
  0.0 14.8 %copy-start.4 = (s32[16]{0:T(128)S(1)}, s32[16]{0:T(128)}, u32[]{:S(2)}) copy-start(s32[16]{0:T(128)} %param.9) | copy-start | bytes 196
  0.0 14.8 %copy-start.5 = (s32[16]{0:T(128)S(1)}, s32[16]{0:T(128)}, u32[]{:S(2)}) copy-start(s32[16]{0:T(128)} %param.11) | copy-start | bytes 196
  14.5 8.7 %collective-permute-start = (bf16[2,5,128,128]{3,2,1,0:T(8,128)(2,1)S(1)}, bf16[2,5,128,128]{3,2,1,0:T(8,128)(2,1)S(1)}, u32[]{:S(2)}, u32[]{:S(2)}) collective-permute-start(bf16[2,5,128,128]{3,2,1,0:T(8,128)(2,1)S(1)} %get-tuple-element.18), channel_id=1, source_target_pairs={{0,1},{1,0},{2,3},{3,2},{4,5},{5,4},{6,7},{7,6},{8,9},{9,8},{10,11... | collective-permute-start | bytes 983048 | tf_op jit(solution)/shard_map/ppermute | solution.py:180
  21.9 6.3 %collective-permute-start.6 = (bf16[2,3,128,128]{3,2,1,0:T(8,128)(2,1)S(1)}, bf16[2,3,128,128]{3,2,1,0:T(8,128)(2,1)S(1)}, u32[]{:S(2)}, u32[]{:S(2)}) collective-permute-start(bf16[2,3,128,128]{3,2,1,0:T(8,128)(2,1)S(1)} %get-tuple-element.24), channel_id=1, source_target_pairs={{0,1},{1,0},{2,3},{3,2},{4,5},{5,4},{6,7},{7,6},{8,9},{9,8},{10,11... | collective-permute-start | bytes 589832 | tf_op jit(solution)/shard_map/ppermute | solution.py:180
  23.3 9.5 %collective-permute-start.1 = (bf16[1,5,128,128]{3,2,1,0:T(8,128)(2,1)S(1)}, bf16[1,5,128,128]{3,2,1,0:T(8,128)(2,1)S(1)}, u32[]{:S(2)}, u32[]{:S(2)}) collective-permute-start(bf16[1,5,128,128]{3,2,1,0:T(8,128)(2,1)S(1)} %get-tuple-element.22), channel_id=1, source_target_pairs={{0,2},{1,3},{2,0},{3,1},{4,6},{5,7},{6,4},{7,5},{8,10},{9,11},{10,... | collective-permute-start | bytes 491528 | tf_op jit(solution)/shard_map/ppermute | solution.py:180
  23.4 6.7 %collective-permute-start.2 = (bf16[16,16]{1,0:T(8,128)(2,1)S(1)}, bf16[16,16]{1,0:T(8,128)(2,1)S(1)}, u32[]{:S(2)}, u32[]{:S(2)}) collective-permute-start(bf16[16,16]{1,0:T(8,128)(2,1)S(1)} %get-tuple-element.23.numbers_ref), channel_id=1, source_target_pairs={{0,4},{4,0},{8,12},{12,8},{16,20},{20,16},{24,28},{28,24},{1,5},{5... | collective-permute-start | bytes 1544 | tf_op jit(solution)/shard_map/ppermute | solution.py:180
  28.2 7.8 %collective-permute-start.7 = (bf16[1,3,128,128]{3,2,1,0:T(8,128)(2,1)S(1)}, bf16[1,3,128,128]{3,2,1,0:T(8,128)(2,1)S(1)}, u32[]{:S(2)}, u32[]{:S(2)}) collective-permute-start(bf16[1,3,128,128]{3,2,1,0:T(8,128)(2,1)S(1)} %get-tuple-element.26), channel_id=1, source_target_pairs={{0,2},{1,3},{2,0},{3,1},{4,6},{5,7},{6,4},{7,5},{8,10},{9,11},{10,... | collective-permute-start | bytes 294920 | tf_op jit(solution)/shard_map/ppermute | solution.py:180
  33.3 5.2 %collective-permute-start.5 = (bf16[656,128]{1,0:T(8,128)(2,1)S(1)}, bf16[656,128]{1,0:T(8,128)(2,1)S(1)}, u32[]{:S(2)}, u32[]{:S(2)}) collective-permute-start(bf16[656,128]{1,0:T(8,128)(2,1)S(1)} %shard_map.67.rest_0_), channel_id=1, source_target_pairs={{0,24},{4,28},{8,16},{12,20},{16,8},{20,12},{24,0},{28,4},{1,25},{... | collective-permute-start | bytes 503816 | tf_op jit(solution)/shard_map/ppermute | solution.py:180
  35.6 4.7 %collective-permute-start.4 = (bf16[656,128]{1,0:T(8,128)(2,1)S(1)}, bf16[656,128]{1,0:T(8,128)(2,1)S(1)}, u32[]{:S(2)}, u32[]{:S(2)}) collective-permute-start(bf16[656,128]{1,0:T(8,128)(2,1)S(1)} %shard_map.67.rest_0_), channel_id=1, source_target_pairs={{0,16},{4,20},{8,24},{12,28},{16,0},{20,4},{24,8},{28,12},{1,17},{... | collective-permute-start | bytes 503816 | tf_op jit(solution)/shard_map/ppermute | solution.py:180
  35.8 4.6 %collective-permute-start.3 = (bf16[656,128]{1,0:T(8,128)(2,1)S(1)}, bf16[656,128]{1,0:T(8,128)(2,1)S(1)}, u32[]{:S(2)}, u32[]{:S(2)}) collective-permute-start(bf16[656,128]{1,0:T(8,128)(2,1)S(1)} %shard_map.67.rest_0_), channel_id=1, source_target_pairs={{0,8},{4,12},{8,0},{12,4},{16,24},{20,28},{24,16},{28,20},{1,9},{5... | collective-permute-start | bytes 503816 | tf_op jit(solution)/shard_map/ppermute | solution.py:180
  40.9 5.7 %collective-permute-start.10 = (bf16[384,128]{1,0:T(8,128)(2,1)S(1)}, bf16[384,128]{1,0:T(8,128)(2,1)S(1)}, u32[]{:S(2)}, u32[]{:S(2)}) collective-permute-start(bf16[384,128]{1,0:T(8,128)(2,1)S(1)} %get-tuple-element.28), channel_id=1, source_target_pairs={{0,24},{4,28},{8,16},{12,20},{16,8},{20,12},{24,0},{28,4},{1,25},{... | collective-permute-start | bytes 294920 | tf_op jit(solution)/shard_map/ppermute | solution.py:180
  42.2 5.6 %collective-permute-start.9 = (bf16[384,128]{1,0:T(8,128)(2,1)S(1)}, bf16[384,128]{1,0:T(8,128)(2,1)S(1)}, u32[]{:S(2)}, u32[]{:S(2)}) collective-permute-start(bf16[384,128]{1,0:T(8,128)(2,1)S(1)} %get-tuple-element.28), channel_id=1, source_target_pairs={{0,16},{4,20},{8,24},{12,28},{16,0},{20,4},{24,8},{28,12},{1,17},{... | collective-permute-start | bytes 294920 | tf_op jit(solution)/shard_map/ppermute | solution.py:180
  43.3 4.6 %collective-permute-start.8 = (bf16[384,128]{1,0:T(8,128)(2,1)S(1)}, bf16[384,128]{1,0:T(8,128)(2,1)S(1)}, u32[]{:S(2)}, u32[]{:S(2)}) collective-permute-start(bf16[384,128]{1,0:T(8,128)(2,1)S(1)} %get-tuple-element.28), channel_id=1, source_target_pairs={{0,8},{4,12},{8,0},{12,4},{16,24},{20,28},{24,16},{28,20},{1,9},{5... | collective-permute-start | bytes 294920 | tf_op jit(solution)/shard_map/ppermute | solution.py:180
  48.0 10.9 %collective-permute-start.11 = (bf16[4,1024,128]{2,1,0:T(8,128)(2,1)S(1)}, bf16[4,1024,128]{2,1,0:T(8,128)(2,1)S(1)}, u32[]{:S(2)}, u32[]{:S(2)}) collective-permute-start(bf16[4,1024,128]{2,1,0:T(8,128)(2,1)S(1)} %maximum_maximum_fusion.near_ref), channel_id=1, source_target_pairs={{0,4},{4,0},{8,12},{12,8},{16,20},{20,16},{24,28},{28,24},{1,5},{5... | collective-permute-start | bytes 3145736 | tf_op jit(solution)/shard_map/ppermute | solution.py:180

commit v5 on v3

--- a/solution.py
+++ b/solution.py
@@ -113,7 +113,8 @@
         pltpu.VMEM((STEP // 2, comp_count * SUB, LANES), jnp.bfloat16),
     ]
     if first:
-        in_specs = [ANY] * 2
+        values, places = (pltpu.with_memory_space_constraint(array, pltpu.HBM) for array in (values, places))
+        in_specs = [pl.BlockSpec(memory_space=pltpu.HBM)] * 2
         out_shape.append(jax.ShapeDtypeStruct((rows_each // SUB, W, TU, NV), jnp.float32))
         out_specs.append(ANY)
         scratch += [
@@ -139,7 +140,7 @@
         in_specs=[SMEM] + in_specs,
         out_specs=out_specs,
         scratch_shapes=scratch,
-        compiler_params=pltpu.CompilerParams(vmem_limit_bytes=(60 if first else 48) << 20),
+        compiler_params=pltpu.CompilerParams(vmem_limit_bytes=48 << 20),
         cost_estimate=pl.CostEstimate(
             flops=8 * (turns[1] - turns[0]) * STEP * row_count * SUB * SUB * comp_count,
             bytes_accessed=2 << 20,
@@ -217,7 +218,8 @@
                     preferred_element_type=jnp.float32,
                 ).astype(jnp.bfloat16)
     if hops:
-        near_ref = rest[hops + 1]
+        near_ref, go_ref = rest[hops + 1 :]
+        go_ref[...] = jnp.zeros(go_ref.shape, jnp.int32)
         for at in range(hops):
             near_ref[at] = rest[at][: near_ref.shape[1], :]
     else:
@@ -233,6 +235,7 @@
     out_shape = [jax.ShapeDtypeStruct((rows if hops else rows + META, lanes), jnp.bfloat16)]
     if hops:
         out_shape.append(jax.ShapeDtypeStruct((len(hops), rows, lanes), jnp.bfloat16))
+        out_shape.append(jax.ShapeDtypeStruct((SUBLANES, LANES), jnp.int32))
     return pl.pallas_call(
         functools.partial(sum_kernel, hops=len(hops), first_sub=first_sub),
         out_shape=out_shape,
@@ -393,19 +396,20 @@
         order=tile_grid,
         numbers=(owner.T, row_offset[None], w_plane[None], col_offset[None]),
     )
-    kept_a, sent_a = halve_all(*parts_a, "tm", parts_b[:1])
+    other_numbers = paired(own_numbers, "uv", 1)
+    kept_a, sent_a = halve_all(*parts_a, "tm", [other_numbers])
     parts_b = grid_parts(visibilities, positions, peers, 1, (split, half // STEP), order=sent_a, earlier=parts_b)
     kept_b, sent_b = halve_all(*parts_b, "tm", [])
     arrived_a, arrived_b = (paired(sent, "tm", peers // 2) for sent in (sent_a, sent_b))
-    (sum_a,) = sum_parts(kept_a, arrived_a, 0, own_numbers, [], [paired(own_numbers, "uv", 1)])
+    (sum_a,) = sum_parts(kept_a, arrived_a, 0, own_numbers, [], [other_numbers])
     hops_a = across(sum_a, "uv")
-    sum_b, near_a = sum_parts(kept_b, arrived_b, half, own_numbers, hops_a, [])
+    sum_b, near_a, go = sum_parts(kept_b, arrived_b, half, own_numbers, hops_a, [])
     near = jnp.concatenate([near_a, jnp.stack(across(sum_b, "uv"), axis=0)], axis=0)
     other = paired(near, "uv", 1)
 
     told = jnp.stack([hop[half * SUB :, : 2 * sub_count] for hop in hops_a], axis=1).astype(jnp.float32).astype(jnp.int32)
     chips = told.shape[1]
-    told = told.reshape(META, -1)
+    told = told.reshape(META, -1) + go[0, 0]
     entry = jnp.arange(told.shape[1], dtype=jnp.int32)
     chip, sub = entry // (2 * sub_count), entry % sub_count
     others = entry // sub_count % 2

time: 63.8 us -> 60.6 us (0.950); the launches traced: 64.6 us -> 60.7 us
  Pallas kernels: 29.3 us -> 26.9 us
  waiting for transfers between devices: 14.2 us -> 12.5 us
    ppermute x12, waiting for transfers between devices: 14.2 us -> 12.5 us  [paired(): lax.ppermute(array, axis, [(i, i ^ mask) for i in range(lax.axis_size(axi...]
    pallas_call x1, Pallas kernels: 6.78 us -> 5.22 us  [place_all(): pl.pallas_call(place_kernel, out_shape=jax.ShapeDtypeStruct(tile_grid.sha...]
    pallas_call x3, Pallas kernels: 21.4 us -> 20.6 us  [grid_parts(): pl.pallas_call(functools.partial(grid_kernel, peers=peers, first=first, t...]
    reduce_sum x1, other arithmetic: 1.42 us -> 0.72 us  [touch_plan(): number = jnp.sum(taken.astype(jnp.int32))]
    add x2, other arithmetic: 0.04 us -> 0.72 us  [the longest x1 0.7 us: body(): told = told.reshape(META, -1) + go[0, 0]]
    slice x0 -> x2, local copies, waits for them, and re-layouts: none -> 0.67 us  [the longest x1 0.59 us: body(): told = told.reshape(META, -1) + go[0, 0]]
  transfers between devices with their start and end apart: 12 -> 12, of which waited for: 8 -> 8; matrix products, arithmetic and copies ran while one was open for 8% -> 9% of each run, Pallas kernels for 16% -> 17%
where the time goes in v5:
time: 60.6 us; the launch traced here: 60.7 us
  Pallas kernels  26.9 us (44%)
  starting transfers between devices  15.2 us (25%)
  waiting for transfers between devices  12.5 us (21%)
  local copies, waits for them, and re-layouts  2.87 us (5%)
  other arithmetic  2.83 us (5%)
    pallas_call x3, Pallas kernels, grid_parts(): pl.pallas_call(functools.partial(grid_kernel, peers=peers, first=first, t...  20.6 us
    ppermute x12, starting transfers between devices, paired(): lax.ppermute(array, axis, [(i, i ^ mask) for i in range(lax.axis_size(axi...  15.2 us
    ppermute x12, waiting for transfers between devices, paired(): lax.ppermute(array, axis, [(i, i ^ mask) for i in range(lax.axis_size(axi...  12.5 us
    pallas_call x1, Pallas kernels, place_all(): pl.pallas_call(place_kernel, out_shape=jax.ShapeDtypeStruct(tile_grid.sha...  5.22 us
  transfers between devices with their start and end apart: 12, of which 8 were waited for; matrix products, arithmetic and copies ran while one was open for 9% of the time, Pallas kernels for 17%

profile of v5, /device:TPU:0, one launch (start us, length us, event | category | flops | bytes accessed | tf_op | source)
XLA Modules:
  0.0 60.7 jit_solution(1765775161347042083)
XLA Ops:
  0.0 11.1 %shard_map.64 = (bf16[2,4,128,128]{3,2,1,0:T(8,128)(2,1)S(1)}, bf16[2,4,128,128]{3,2,1,0:T(8,128)(2,1)S(1)}, f32[2,8,128,2048]{3,2,1,0:T(8,128)}) custom-call(s32[1]{0:T(128)} %bitcast.me_ref, bf16[8,16,4096]{2,1,0:T(8,128)(2,1)} %values_ref.5, f32[2,16,4096]{2,1,0:T(8,128)} %places_ref.5), custom_call_target="tpu_custom_call" | custom-call | flops 8589934592 | bytes 2097152 | tf_op jit(solution)/shard_map/pallas_call | solution.py:136
  11.1 3.1 %collective-permute-start = (bf16[2,4,128,128]{3,2,1,0:T(8,128)(2,1)S(1)}, bf16[2,4,128,128]{3,2,1,0:T(8,128)(2,1)S(1)}, u32[]{:S(2)}, u32[]{:S(2)}) collective-permute-start(bf16[2,4,128,128]{3,2,1,0:T(8,128)(2,1)S(1)} %get-tuple-element.21), channel_id=1, source_target_pairs={{0,1},{1,0},{2,3},{3,2},{4,5},{5,4},{6,7},{7,6},{8,9},{9,8},{10,11... | collective-permute-start | bytes 786440 | tf_op jit(solution)/shard_map/ppermute | solution.py:175
  14.2 4.8 %shard_map.65 = (bf16[2,2,128,128]{3,2,1,0:T(8,128)(2,1)S(1)}, bf16[2,2,128,128]{3,2,1,0:T(8,128)(2,1)S(1)}, bf16[16,16]{1,0:T(8,128)(2,1)S(1)}) custom-call(s32[1]{0:T(128)} %bitcast.me_ref, bf16[8,16,4096]{2,1,0:T(8,128)(2,1)S(1)} %copy-done, f32[2,16,4096]{2,1,0:T(8,128)S(1)} %copy-done.1, f32[2,8,128,2048]{3,2,1,0:T(8,128)} %get-tuple-element.22.rest_0_._, ...), custom_call_target="tpu_custom_call" | custom-call | flops 4294967296 | bytes 2097152 | tf_op jit(solution)/shard_map/pallas_call | solution.py:136
  19.1 1.2 %collective-permute-done.1.rest_0_ = bf16[16,16]{1,0:T(8,128)(2,1)S(1)} collective-permute-done((bf16[16,16]{1,0:T(8,128)(2,1)S(1)}, bf16[16,16]{1,0:T(8,128)(2,1)S(1)}, u32[]{:S(2)}, u32[]{:S(2)}) %collective-permute-start.1) | collective-permute-done | bytes 544 | tf_op jit(solution)/shard_map/ppermute | solution.py:175
  20.6 2.8 %collective-permute-start.2 = (bf16[1,4,128,128]{3,2,1,0:T(8,128)(2,1)S(1)}, bf16[1,4,128,128]{3,2,1,0:T(8,128)(2,1)S(1)}, u32[]{:S(2)}, u32[]{:S(2)}) collective-permute-start(bf16[1,4,128,128]{3,2,1,0:T(8,128)(2,1)S(1)} %get-tuple-element.25.rest_0_), channel_id=1, source_target_pairs={{0,2},{1,3},{2,0},{3,1},{4,6},{5,7},{6,4},{7,5},{8,10},{9,11},{10,... | collective-permute-start | bytes 393224 | tf_op jit(solution)/shard_map/ppermute | solution.py:175
  23.4 4.8 %shard_map.68 = (bf16[2,4,128,128]{3,2,1,0:T(8,128)(2,1)S(1)}, bf16[2,4,128,128]{3,2,1,0:T(8,128)(2,1)S(1)}) custom-call(s32[1]{0:T(128)} %bitcast.me_ref, bf16[8,16,4096]{2,1,0:T(8,128)(2,1)S(1)} %copy-done, f32[2,16,4096]{2,1,0:T(8,128)S(1)} %copy-done.1, bf16[1,4,128,128]{3,2,1,0:T(8,128)(2,1)S(1)} %get-tuple-element.25.rest_0_, ...), custom_call_target="tpu_custom_call" | custom-call | flops 4294967296 | bytes 2097152 | tf_op jit(solution)/shard_map/pallas_call | solution.py:136
  28.2 1.6 %collective-permute-start.6 = (bf16[2,4,128,128]{3,2,1,0:T(8,128)(2,1)S(1)}, bf16[2,4,128,128]{3,2,1,0:T(8,128)(2,1)S(1)}, u32[]{:S(2)}, u32[]{:S(2)}) collective-permute-start(bf16[2,4,128,128]{3,2,1,0:T(8,128)(2,1)S(1)} %get-tuple-element.29), channel_id=1, source_target_pairs={{0,1},{1,0},{2,3},{3,2},{4,5},{5,4},{6,7},{7,6},{8,9},{9,8},{10,11... | collective-permute-start | bytes 786440 | tf_op jit(solution)/shard_map/ppermute | solution.py:175
  30.3 2.5 %collective-permute-start.5 = (bf16[528,128]{1,0:T(8,128)(2,1)S(1)}, bf16[528,128]{1,0:T(8,128)(2,1)S(1)}, u32[]{:S(2)}, u32[]{:S(2)}) collective-permute-start(bf16[528,128]{1,0:T(8,128)(2,1)S(1)} %shard_map.67.rest_0_), channel_id=1, source_target_pairs={{0,24},{4,28},{8,16},{12,20},{16,8},{20,12},{24,0},{28,4},{1,25},{... | collective-permute-start | bytes 405512 | tf_op jit(solution)/shard_map/ppermute | solution.py:175
  32.8 0.5 collective-permute-start.4
  33.3 0.5 collective-permute-start.3
  33.9 2.1 %collective-permute-done.6.arrived_ref = bf16[2,4,128,128]{3,2,1,0:T(8,128)(2,1)S(1)} collective-permute-done((bf16[2,4,128,128]{3,2,1,0:T(8,128)(2,1)S(1)}, bf16[2,4,128,128]{3,2,1,0:T(8,128)(2,1)S(1)}, u32[]{:S(2)}, u32[]{:S(2)}) %collective-permute-start.6) | collective-permute-done | bytes 262176 | tf_op jit(solution)/shard_map/ppermute | solution.py:175
  36.8 2.4 %collective-permute-done.4.rest_2_ = bf16[528,128]{1,0:T(8,128)(2,1)S(1)} collective-permute-done((bf16[528,128]{1,0:T(8,128)(2,1)S(1)}, bf16[528,128]{1,0:T(8,128)(2,1)S(1)}, u32[]{:S(2)}, u32[]{:S(2)}) %collective-permute-start.4) | collective-permute-done | bytes 135200 | tf_op jit(solution)/shard_map/ppermute | solution.py:175
  39.3 4.4 %collective-permute-done.7.arrived_ref = bf16[1,4,128,128]{3,2,1,0:T(8,128)(2,1)S(1)} collective-permute-done((bf16[1,4,128,128]{3,2,1,0:T(8,128)(2,1)S(1)}, bf16[1,4,128,128]{3,2,1,0:T(8,128)(2,1)S(1)}, u32[]{:S(2)}, u32[]{:S(2)}) %collective-permute-start.7) | collective-permute-done | bytes 131104 | tf_op jit(solution)/shard_map/ppermute | solution.py:175
  44.2 2.5 %collective-permute-start.10 = (bf16[512,128]{1,0:T(8,128)(2,1)S(1)}, bf16[512,128]{1,0:T(8,128)(2,1)S(1)}, u32[]{:S(2)}, u32[]{:S(2)}) collective-permute-start(bf16[512,128]{1,0:T(8,128)(2,1)S(1)} %get-tuple-element.34), channel_id=1, source_target_pairs={{0,24},{4,28},{8,16},{12,20},{16,8},{20,12},{24,0},{28,4},{1,25},{... | collective-permute-start | bytes 393224 | tf_op jit(solution)/shard_map/ppermute | solution.py:175
  46.7 0.5 collective-permute-start.9
  47.2 0.5 collective-permute-start.8
  47.7 0.6 slice.44
  48.3 0.7 %convert_add_fusion = s32[16,4,32]{2,0,1:T(8,128)S(1)} fusion(bf16[16,1,32]{2,0,1:T(8,128)(2,1)S(1)} %slice_bitcast_fusion, bf16[16,1,32]{2,0,1:T(8,128)(2,1)S(1)} %slice_bitcast_fusion.1, bf16[16,1,32]{2,0,1:T(8,128)(2,1)S(1)} %slice_bitcast_fusion.2, bf16[16,1,32]{2,0,1:T(8,128)(2,1)S(1)} %slice_bitcast_fusion.3, s32[]{:T(128)} %bitcast.9), kind=kLoop, calls=%fused_computation.18 | loop fusion | flops 12288 | bytes 12292 | tf_op jit(solution)/shard_map/add | solution.py:412
  49.0 0.6 broadcast.812
  49.6 0.7 %fusion.23 = (s32[4,32]{1,0:T(4,128)S(1)}, s32[1,4,32]{2,0,1:T(1,128)S(1)}, s32[1,4,32]{2,0,1:T(1,128)S(1)}, s32[1,4,32]{2,0,1:T(1,128)S(1)}, s32[1,4,32]{2,0,1:...) fusion(s32[]{:T(128)} %broadcast.812, ...), kind=kLoop, calls=%fused_computation.93 | loop fusion | flops 640 | bytes 7688 | tf_op jit(solution)/shard_map/add | solution.py:419
  51.1 1.3 %collective-permute-done.8 = bf16[512,128]{1,0:T(8,128)(2,1)S(1)} collective-permute-done((bf16[512,128]{1,0:T(8,128)(2,1)S(1)}, bf16[512,128]{1,0:T(8,128)(2,1)S(1)}, u32[]{:S(2)}, u32[]{:S(2)}) %collective-permute-start.8) | collective-permute-done | bytes 131104 | tf_op jit(solution)/shard_map/ppermute | solution.py:175
  52.6 0.7 %convert_reduce_fusion = (s32[]{:T(128)}, pred[128]{0:T(512)(128)(4,1)S(1)}) fusion(s32[128]{0:T(128)S(1)} %add.276, s32[128]{0:T(128)S(1)} %sub.64, s32[128]{0:T(128)S(1)} %sub.63), kind=kLoop, calls=%fused_computation.84 | loop fusion | flops 2303 | bytes 1668 | tf_op jit(solution)/shard_map/reduce_sum | solution.py:274
  54.2 0.7 %concatenate.6.table_ref = s32[6,128]{1,0:T(8,128)S(1)} pad(s32[5,128]{1,0:T(8,128)S(1)} %select_reduce_fusion, s32[]{:T(128)} %get-tuple-element.44), padding=0_1x0_0 | pad | bytes 5636 | tf_op jit(solution)/shard_map/concatenate | solution.py:275
  55.3 5.2 %shard_map.71 = f32[2,8,128,2048]{3,2,1,0:T(8,128)} custom-call(s32[6,128]{1,0:T(8,128)S(1)} %concatenate.6.table_ref, bf16[8,512,128]{2,1,0:T(8,128)(2,1)S(1)} %bitcast_dynamic-update-slice_fusion.near_ref, bf16[8,512,128]{2,1,0:T(8,128)(2,1)S(1)} %collective-permute-done.11.other_ref, ...), custom_call_target="tpu_custom_call", output_to_operand_aliasing={{}: (3, {})} | custom-call | bytes 16777216 | tf_op jit(solution)/shard_map/pallas_call | solution.py:365
  (54 shorter events, 4.4 us)
Async XLA Ops:
  0.0 14.2 %copy-start.1 = (f32[2,16,4096]{2,1,0:T(8,128)S(1)}, f32[2,16,4096]{2,1,0:T(8,128)}, u32[]{:S(2)}) copy-start(f32[2,16,4096]{2,1,0:T(8,128)} %places_ref.5) | copy-start | bytes 1572868
  0.0 14.2 %copy-start = (bf16[8,16,4096]{2,1,0:T(8,128)(2,1)S(1)}, bf16[8,16,4096]{2,1,0:T(8,128)(2,1)}, u32[]{:S(2)}) copy-start(bf16[8,16,4096]{2,1,0:T(8,128)(2,1)} %values_ref.5) | copy-start | bytes 3145732
  0.0 14.2 %copy-start.5 = (s32[16]{0:T(128)S(1)}, s32[16]{0:T(128)}, u32[]{:S(2)}) copy-start(s32[16]{0:T(128)} %param.11) | copy-start | bytes 196
  0.0 14.2 %copy-start.3 = (s32[16]{0:T(128)S(1)}, s32[16]{0:T(128)}, u32[]{:S(2)}) copy-start(s32[16]{0:T(128)} %param.10) | copy-start | bytes 196
  0.0 14.2 %copy-start.4 = (s32[16]{0:T(128)S(1)}, s32[16]{0:T(128)}, u32[]{:S(2)}) copy-start(s32[16]{0:T(128)} %param.9) | copy-start | bytes 196
  0.0 14.2 %copy-start.2 = (s32[16,1]{0,1:T(1,128)S(1)}, s32[16,1]{0,1:T(1,128)}, u32[]{:S(2)}) copy-start(s32[16,1]{0,1:T(1,128)} %param.8) | copy-start | bytes 196
  11.1 9.4 %collective-permute-start = (bf16[2,4,128,128]{3,2,1,0:T(8,128)(2,1)S(1)}, bf16[2,4,128,128]{3,2,1,0:T(8,128)(2,1)S(1)}, u32[]{:S(2)}, u32[]{:S(2)}) collective-permute-start(bf16[2,4,128,128]{3,2,1,0:T(8,128)(2,1)S(1)} %get-tuple-element.21), channel_id=1, source_target_pairs={{0,1},{1,0},{2,3},{3,2},{4,5},{5,4},{6,7},{7,6},{8,9},{9,8},{10,11... | collective-permute-start | bytes 786440 | tf_op jit(solution)/shard_map/ppermute | solution.py:175
  19.0 1.2 %collective-permute-start.1 = (bf16[16,16]{1,0:T(8,128)(2,1)S(1)}, bf16[16,16]{1,0:T(8,128)(2,1)S(1)}, u32[]{:S(2)}, u32[]{:S(2)}) collective-permute-start(bf16[16,16]{1,0:T(8,128)(2,1)S(1)} %get-tuple-element.23.numbers_ref), channel_id=1, source_target_pairs={{0,4},{4,0},{8,12},{12,8},{16,20},{20,16},{24,28},{28,24},{1,5},{5... | collective-permute-start | bytes 1544 | tf_op jit(solution)/shard_map/ppermute | solution.py:175
  20.6 9.3 %collective-permute-start.2 = (bf16[1,4,128,128]{3,2,1,0:T(8,128)(2,1)S(1)}, bf16[1,4,128,128]{3,2,1,0:T(8,128)(2,1)S(1)}, u32[]{:S(2)}, u32[]{:S(2)}) collective-permute-start(bf16[1,4,128,128]{3,2,1,0:T(8,128)(2,1)S(1)} %get-tuple-element.25.rest_0_), channel_id=1, source_target_pairs={{0,2},{1,3},{2,0},{3,1},{4,6},{5,7},{6,4},{7,5},{8,10},{9,11},{10,... | collective-permute-start | bytes 393224 | tf_op jit(solution)/shard_map/ppermute | solution.py:175
  28.2 7.7 %collective-permute-start.6 = (bf16[2,4,128,128]{3,2,1,0:T(8,128)(2,1)S(1)}, bf16[2,4,128,128]{3,2,1,0:T(8,128)(2,1)S(1)}, u32[]{:S(2)}, u32[]{:S(2)}) collective-permute-start(bf16[2,4,128,128]{3,2,1,0:T(8,128)(2,1)S(1)} %get-tuple-element.29), channel_id=1, source_target_pairs={{0,1},{1,0},{2,3},{3,2},{4,5},{5,4},{6,7},{7,6},{8,9},{9,8},{10,11... | collective-permute-start | bytes 786440 | tf_op jit(solution)/shard_map/ppermute | solution.py:175
  30.3 6.5 %collective-permute-start.5 = (bf16[528,128]{1,0:T(8,128)(2,1)S(1)}, bf16[528,128]{1,0:T(8,128)(2,1)S(1)}, u32[]{:S(2)}, u32[]{:S(2)}) collective-permute-start(bf16[528,128]{1,0:T(8,128)(2,1)S(1)} %shard_map.67.rest_0_), channel_id=1, source_target_pairs={{0,24},{4,28},{8,16},{12,20},{16,8},{20,12},{24,0},{28,4},{1,25},{... | collective-permute-start | bytes 405512 | tf_op jit(solution)/shard_map/ppermute | solution.py:175
  32.8 6.5 %collective-permute-start.4 = (bf16[528,128]{1,0:T(8,128)(2,1)S(1)}, bf16[528,128]{1,0:T(8,128)(2,1)S(1)}, u32[]{:S(2)}, u32[]{:S(2)}) collective-permute-start(bf16[528,128]{1,0:T(8,128)(2,1)S(1)} %shard_map.67.rest_0_), channel_id=1, source_target_pairs={{0,16},{4,20},{8,24},{12,28},{16,0},{20,4},{24,8},{28,12},{1,17},{... | collective-permute-start | bytes 405512 | tf_op jit(solution)/shard_map/ppermute | solution.py:175
  33.3 6.0 %collective-permute-start.3 = (bf16[528,128]{1,0:T(8,128)(2,1)S(1)}, bf16[528,128]{1,0:T(8,128)(2,1)S(1)}, u32[]{:S(2)}, u32[]{:S(2)}) collective-permute-start(bf16[528,128]{1,0:T(8,128)(2,1)S(1)} %shard_map.67.rest_0_), channel_id=1, source_target_pairs={{0,8},{4,12},{8,0},{12,4},{16,24},{20,28},{24,16},{28,20},{1,9},{5... | collective-permute-start | bytes 405512 | tf_op jit(solution)/shard_map/ppermute | solution.py:175
  36.0 7.7 %collective-permute-start.7 = (bf16[1,4,128,128]{3,2,1,0:T(8,128)(2,1)S(1)}, bf16[1,4,128,128]{3,2,1,0:T(8,128)(2,1)S(1)}, u32[]{:S(2)}, u32[]{:S(2)}) collective-permute-start(bf16[1,4,128,128]{3,2,1,0:T(8,128)(2,1)S(1)} %get-tuple-element.31), channel_id=1, source_target_pairs={{0,2},{1,3},{2,0},{3,1},{4,6},{5,7},{6,4},{7,5},{8,10},{9,11},{10,... | collective-permute-start | bytes 393224 | tf_op jit(solution)/shard_map/ppermute | solution.py:175
  44.2 8.3 %collective-permute-start.10 = (bf16[512,128]{1,0:T(8,128)(2,1)S(1)}, bf16[512,128]{1,0:T(8,128)(2,1)S(1)}, u32[]{:S(2)}, u32[]{:S(2)}) collective-permute-start(bf16[512,128]{1,0:T(8,128)(2,1)S(1)} %get-tuple-element.34), channel_id=1, source_target_pairs={{0,24},{4,28},{8,16},{12,20},{16,8},{20,12},{24,0},{28,4},{1,25},{... | collective-permute-start | bytes 393224 | tf_op jit(solution)/shard_map/ppermute | solution.py:175
  46.7 5.8 %collective-permute-start.9 = (bf16[512,128]{1,0:T(8,128)(2,1)S(1)}, bf16[512,128]{1,0:T(8,128)(2,1)S(1)}, u32[]{:S(2)}, u32[]{:S(2)}) collective-permute-start(bf16[512,128]{1,0:T(8,128)(2,1)S(1)} %get-tuple-element.34), channel_id=1, source_target_pairs={{0,16},{4,20},{8,24},{12,28},{16,0},{20,4},{24,8},{28,12},{1,17},{... | collective-permute-start | bytes 393224 | tf_op jit(solution)/shard_map/ppermute | solution.py:175
  47.2 5.3 %collective-permute-start.8 = (bf16[512,128]{1,0:T(8,128)(2,1)S(1)}, bf16[512,128]{1,0:T(8,128)(2,1)S(1)}, u32[]{:S(2)}, u32[]{:S(2)}) collective-permute-start(bf16[512,128]{1,0:T(8,128)(2,1)S(1)} %get-tuple-element.34), channel_id=1, source_target_pairs={{0,8},{4,12},{8,0},{12,4},{16,24},{20,28},{24,16},{28,20},{1,9},{5... | collective-permute-start | bytes 393224 | tf_op jit(solution)/shard_map/ppermute | solution.py:175
  52.6 2.7 %collective-permute-start.11 = (bf16[8,512,128]{2,1,0:T(8,128)(2,1)S(1)}, bf16[8,512,128]{2,1,0:T(8,128)(2,1)S(1)}, u32[]{:S(2)}, u32[]{:S(2)}) collective-permute-start(bf16[8,512,128]{2,1,0:T(8,128)(2,1)S(1)} %bitcast_dynamic-update-slice_fusion.near_ref), channel_id=1, source_target_pairs={{0,4},{4,0},{8,12},{12,8},{16,20},{20,16},{24,28},{28,24},{1,5},{5... | collective-permute-start | bytes 3145736 | tf_op jit(solution)/shard_map/ppermute | solution.py:175

commit v6 on v5

--- a/solution.py
+++ b/solution.py
@@ -1,4 +1,5 @@
 import functools
+import math
 
 import jax
 import jax.numpy as jnp
@@ -16,6 +17,7 @@
 SUBLANES = 8
 BLOCKS = NV // LANES
 META = 16
+MIXED = 256
 STEP = 4
 
 VMEM = pl.BlockSpec(memory_space=pltpu.VMEM)
@@ -65,21 +67,29 @@
     rows_each = comp_count // peers * SUB
     for comp in range(comp_count):
         values_wide[comp * sub_count : (comp + 1) * sub_count, :] = values_ref[comp].astype(jnp.float32)
-    cells = lax.broadcasted_iota(jnp.int32, (SUB, row_count), 0).astype(jnp.float32) * (2.0 / TAPS)
+    span = math.gcd(row_count, MIXED)
+    cells = lax.broadcasted_iota(jnp.int32, (SUB, span), 0).astype(jnp.float32) * (2.0 / TAPS)
 
     def one_sub(sub):
-        row_taps = taper(cells - places_ref[0, pl.ds(sub, 1), :] * (2.0 / TAPS)).astype(jnp.bfloat16)
-        col_taps = taper(cells - places_ref[1, pl.ds(sub, 1), :] * (2.0 / TAPS))
-        weighted = jnp.concatenate(
-            [
-                (values_wide[pl.ds(comp * sub_count + sub, 1), :] * col_taps).astype(jnp.bfloat16)
-                for comp in range(comp_count)
-            ],
-            axis=0,
-        )
-        return lax.dot_general(
-            weighted, row_taps, (((1,), (1,)), ((), ())), preferred_element_type=jnp.float32
-        )
+        straight = jnp.zeros((comp_count * SUB, SUB), jnp.float32)
+        crossed = jnp.zeros((SUB, comp_count * SUB), jnp.float32)
+        for at in range(0, row_count, span):
+            some = slice(at, at + span)
+            row_taps = taper(cells - places_ref[0, pl.ds(sub, 1), some] * (2.0 / TAPS)).astype(jnp.bfloat16)
+            col_taps = taper(cells - places_ref[1, pl.ds(sub, 1), some] * (2.0 / TAPS))
+            weighted = jnp.concatenate(
+                [
+                    (values_wide[pl.ds(comp * sub_count + sub, 1), some] * col_taps).astype(jnp.bfloat16)
+                    for comp in range(comp_count)
+                ],
+                axis=0,
+            )
+            last = (((1,), (1,)), ((), ()))
+            if at // span % 2:
+                crossed += lax.dot_general(row_taps, weighted, last, preferred_element_type=jnp.float32)
+            else:
+                straight += lax.dot_general(weighted, row_taps, last, preferred_element_type=jnp.float32)
+        return straight + jnp.transpose(crossed)
 
     def some_subs(turn, carry):
         for pair in range(STEP // 2):
@@ -278,8 +288,8 @@
 def place_kernel(table_ref, near_ref, other_ref, _, out_ref, canvas, sem):
     comp_count = canvas.shape[1]
     number = table_ref[5, 0]
-    row = lax.broadcasted_iota(jnp.int32, (SUB + SUBLANES, LANES), 0)
-    lane = lax.broadcasted_iota(jnp.int32, (SUB + SUBLANES, LANES), 1)
+    row = lax.broadcasted_iota(jnp.int32, (1, SUBLANES, LANES), 1)
+    lane = lax.broadcasted_iota(jnp.int32, (1, SUBLANES, LANES), 2)
 
     def lanes_of(block):
         return pl.ds(pl.multiple_of(block * LANES, LANES), LANES)
@@ -306,11 +316,15 @@
         patch = jnp.where((table_ref[4, index] & 16) != 0, other_ref[block, at, :], near_ref[block, at, :])
         patch = patch.astype(jnp.float32)
         patches = []
+        skip = table_ref[0, index] & (SUBLANES - 1)
         for comp in range(comp_count):
             values = patch[:, comp // 2 * LANES : (comp // 2 + 1) * LANES]
             if comp % 2:
                 values = pltpu.roll(values, SUB, 1)
-            patches.append(jnp.concatenate([values, values[:SUBLANES]], axis=0))
+            values = values.reshape(SUB // SUBLANES, SUBLANES, LANES)
+            head = jnp.where(row >= skip, values[:1], 0.0)
+            tail = jnp.where(row < skip, values[:1], 0.0)
+            patches.append(jnp.concatenate([head, values[1:], tail], axis=0))
         return patches
 
     def add_patch(index, patches):
@@ -320,31 +334,32 @@
         flags = table_ref[4, index]
         block = col >> 7
         shift = col & (LANES - 1)
-        skip = start & (SUBLANES - 1)
-        rows = pl.ds(pl.multiple_of(start - skip, SUBLANES), SUB + SUBLANES)
-        inside = (row >= skip) & (row < skip + SUB)
+        rows = pl.ds(pl.multiple_of(start & ~(SUBLANES - 1), SUBLANES), SUB + SUBLANES)
+
+        def add(at, here):
+            for comp in range(comp_count):
+                values = jnp.where(here, patches[comp], 0.0).reshape(SUB + SUBLANES, LANES)
+                canvas[plane, comp, rows, lanes_of(at)] += values
+
         when_set(flags, 1, lambda: clear(plane, block))
-        here = inside & (lane >= shift) & (lane < shift + SUB)
-        for comp in range(comp_count):
-            canvas[plane, comp, rows, lanes_of(block)] += jnp.where(here, patches[comp], 0.0)
+        add(block, (lane >= shift) & (lane < shift + SUB))
         when_set(flags, 2, lambda: out_copy(plane, block).start())
 
         @pl.when(shift > LANES - SUB)
         def _():
             when_set(flags, 4, lambda: clear(plane, block + 1))
-            there = inside & (lane < shift + SUB - LANES)
-            for comp in range(comp_count):
-                canvas[plane, comp, rows, lanes_of(block + 1)] += jnp.where(there, patches[comp], 0.0)
+            add(block + 1, lane < shift + SUB - LANES)
             when_set(flags, 8, lambda: out_copy(plane, block + 1).start())
 
     def add_two(turn_index, carry):
-        index = turn_index * 2
-        first, second = patch_of(index), patch_of(index + 1)
-        add_patch(index, first)
-
-        @pl.when(index + 1 < number)
-        def _():
-            add_patch(index + 1, second)
+        index = turn_index * 4
+        several = [patch_of(index + more) for more in range(4)]
+        add_patch(index, several[0])
+        for more in range(1, 4):
+
+            @pl.when(index + more < number)
+            def _(more=more):
+                add_patch(index + more, several[more])
 
         return carry
 
@@ -356,7 +371,7 @@
         when_set(flags, 8, lambda: out_copy(plane, block + 1).wait())
         return carry
 
-    lax.fori_loop(0, (number + 1) // 2, add_two, 0)
+    lax.fori_loop(0, (number + 3) // 4, add_two, 0)
     lax.fori_loop(0, number, finish, 0)
 
 

time: 60.6 us -> 59.7 us (0.985); the launches traced: 60.7 us -> 59.2 us
  Pallas kernels: 26.9 us -> 25.2 us
    pallas_call x1, Pallas kernels: 5.22 us -> 3.71 us  [place_all(): pl.pallas_call(place_kernel, out_shape=jax.ShapeDtypeStruct(tile_grid.sha...]
  transfers between devices with their start and end apart: 12 -> 12, of which waited for: 8 -> 9; matrix products, arithmetic and copies ran while one was open for 9% -> 10% of each run, Pallas kernels for 17% -> 17%
where the time goes in v6:
time: 59.7 us; the launch traced here: 59.2 us
  Pallas kernels  25.2 us (42%)
  starting transfers between devices  15.2 us (25%)
  waiting for transfers between devices  12.7 us (21%)
  local copies, waits for them, and re-layouts  2.87 us (5%)
  other arithmetic  2.83 us (5%)
    pallas_call x3, Pallas kernels, grid_parts(): pl.pallas_call(functools.partial(grid_kernel, peers=peers, first=first, t...  20.4 us
    ppermute x12, starting transfers between devices, paired(): lax.ppermute(array, axis, [(i, i ^ mask) for i in range(lax.axis_size(axi...  15.2 us
    ppermute x12, waiting for transfers between devices, paired(): lax.ppermute(array, axis, [(i, i ^ mask) for i in range(lax.axis_size(axi...  12.7 us
    pallas_call x1, Pallas kernels, place_all(): pl.pallas_call(place_kernel, out_shape=jax.ShapeDtypeStruct(tile_grid.sha...  3.71 us
  transfers between devices with their start and end apart: 12, of which 9 were waited for; matrix products, arithmetic and copies ran while one was open for 10% of the time, Pallas kernels for 17%

profile of v6, /device:TPU:0, one launch (start us, length us, event | category | flops | bytes accessed | tf_op | source)
XLA Modules:
  0.0 59.2 jit_solution(325587187926987699)
XLA Ops:
  0.0 10.7 %shard_map.64 = (bf16[2,4,128,128]{3,2,1,0:T(8,128)(2,1)S(1)}, bf16[2,4,128,128]{3,2,1,0:T(8,128)(2,1)S(1)}, f32[2,8,128,2048]{3,2,1,0:T(8,128)}) custom-call(s32[1]{0:T(128)} %bitcast.me_ref, bf16[8,16,4096]{2,1,0:T(8,128)(2,1)} %values_ref.5, f32[2,16,4096]{2,1,0:T(8,128)} %places_ref.5), custom_call_target="tpu_custom_call" | custom-call | flops 8589934592 | bytes 2097152 | tf_op jit(solution)/shard_map/pallas_call | solution.py:146
  10.8 3.1 %collective-permute-start = (bf16[2,4,128,128]{3,2,1,0:T(8,128)(2,1)S(1)}, bf16[2,4,128,128]{3,2,1,0:T(8,128)(2,1)S(1)}, u32[]{:S(2)}, u32[]{:S(2)}) collective-permute-start(bf16[2,4,128,128]{3,2,1,0:T(8,128)(2,1)S(1)} %get-tuple-element.21), channel_id=1, source_target_pairs={{0,1},{1,0},{2,3},{3,2},{4,5},{5,4},{6,7},{7,6},{8,9},{9,8},{10,11... | collective-permute-start | bytes 786440 | tf_op jit(solution)/shard_map/ppermute | solution.py:185
  13.9 4.9 %shard_map.65 = (bf16[2,2,128,128]{3,2,1,0:T(8,128)(2,1)S(1)}, bf16[2,2,128,128]{3,2,1,0:T(8,128)(2,1)S(1)}, bf16[16,16]{1,0:T(8,128)(2,1)S(1)}) custom-call(s32[1]{0:T(128)} %bitcast.me_ref, bf16[8,16,4096]{2,1,0:T(8,128)(2,1)S(1)} %copy-done, f32[2,16,4096]{2,1,0:T(8,128)S(1)} %copy-done.1, f32[2,8,128,2048]{3,2,1,0:T(8,128)} %get-tuple-element.22.rest_0_._, ...), custom_call_target="tpu_custom_call" | custom-call | flops 4294967296 | bytes 2097152 | tf_op jit(solution)/shard_map/pallas_call | solution.py:146
  18.8 1.2 %collective-permute-done.1.rest_0_ = bf16[16,16]{1,0:T(8,128)(2,1)S(1)} collective-permute-done((bf16[16,16]{1,0:T(8,128)(2,1)S(1)}, bf16[16,16]{1,0:T(8,128)(2,1)S(1)}, u32[]{:S(2)}, u32[]{:S(2)}) %collective-permute-start.1) | collective-permute-done | bytes 544 | tf_op jit(solution)/shard_map/ppermute | solution.py:185
  20.2 2.8 %collective-permute-start.2 = (bf16[1,4,128,128]{3,2,1,0:T(8,128)(2,1)S(1)}, bf16[1,4,128,128]{3,2,1,0:T(8,128)(2,1)S(1)}, u32[]{:S(2)}, u32[]{:S(2)}) collective-permute-start(bf16[1,4,128,128]{3,2,1,0:T(8,128)(2,1)S(1)} %get-tuple-element.25.rest_0_), channel_id=1, source_target_pairs={{0,2},{1,3},{2,0},{3,1},{4,6},{5,7},{6,4},{7,5},{8,10},{9,11},{10,... | collective-permute-start | bytes 393224 | tf_op jit(solution)/shard_map/ppermute | solution.py:185
  23.0 4.8 %shard_map.68 = (bf16[2,4,128,128]{3,2,1,0:T(8,128)(2,1)S(1)}, bf16[2,4,128,128]{3,2,1,0:T(8,128)(2,1)S(1)}) custom-call(s32[1]{0:T(128)} %bitcast.me_ref, bf16[8,16,4096]{2,1,0:T(8,128)(2,1)S(1)} %copy-done, f32[2,16,4096]{2,1,0:T(8,128)S(1)} %copy-done.1, bf16[1,4,128,128]{3,2,1,0:T(8,128)(2,1)S(1)} %get-tuple-element.25.rest_0_, ...), custom_call_target="tpu_custom_call" | custom-call | flops 4294967296 | bytes 2097152 | tf_op jit(solution)/shard_map/pallas_call | solution.py:146
  27.9 1.7 %collective-permute-start.6 = (bf16[2,4,128,128]{3,2,1,0:T(8,128)(2,1)S(1)}, bf16[2,4,128,128]{3,2,1,0:T(8,128)(2,1)S(1)}, u32[]{:S(2)}, u32[]{:S(2)}) collective-permute-start(bf16[2,4,128,128]{3,2,1,0:T(8,128)(2,1)S(1)} %get-tuple-element.29), channel_id=1, source_target_pairs={{0,1},{1,0},{2,3},{3,2},{4,5},{5,4},{6,7},{7,6},{8,9},{9,8},{10,11... | collective-permute-start | bytes 786440 | tf_op jit(solution)/shard_map/ppermute | solution.py:185
  30.0 2.5 %collective-permute-start.5 = (bf16[528,128]{1,0:T(8,128)(2,1)S(1)}, bf16[528,128]{1,0:T(8,128)(2,1)S(1)}, u32[]{:S(2)}, u32[]{:S(2)}) collective-permute-start(bf16[528,128]{1,0:T(8,128)(2,1)S(1)} %shard_map.67.rest_0_), channel_id=1, source_target_pairs={{0,24},{4,28},{8,16},{12,20},{16,8},{20,12},{24,0},{28,4},{1,25},{... | collective-permute-start | bytes 405512 | tf_op jit(solution)/shard_map/ppermute | solution.py:185
  32.5 0.5 collective-permute-start.4
  33.0 0.5 collective-permute-start.3
  33.6 2.1 %collective-permute-done.6.arrived_ref = bf16[2,4,128,128]{3,2,1,0:T(8,128)(2,1)S(1)} collective-permute-done((bf16[2,4,128,128]{3,2,1,0:T(8,128)(2,1)S(1)}, bf16[2,4,128,128]{3,2,1,0:T(8,128)(2,1)S(1)}, u32[]{:S(2)}, u32[]{:S(2)}) %collective-permute-start.6) | collective-permute-done | bytes 262176 | tf_op jit(solution)/shard_map/ppermute | solution.py:185
  36.6 2.5 %collective-permute-done.4.rest_2_ = bf16[528,128]{1,0:T(8,128)(2,1)S(1)} collective-permute-done((bf16[528,128]{1,0:T(8,128)(2,1)S(1)}, bf16[528,128]{1,0:T(8,128)(2,1)S(1)}, u32[]{:S(2)}, u32[]{:S(2)}) %collective-permute-start.4) | collective-permute-done | bytes 135200 | tf_op jit(solution)/shard_map/ppermute | solution.py:185
  39.1 4.5 %collective-permute-done.7.arrived_ref = bf16[1,4,128,128]{3,2,1,0:T(8,128)(2,1)S(1)} collective-permute-done((bf16[1,4,128,128]{3,2,1,0:T(8,128)(2,1)S(1)}, bf16[1,4,128,128]{3,2,1,0:T(8,128)(2,1)S(1)}, u32[]{:S(2)}, u32[]{:S(2)}) %collective-permute-start.7) | collective-permute-done | bytes 131104 | tf_op jit(solution)/shard_map/ppermute | solution.py:185
  44.1 2.5 %collective-permute-start.10 = (bf16[512,128]{1,0:T(8,128)(2,1)S(1)}, bf16[512,128]{1,0:T(8,128)(2,1)S(1)}, u32[]{:S(2)}, u32[]{:S(2)}) collective-permute-start(bf16[512,128]{1,0:T(8,128)(2,1)S(1)} %get-tuple-element.34), channel_id=1, source_target_pairs={{0,24},{4,28},{8,16},{12,20},{16,8},{20,12},{24,0},{28,4},{1,25},{... | collective-permute-start | bytes 393224 | tf_op jit(solution)/shard_map/ppermute | solution.py:185
  46.6 0.5 collective-permute-start.9
  47.1 0.5 collective-permute-start.8
  47.6 0.6 slice.44
  48.2 0.7 %convert_add_fusion = s32[16,4,32]{2,0,1:T(8,128)S(1)} fusion(bf16[16,1,32]{2,0,1:T(8,128)(2,1)S(1)} %slice_bitcast_fusion, bf16[16,1,32]{2,0,1:T(8,128)(2,1)S(1)} %slice_bitcast_fusion.1, bf16[16,1,32]{2,0,1:T(8,128)(2,1)S(1)} %slice_bitcast_fusion.2, bf16[16,1,32]{2,0,1:T(8,128)(2,1)S(1)} %slice_bitcast_fusion.3, s32[]{:T(128)} %bitcast.9), kind=kLoop, calls=%fused_computation.18 | loop fusion | flops 12288 | bytes 12292 | tf_op jit(solution)/shard_map/add | solution.py:427
  48.9 0.6 %broadcast.812 = s32[]{:T(128)} broadcast(s32[]{:T(128)} %constant.117.clone.1), dimensions={} | broadcast | bytes 8 | tf_op jit(solution)/shard_map/sub | solution.py:432
  49.5 0.7 %fusion.23 = (s32[4,32]{1,0:T(4,128)S(1)}, s32[1,4,32]{2,0,1:T(1,128)S(1)}, s32[1,4,32]{2,0,1:T(1,128)S(1)}, s32[1,4,32]{2,0,1:T(1,128)S(1)}, s32[1,4,32]{2,0,1:...) fusion(s32[]{:T(128)} %broadcast.812, ...), kind=kLoop, calls=%fused_computation.93 | loop fusion | flops 640 | bytes 7688 | tf_op jit(solution)/shard_map/add | solution.py:434
  51.0 1.4 %collective-permute-done.8 = bf16[512,128]{1,0:T(8,128)(2,1)S(1)} collective-permute-done((bf16[512,128]{1,0:T(8,128)(2,1)S(1)}, bf16[512,128]{1,0:T(8,128)(2,1)S(1)}, u32[]{:S(2)}, u32[]{:S(2)}) %collective-permute-start.8) | collective-permute-done | bytes 131104 | tf_op jit(solution)/shard_map/ppermute | solution.py:185
  52.6 0.7 %convert_reduce_fusion = (s32[]{:T(128)}, pred[128]{0:T(512)(128)(4,1)S(1)}) fusion(s32[128]{0:T(128)S(1)} %add.276, s32[128]{0:T(128)S(1)} %sub.64, s32[128]{0:T(128)S(1)} %sub.63), kind=kLoop, calls=%fused_computation.84 | loop fusion | flops 2303 | bytes 1668 | tf_op jit(solution)/shard_map/reduce_sum | solution.py:284
  54.2 0.7 %concatenate.6.table_ref = s32[6,128]{1,0:T(8,128)S(1)} pad(s32[5,128]{1,0:T(8,128)S(1)} %select_reduce_fusion, s32[]{:T(128)} %get-tuple-element.44), padding=0_1x0_0 | pad | bytes 5636 | tf_op jit(solution)/shard_map/concatenate | solution.py:285
  55.3 3.7 %shard_map.71 = f32[2,8,128,2048]{3,2,1,0:T(8,128)} custom-call(s32[6,128]{1,0:T(8,128)S(1)} %concatenate.6.table_ref, bf16[8,512,128]{2,1,0:T(8,128)(2,1)S(1)} %bitcast_dynamic-update-slice_fusion.near_ref, bf16[8,512,128]{2,1,0:T(8,128)(2,1)S(1)} %collective-permute-done.11.other_ref, ...), custom_call_target="tpu_custom_call", output_to_operand_aliasing={{}: (3, {})} | custom-call | bytes 16777216 | tf_op jit(solution)/shard_map/pallas_call | solution.py:380
  (54 shorter events, 4.3 us)
Async XLA Ops:
  0.0 13.8 %copy-start.1 = (f32[2,16,4096]{2,1,0:T(8,128)S(1)}, f32[2,16,4096]{2,1,0:T(8,128)}, u32[]{:S(2)}) copy-start(f32[2,16,4096]{2,1,0:T(8,128)} %places_ref.5) | copy-start | bytes 1572868
  0.0 13.8 %copy-start = (bf16[8,16,4096]{2,1,0:T(8,128)(2,1)S(1)}, bf16[8,16,4096]{2,1,0:T(8,128)(2,1)}, u32[]{:S(2)}) copy-start(bf16[8,16,4096]{2,1,0:T(8,128)(2,1)} %values_ref.5) | copy-start | bytes 3145732
  0.0 13.9 %copy-start.5 = (s32[16]{0:T(128)S(1)}, s32[16]{0:T(128)}, u32[]{:S(2)}) copy-start(s32[16]{0:T(128)} %param.11) | copy-start | bytes 196
  0.0 13.9 %copy-start.3 = (s32[16]{0:T(128)S(1)}, s32[16]{0:T(128)}, u32[]{:S(2)}) copy-start(s32[16]{0:T(128)} %param.10) | copy-start | bytes 196
  0.0 13.9 %copy-start.4 = (s32[16]{0:T(128)S(1)}, s32[16]{0:T(128)}, u32[]{:S(2)}) copy-start(s32[16]{0:T(128)} %param.9) | copy-start | bytes 196
  0.0 13.9 %copy-start.2 = (s32[16,1]{0,1:T(1,128)S(1)}, s32[16,1]{0,1:T(1,128)}, u32[]{:S(2)}) copy-start(s32[16,1]{0,1:T(1,128)} %param.8) | copy-start | bytes 196
  10.8 9.4 %collective-permute-start = (bf16[2,4,128,128]{3,2,1,0:T(8,128)(2,1)S(1)}, bf16[2,4,128,128]{3,2,1,0:T(8,128)(2,1)S(1)}, u32[]{:S(2)}, u32[]{:S(2)}) collective-permute-start(bf16[2,4,128,128]{3,2,1,0:T(8,128)(2,1)S(1)} %get-tuple-element.21), channel_id=1, source_target_pairs={{0,1},{1,0},{2,3},{3,2},{4,5},{5,4},{6,7},{7,6},{8,9},{9,8},{10,11... | collective-permute-start | bytes 786440 | tf_op jit(solution)/shard_map/ppermute | solution.py:185
  18.7 1.2 %collective-permute-start.1 = (bf16[16,16]{1,0:T(8,128)(2,1)S(1)}, bf16[16,16]{1,0:T(8,128)(2,1)S(1)}, u32[]{:S(2)}, u32[]{:S(2)}) collective-permute-start(bf16[16,16]{1,0:T(8,128)(2,1)S(1)} %get-tuple-element.23.numbers_ref), channel_id=1, source_target_pairs={{0,4},{4,0},{8,12},{12,8},{16,20},{20,16},{24,28},{28,24},{1,5},{5... | collective-permute-start | bytes 1544 | tf_op jit(solution)/shard_map/ppermute | solution.py:185
  20.2 9.3 %collective-permute-start.2 = (bf16[1,4,128,128]{3,2,1,0:T(8,128)(2,1)S(1)}, bf16[1,4,128,128]{3,2,1,0:T(8,128)(2,1)S(1)}, u32[]{:S(2)}, u32[]{:S(2)}) collective-permute-start(bf16[1,4,128,128]{3,2,1,0:T(8,128)(2,1)S(1)} %get-tuple-element.25.rest_0_), channel_id=1, source_target_pairs={{0,2},{1,3},{2,0},{3,1},{4,6},{5,7},{6,4},{7,5},{8,10},{9,11},{10,... | collective-permute-start | bytes 393224 | tf_op jit(solution)/shard_map/ppermute | solution.py:185
  27.9 7.8 %collective-permute-start.6 = (bf16[2,4,128,128]{3,2,1,0:T(8,128)(2,1)S(1)}, bf16[2,4,128,128]{3,2,1,0:T(8,128)(2,1)S(1)}, u32[]{:S(2)}, u32[]{:S(2)}) collective-permute-start(bf16[2,4,128,128]{3,2,1,0:T(8,128)(2,1)S(1)} %get-tuple-element.29), channel_id=1, source_target_pairs={{0,1},{1,0},{2,3},{3,2},{4,5},{5,4},{6,7},{7,6},{8,9},{9,8},{10,11... | collective-permute-start | bytes 786440 | tf_op jit(solution)/shard_map/ppermute | solution.py:185
  30.0 6.6 %collective-permute-start.5 = (bf16[528,128]{1,0:T(8,128)(2,1)S(1)}, bf16[528,128]{1,0:T(8,128)(2,1)S(1)}, u32[]{:S(2)}, u32[]{:S(2)}) collective-permute-start(bf16[528,128]{1,0:T(8,128)(2,1)S(1)} %shard_map.67.rest_0_), channel_id=1, source_target_pairs={{0,24},{4,28},{8,16},{12,20},{16,8},{20,12},{24,0},{28,4},{1,25},{... | collective-permute-start | bytes 405512 | tf_op jit(solution)/shard_map/ppermute | solution.py:185
  32.5 6.5 %collective-permute-start.4 = (bf16[528,128]{1,0:T(8,128)(2,1)S(1)}, bf16[528,128]{1,0:T(8,128)(2,1)S(1)}, u32[]{:S(2)}, u32[]{:S(2)}) collective-permute-start(bf16[528,128]{1,0:T(8,128)(2,1)S(1)} %shard_map.67.rest_0_), channel_id=1, source_target_pairs={{0,16},{4,20},{8,24},{12,28},{16,0},{20,4},{24,8},{28,12},{1,17},{... | collective-permute-start | bytes 405512 | tf_op jit(solution)/shard_map/ppermute | solution.py:185
  33.0 6.1 %collective-permute-start.3 = (bf16[528,128]{1,0:T(8,128)(2,1)S(1)}, bf16[528,128]{1,0:T(8,128)(2,1)S(1)}, u32[]{:S(2)}, u32[]{:S(2)}) collective-permute-start(bf16[528,128]{1,0:T(8,128)(2,1)S(1)} %shard_map.67.rest_0_), channel_id=1, source_target_pairs={{0,8},{4,12},{8,0},{12,4},{16,24},{20,28},{24,16},{28,20},{1,9},{5... | collective-permute-start | bytes 405512 | tf_op jit(solution)/shard_map/ppermute | solution.py:185
  35.8 7.8 %collective-permute-start.7 = (bf16[1,4,128,128]{3,2,1,0:T(8,128)(2,1)S(1)}, bf16[1,4,128,128]{3,2,1,0:T(8,128)(2,1)S(1)}, u32[]{:S(2)}, u32[]{:S(2)}) collective-permute-start(bf16[1,4,128,128]{3,2,1,0:T(8,128)(2,1)S(1)} %get-tuple-element.31), channel_id=1, source_target_pairs={{0,2},{1,3},{2,0},{3,1},{4,6},{5,7},{6,4},{7,5},{8,10},{9,11},{10,... | collective-permute-start | bytes 393224 | tf_op jit(solution)/shard_map/ppermute | solution.py:185
  44.1 8.4 %collective-permute-start.10 = (bf16[512,128]{1,0:T(8,128)(2,1)S(1)}, bf16[512,128]{1,0:T(8,128)(2,1)S(1)}, u32[]{:S(2)}, u32[]{:S(2)}) collective-permute-start(bf16[512,128]{1,0:T(8,128)(2,1)S(1)} %get-tuple-element.34), channel_id=1, source_target_pairs={{0,24},{4,28},{8,16},{12,20},{16,8},{20,12},{24,0},{28,4},{1,25},{... | collective-permute-start | bytes 393224 | tf_op jit(solution)/shard_map/ppermute | solution.py:185
  46.6 5.9 %collective-permute-start.9 = (bf16[512,128]{1,0:T(8,128)(2,1)S(1)}, bf16[512,128]{1,0:T(8,128)(2,1)S(1)}, u32[]{:S(2)}, u32[]{:S(2)}) collective-permute-start(bf16[512,128]{1,0:T(8,128)(2,1)S(1)} %get-tuple-element.34), channel_id=1, source_target_pairs={{0,16},{4,20},{8,24},{12,28},{16,0},{20,4},{24,8},{28,12},{1,17},{... | collective-permute-start | bytes 393224 | tf_op jit(solution)/shard_map/ppermute | solution.py:185
  47.1 5.4 %collective-permute-start.8 = (bf16[512,128]{1,0:T(8,128)(2,1)S(1)}, bf16[512,128]{1,0:T(8,128)(2,1)S(1)}, u32[]{:S(2)}, u32[]{:S(2)}) collective-permute-start(bf16[512,128]{1,0:T(8,128)(2,1)S(1)} %get-tuple-element.34), channel_id=1, source_target_pairs={{0,8},{4,12},{8,0},{12,4},{16,24},{20,28},{24,16},{28,20},{1,9},{5... | collective-permute-start | bytes 393224 | tf_op jit(solution)/shard_map/ppermute | solution.py:185
  52.6 2.7 %collective-permute-start.11 = (bf16[8,512,128]{2,1,0:T(8,128)(2,1)S(1)}, bf16[8,512,128]{2,1,0:T(8,128)(2,1)S(1)}, u32[]{:S(2)}, u32[]{:S(2)}) collective-permute-start(bf16[8,512,128]{2,1,0:T(8,128)(2,1)S(1)} %bitcast_dynamic-update-slice_fusion.near_ref), channel_id=1, source_target_pairs={{0,4},{4,0},{8,12},{12,8},{16,20},{20,16},{24,28},{28,24},{1,5},{5... | collective-permute-start | bytes 3145736 | tf_op jit(solution)/shard_map/ppermute | solution.py:185

commit v7 on v6

--- a/solution.py
+++ b/solution.py
@@ -38,7 +38,13 @@
 
 def grid_kernel(me_ref, values_ref, places_ref, *rest, peers, first, turns, earlier):
     if first:
-        kept_ref, sent_ref, out_ref, values_wide, sums, blank, sem, values, places, in_sem = rest
+        places_from, (kept_ref, sent_ref, out_ref, numbers_ref), rest = rest[:4], rest[4:8], rest[8:]
+        values_wide, sums, blank, sem, values, places, in_sem, numbers, numbers_sem = rest
+        number_copies = [
+            pltpu.make_async_copy(source, numbers.at[at], numbers_sem.at[at]) for at, source in enumerate(places_from)
+        ]
+        for copy in number_copies:
+            copy.start()
         _, sub_count, row_count = values.shape
         in_copies = [
             pltpu.make_async_copy(values_ref.at[:, pl.ds(0, sub_count), :], values, in_sem.at[0]),
@@ -48,10 +54,11 @@
             copy.start()
         blank[...] = jnp.zeros(blank.shape, jnp.float32)
         zero_copies = [pltpu.make_async_copy(blank, out_ref.at[:, plane], sem.at[plane]) for plane in range(W)]
-        for copy in in_copies:
+        for copy in in_copies + number_copies:
             copy.wait()
         for copy in zero_copies:
             copy.start()
+        numbers_ref[...] = number_rows(*(numbers[at] for at in range(4)))
         values_ref, places_ref = values, places
     else:
         rest = rest[1:]
@@ -61,8 +68,7 @@
             kept_ref[:, :done] = earlier_kept[...]
             sent_ref[:, :done] = earlier_sent[...]
         else:
-            owner_ref, row_ref, plane_ref, col_ref, kept_ref, sent_ref, numbers_ref, values_wide, sums = rest
-            numbers_ref[...] = number_rows(owner_ref[...], row_ref[...], plane_ref[...], col_ref[...])
+            kept_ref, sent_ref, values_wide, sums = rest
     comp_count, sub_count, row_count = values_ref.shape
     rows_each = comp_count // peers * SUB
     for comp in range(comp_count):
@@ -125,24 +131,25 @@
     if first:
         values, places = (pltpu.with_memory_space_constraint(array, pltpu.HBM) for array in (values, places))
         in_specs = [pl.BlockSpec(memory_space=pltpu.HBM)] * 2
+        in_specs += [pl.BlockSpec(memory_space=pltpu.HBM)] * len(numbers)
         out_shape.append(jax.ShapeDtypeStruct((rows_each // SUB, W, TU, NV), jnp.float32))
-        out_specs.append(ANY)
+        out_shape.append(jax.ShapeDtypeStruct((META, all_subs), jnp.bfloat16))
+        out_specs += [ANY, pl.BlockSpec((META, all_subs), lambda i: (0, 0))]
         scratch += [
             pltpu.VMEM((rows_each // SUB, TU, NV), jnp.float32),
             pltpu.SemaphoreType.DMA((W,)),
             pltpu.VMEM(values_block, values.dtype),
             pltpu.VMEM(places_block, places.dtype),
             pltpu.SemaphoreType.DMA((2,)),
+            pltpu.VMEM((len(numbers), 1, all_subs), jnp.int32),
+            pltpu.SemaphoreType.DMA((len(numbers),)),
         ]
-        more = []
+        more = [pltpu.with_memory_space_constraint(array, pltpu.HBM) for array in numbers]
     else:
         in_specs = [pl.BlockSpec(block, lambda i: (0, chunk, 0)) for block in (values_block, places_block)]
-        in_specs += [ANY] + [pl.BlockSpec((1, all_subs), lambda i: (0, 0))] * len(numbers)
+        in_specs.append(ANY)
         in_specs += [pl.BlockSpec(array.shape, lambda i: (0, 0, 0, 0)) for array in earlier]
-        more = [order, *numbers, *earlier]
-        if numbers:
-            out_shape.append(jax.ShapeDtypeStruct((META, all_subs), jnp.bfloat16))
-            out_specs.append(pl.BlockSpec((META, all_subs), lambda i: (0, 0)))
+        more = [order, *earlier]
     return pl.pallas_call(
         functools.partial(grid_kernel, peers=peers, first=first, turns=turns, earlier=bool(earlier)),
         grid=(1,),
@@ -401,18 +408,17 @@
     half = sub_count // 2
 
     split = half // STEP // 2
-    *parts_a, tile_grid = grid_parts(visibilities, positions, peers, 0, (0, half // STEP))
-    *parts_b, own_numbers = grid_parts(
+    *parts_a, tile_grid, own_numbers = grid_parts(
         visibilities,
         positions,
         peers,
-        1,
-        (0, split),
-        order=tile_grid,
+        0,
+        (0, half // STEP),
         numbers=(owner.T, row_offset[None], w_plane[None], col_offset[None]),
     )
     other_numbers = paired(own_numbers, "uv", 1)
-    kept_a, sent_a = halve_all(*parts_a, "tm", [other_numbers])
+    parts_b = grid_parts(visibilities, positions, peers, 1, (0, split), order=tile_grid)
+    kept_a, sent_a = halve_all(*parts_a, "tm", [parts_b[0], other_numbers])
     parts_b = grid_parts(visibilities, positions, peers, 1, (split, half // STEP), order=sent_a, earlier=parts_b)
     kept_b, sent_b = halve_all(*parts_b, "tm", [])
     arrived_a, arrived_b = (paired(sent, "tm", peers // 2) for sent in (sent_a, sent_b))

time: 59.7 us -> 61.4 us (1.028); the launches traced: 59.2 us -> 61.7 us
  Pallas kernels: 25.2 us -> 27.6 us
    pallas_call x1, Pallas kernels: 3.71 us -> 5.86 us  [place_all(): pl.pallas_call(place_kernel, out_shape=jax.ShapeDtypeStruct(tile_grid.sha...]
  transfers between devices with their start and end apart: 12 -> 12, of which waited for: 9 -> 8; matrix products, arithmetic and copies ran while one was open for 10% -> 9% of each run, Pallas kernels for 17% -> 17%
where the time goes in v7:
time: 61.4 us; the launch traced here: 61.7 us
  Pallas kernels  27.6 us (45%)
  starting transfers between devices  15.7 us (26%)
  waiting for transfers between devices  12.3 us (20%)
  local copies, waits for them, and re-layouts  2.86 us (5%)
  other arithmetic  2.83 us (5%)
    pallas_call x3, Pallas kernels, grid_parts(): pl.pallas_call(functools.partial(grid_kernel, peers=peers, first=first, t...  20.6 us
    ppermute x12, starting transfers between devices, paired(): lax.ppermute(array, axis, [(i, i ^ mask) for i in range(lax.axis_size(axi...  15.7 us
    ppermute x12, waiting for transfers between devices, paired(): lax.ppermute(array, axis, [(i, i ^ mask) for i in range(lax.axis_size(axi...  12.3 us
    pallas_call x1, Pallas kernels, place_all(): pl.pallas_call(place_kernel, out_shape=jax.ShapeDtypeStruct(tile_grid.sha...  5.86 us
  transfers between devices with their start and end apart: 12, of which 8 were waited for; matrix products, arithmetic and copies ran while one was open for 9% of the time, Pallas kernels for 17%

profile of v7, /device:TPU:0, one launch (start us, length us, event | category | flops | bytes accessed | tf_op | source)
XLA Modules:
  0.0 61.7 jit_solution(15755326296701630862)
XLA Ops:
  0.0 10.9 %shard_map.64 = (bf16[2,4,128,128]{3,2,1,0:T(8,128)(2,1)S(1)}, bf16[2,4,128,128]{3,2,1,0:T(8,128)(2,1)S(1)}, f32[2,8,128,2048]{3,2,1,0:T(8,128)}, bf16[16,16]{1,0:T(8,128)(2,1)S(1)}) custom-call(s32[1]{0:T(128)} %bitcast.me_ref, bf16[8,16,4096]{2,1,0:T(8,128)(2,1)} %values_ref.5, f32[2,16,4096]{2,1,0:T(8,128)} %places_ref.5, s32[1,16]{1,0:T(1,128)} %bitcast.50, ...), custom_call_target="tpu_custom_call" | custom-call | flops 8589934592 | bytes 2097152 | tf_op jit(solution)/shard_map/pallas_call | solution.py:153
  10.9 0.5 collective-permute-start.1
  11.5 2.7 %collective-permute-start = (bf16[2,4,128,128]{3,2,1,0:T(8,128)(2,1)S(1)}, bf16[2,4,128,128]{3,2,1,0:T(8,128)(2,1)S(1)}, u32[]{:S(2)}, u32[]{:S(2)}) collective-permute-start(bf16[2,4,128,128]{3,2,1,0:T(8,128)(2,1)S(1)} %get-tuple-element.21), channel_id=1, source_target_pairs={{0,1},{1,0},{2,3},{3,2},{4,5},{5,4},{6,7},{7,6},{8,9},{9,8},{10,11... | collective-permute-start | bytes 786440 | tf_op jit(solution)/shard_map/ppermute | solution.py:192
  14.1 4.9 %shard_map.65 = (bf16[2,2,128,128]{3,2,1,0:T(8,128)(2,1)S(1)}, bf16[2,2,128,128]{3,2,1,0:T(8,128)(2,1)S(1)}) custom-call(s32[1]{0:T(128)} %bitcast.me_ref, bf16[8,16,4096]{2,1,0:T(8,128)(2,1)S(1)} %copy-done, f32[2,16,4096]{2,1,0:T(8,128)S(1)} %copy-done.1, f32[2,8,128,2048]{3,2,1,0:T(8,128)} %get-tuple-element.22.rest_0_._), custom_call_target="tpu_custom_call" | custom-call | flops 4294967296 | bytes 2097152 | tf_op jit(solution)/shard_map/pallas_call | solution.py:153
  19.0 2.0 %collective-permute-done.arrived_ref = bf16[2,4,128,128]{3,2,1,0:T(8,128)(2,1)S(1)} collective-permute-done((bf16[2,4,128,128]{3,2,1,0:T(8,128)(2,1)S(1)}, bf16[2,4,128,128]{3,2,1,0:T(8,128)(2,1)S(1)}, u32[]{:S(2)}, u32[]{:S(2)}) %collective-permute-start) | collective-permute-done | bytes 262176 | tf_op jit(solution)/shard_map/ppermute | solution.py:192
  21.1 2.8 %collective-permute-start.2 = (bf16[1,4,128,128]{3,2,1,0:T(8,128)(2,1)S(1)}, bf16[1,4,128,128]{3,2,1,0:T(8,128)(2,1)S(1)}, u32[]{:S(2)}, u32[]{:S(2)}) collective-permute-start(bf16[1,4,128,128]{3,2,1,0:T(8,128)(2,1)S(1)} %get-tuple-element.26.rest_0_), channel_id=1, source_target_pairs={{0,2},{1,3},{2,0},{3,1},{4,6},{5,7},{6,4},{7,5},{8,10},{9,11},{10,... | collective-permute-start | bytes 393224 | tf_op jit(solution)/shard_map/ppermute | solution.py:192
  23.9 4.9 %shard_map.68 = (bf16[2,4,128,128]{3,2,1,0:T(8,128)(2,1)S(1)}, bf16[2,4,128,128]{3,2,1,0:T(8,128)(2,1)S(1)}) custom-call(s32[1]{0:T(128)} %bitcast.me_ref, bf16[8,16,4096]{2,1,0:T(8,128)(2,1)S(1)} %copy-done, f32[2,16,4096]{2,1,0:T(8,128)S(1)} %copy-done.1, bf16[1,4,128,128]{3,2,1,0:T(8,128)(2,1)S(1)} %get-tuple-element.26.rest_0_, ...), custom_call_target="tpu_custom_call" | custom-call | flops 4294967296 | bytes 2097152 | tf_op jit(solution)/shard_map/pallas_call | solution.py:153
  28.8 1.6 %collective-permute-start.6 = (bf16[2,4,128,128]{3,2,1,0:T(8,128)(2,1)S(1)}, bf16[2,4,128,128]{3,2,1,0:T(8,128)(2,1)S(1)}, u32[]{:S(2)}, u32[]{:S(2)}) collective-permute-start(bf16[2,4,128,128]{3,2,1,0:T(8,128)(2,1)S(1)} %get-tuple-element.29), channel_id=1, source_target_pairs={{0,1},{1,0},{2,3},{3,2},{4,5},{5,4},{6,7},{7,6},{8,9},{9,8},{10,11... | collective-permute-start | bytes 786440 | tf_op jit(solution)/shard_map/ppermute | solution.py:192
  30.9 2.5 %collective-permute-start.5 = (bf16[528,128]{1,0:T(8,128)(2,1)S(1)}, bf16[528,128]{1,0:T(8,128)(2,1)S(1)}, u32[]{:S(2)}, u32[]{:S(2)}) collective-permute-start(bf16[528,128]{1,0:T(8,128)(2,1)S(1)} %shard_map.67.rest_0_), channel_id=1, source_target_pairs={{0,24},{4,28},{8,16},{12,20},{16,8},{20,12},{24,0},{28,4},{1,25},{... | collective-permute-start | bytes 405512 | tf_op jit(solution)/shard_map/ppermute | solution.py:192
  33.9 0.5 collective-permute-start.3
  34.5 2.0 %collective-permute-done.6.arrived_ref = bf16[2,4,128,128]{3,2,1,0:T(8,128)(2,1)S(1)} collective-permute-done((bf16[2,4,128,128]{3,2,1,0:T(8,128)(2,1)S(1)}, bf16[2,4,128,128]{3,2,1,0:T(8,128)(2,1)S(1)}, u32[]{:S(2)}, u32[]{:S(2)}) %collective-permute-start.6) | collective-permute-done | bytes 262176 | tf_op jit(solution)/shard_map/ppermute | solution.py:192
  36.5 0.9 %collective-permute-start.7 = (bf16[1,4,128,128]{3,2,1,0:T(8,128)(2,1)S(1)}, bf16[1,4,128,128]{3,2,1,0:T(8,128)(2,1)S(1)}, u32[]{:S(2)}, u32[]{:S(2)}) collective-permute-start(bf16[1,4,128,128]{3,2,1,0:T(8,128)(2,1)S(1)} %get-tuple-element.31), channel_id=1, source_target_pairs={{0,2},{1,3},{2,0},{3,1},{4,6},{5,7},{6,4},{7,5},{8,10},{9,11},{10,... | collective-permute-start | bytes 393224 | tf_op jit(solution)/shard_map/ppermute | solution.py:192
  37.8 1.6 %collective-permute-done.4.rest_2_ = bf16[528,128]{1,0:T(8,128)(2,1)S(1)} collective-permute-done((bf16[528,128]{1,0:T(8,128)(2,1)S(1)}, bf16[528,128]{1,0:T(8,128)(2,1)S(1)}, u32[]{:S(2)}, u32[]{:S(2)}) %collective-permute-start.4) | collective-permute-done | bytes 135200 | tf_op jit(solution)/shard_map/ppermute | solution.py:192
  39.4 4.9 %collective-permute-done.7.arrived_ref = bf16[1,4,128,128]{3,2,1,0:T(8,128)(2,1)S(1)} collective-permute-done((bf16[1,4,128,128]{3,2,1,0:T(8,128)(2,1)S(1)}, bf16[1,4,128,128]{3,2,1,0:T(8,128)(2,1)S(1)}, u32[]{:S(2)}, u32[]{:S(2)}) %collective-permute-start.7) | collective-permute-done | bytes 131104 | tf_op jit(solution)/shard_map/ppermute | solution.py:192
  44.8 2.5 %collective-permute-start.10 = (bf16[512,128]{1,0:T(8,128)(2,1)S(1)}, bf16[512,128]{1,0:T(8,128)(2,1)S(1)}, u32[]{:S(2)}, u32[]{:S(2)}) collective-permute-start(bf16[512,128]{1,0:T(8,128)(2,1)S(1)} %get-tuple-element.34), channel_id=1, source_target_pairs={{0,24},{4,28},{8,16},{12,20},{16,8},{20,12},{24,0},{28,4},{1,25},{... | collective-permute-start | bytes 393224 | tf_op jit(solution)/shard_map/ppermute | solution.py:192
  47.3 0.5 collective-permute-start.9
  48.4 0.6 slice.44
  49.0 0.7 %convert_add_fusion = s32[16,4,32]{2,0,1:T(8,128)S(1)} fusion(bf16[16,1,32]{2,0,1:T(8,128)(2,1)S(1)} %slice_bitcast_fusion, bf16[16,1,32]{2,0,1:T(8,128)(2,1)S(1)} %slice_bitcast_fusion.1, bf16[16,1,32]{2,0,1:T(8,128)(2,1)S(1)} %slice_bitcast_fusion.2, bf16[16,1,32]{2,0,1:T(8,128)(2,1)S(1)} %slice_bitcast_fusion.3, s32[]{:T(128)} %bitcast.9), kind=kLoop, calls=%fused_computation.18 | loop fusion | flops 12288 | bytes 12292 | tf_op jit(solution)/shard_map/add | solution.py:433
  49.7 0.6 broadcast.812
  50.3 0.7 %fusion.23 = (s32[4,32]{1,0:T(4,128)S(1)}, s32[1,4,32]{2,0,1:T(1,128)S(1)}, s32[1,4,32]{2,0,1:T(1,128)S(1)}, s32[1,4,32]{2,0,1:T(1,128)S(1)}, s32[1,4,32]{2,0,1:...) fusion(s32[]{:T(128)} %broadcast.812, ...), kind=kLoop, calls=%fused_computation.93 | loop fusion | flops 640 | bytes 7688 | tf_op jit(solution)/shard_map/add | solution.py:440
  51.8 1.0 %collective-permute-done.8 = bf16[512,128]{1,0:T(8,128)(2,1)S(1)} collective-permute-done((bf16[512,128]{1,0:T(8,128)(2,1)S(1)}, bf16[512,128]{1,0:T(8,128)(2,1)S(1)}, u32[]{:S(2)}, u32[]{:S(2)}) %collective-permute-start.8) | collective-permute-done | bytes 131104 | tf_op jit(solution)/shard_map/ppermute | solution.py:192
  53.0 0.7 %convert_reduce_fusion = (s32[]{:T(128)}, pred[128]{0:T(512)(128)(4,1)S(1)}) fusion(s32[128]{0:T(128)S(1)} %add.276, s32[128]{0:T(128)S(1)} %sub.64, s32[128]{0:T(128)S(1)} %sub.63), kind=kLoop, calls=%fused_computation.84 | loop fusion | flops 2303 | bytes 1668 | tf_op jit(solution)/shard_map/reduce_sum | solution.py:291
  54.6 0.7 %concatenate.6.table_ref = s32[6,128]{1,0:T(8,128)S(1)} pad(s32[5,128]{1,0:T(8,128)S(1)} %select_reduce_fusion, s32[]{:T(128)} %get-tuple-element.44), padding=0_1x0_0 | pad | bytes 5636 | tf_op jit(solution)/shard_map/concatenate | solution.py:292
  55.6 5.9 %shard_map.71 = f32[2,8,128,2048]{3,2,1,0:T(8,128)} custom-call(s32[6,128]{1,0:T(8,128)S(1)} %concatenate.6.table_ref, bf16[8,512,128]{2,1,0:T(8,128)(2,1)S(1)} %bitcast_dynamic-update-slice_fusion.near_ref, bf16[8,512,128]{2,1,0:T(8,128)(2,1)S(1)} %collective-permute-done.11.other_ref, ...), custom_call_target="tpu_custom_call", output_to_operand_aliasing={{}: (3, {})} | custom-call | bytes 16777216 | tf_op jit(solution)/shard_map/pallas_call | solution.py:387
  (46 shorter events, 4.6 us)
Async XLA Ops:
  0.0 14.1 %copy-start.1 = (f32[2,16,4096]{2,1,0:T(8,128)S(1)}, f32[2,16,4096]{2,1,0:T(8,128)}, u32[]{:S(2)}) copy-start(f32[2,16,4096]{2,1,0:T(8,128)} %places_ref.5) | copy-start | bytes 1572868
  0.0 14.1 %copy-start = (bf16[8,16,4096]{2,1,0:T(8,128)(2,1)S(1)}, bf16[8,16,4096]{2,1,0:T(8,128)(2,1)}, u32[]{:S(2)}) copy-start(bf16[8,16,4096]{2,1,0:T(8,128)(2,1)} %values_ref.5) | copy-start | bytes 3145732
  10.9 8.1 %collective-permute-start.1 = (bf16[16,16]{1,0:T(8,128)(2,1)S(1)}, bf16[16,16]{1,0:T(8,128)(2,1)S(1)}, u32[]{:S(2)}, u32[]{:S(2)}) collective-permute-start(bf16[16,16]{1,0:T(8,128)(2,1)S(1)} %get-tuple-element.24.numbers_ref), channel_id=1, source_target_pairs={{0,4},{4,0},{8,12},{12,8},{16,20},{20,16},{24,28},{28,24},{1,5},{5... | collective-permute-start | bytes 1544 | tf_op jit(solution)/shard_map/ppermute | solution.py:192
  11.5 9.6 %collective-permute-start = (bf16[2,4,128,128]{3,2,1,0:T(8,128)(2,1)S(1)}, bf16[2,4,128,128]{3,2,1,0:T(8,128)(2,1)S(1)}, u32[]{:S(2)}, u32[]{:S(2)}) collective-permute-start(bf16[2,4,128,128]{3,2,1,0:T(8,128)(2,1)S(1)} %get-tuple-element.21), channel_id=1, source_target_pairs={{0,1},{1,0},{2,3},{3,2},{4,5},{5,4},{6,7},{7,6},{8,9},{9,8},{10,11... | collective-permute-start | bytes 786440 | tf_op jit(solution)/shard_map/ppermute | solution.py:192
  21.1 9.3 %collective-permute-start.2 = (bf16[1,4,128,128]{3,2,1,0:T(8,128)(2,1)S(1)}, bf16[1,4,128,128]{3,2,1,0:T(8,128)(2,1)S(1)}, u32[]{:S(2)}, u32[]{:S(2)}) collective-permute-start(bf16[1,4,128,128]{3,2,1,0:T(8,128)(2,1)S(1)} %get-tuple-element.26.rest_0_), channel_id=1, source_target_pairs={{0,2},{1,3},{2,0},{3,1},{4,6},{5,7},{6,4},{7,5},{8,10},{9,11},{10,... | collective-permute-start | bytes 393224 | tf_op jit(solution)/shard_map/ppermute | solution.py:192
  28.8 7.7 %collective-permute-start.6 = (bf16[2,4,128,128]{3,2,1,0:T(8,128)(2,1)S(1)}, bf16[2,4,128,128]{3,2,1,0:T(8,128)(2,1)S(1)}, u32[]{:S(2)}, u32[]{:S(2)}) collective-permute-start(bf16[2,4,128,128]{3,2,1,0:T(8,128)(2,1)S(1)} %get-tuple-element.29), channel_id=1, source_target_pairs={{0,1},{1,0},{2,3},{3,2},{4,5},{5,4},{6,7},{7,6},{8,9},{9,8},{10,11... | collective-permute-start | bytes 786440 | tf_op jit(solution)/shard_map/ppermute | solution.py:192
  30.9 6.9 %collective-permute-start.5 = (bf16[528,128]{1,0:T(8,128)(2,1)S(1)}, bf16[528,128]{1,0:T(8,128)(2,1)S(1)}, u32[]{:S(2)}, u32[]{:S(2)}) collective-permute-start(bf16[528,128]{1,0:T(8,128)(2,1)S(1)} %shard_map.67.rest_0_), channel_id=1, source_target_pairs={{0,24},{4,28},{8,16},{12,20},{16,8},{20,12},{24,0},{28,4},{1,25},{... | collective-permute-start | bytes 405512 | tf_op jit(solution)/shard_map/ppermute | solution.py:192
  33.4 5.9 %collective-permute-start.4 = (bf16[528,128]{1,0:T(8,128)(2,1)S(1)}, bf16[528,128]{1,0:T(8,128)(2,1)S(1)}, u32[]{:S(2)}, u32[]{:S(2)}) collective-permute-start(bf16[528,128]{1,0:T(8,128)(2,1)S(1)} %shard_map.67.rest_0_), channel_id=1, source_target_pairs={{0,16},{4,20},{8,24},{12,28},{16,0},{20,4},{24,8},{28,12},{1,17},{... | collective-permute-start | bytes 405512 | tf_op jit(solution)/shard_map/ppermute | solution.py:192
  33.9 5.5 %collective-permute-start.3 = (bf16[528,128]{1,0:T(8,128)(2,1)S(1)}, bf16[528,128]{1,0:T(8,128)(2,1)S(1)}, u32[]{:S(2)}, u32[]{:S(2)}) collective-permute-start(bf16[528,128]{1,0:T(8,128)(2,1)S(1)} %shard_map.67.rest_0_), channel_id=1, source_target_pairs={{0,8},{4,12},{8,0},{12,4},{16,24},{20,28},{24,16},{28,20},{1,9},{5... | collective-permute-start | bytes 405512 | tf_op jit(solution)/shard_map/ppermute | solution.py:192
  36.5 7.8 %collective-permute-start.7 = (bf16[1,4,128,128]{3,2,1,0:T(8,128)(2,1)S(1)}, bf16[1,4,128,128]{3,2,1,0:T(8,128)(2,1)S(1)}, u32[]{:S(2)}, u32[]{:S(2)}) collective-permute-start(bf16[1,4,128,128]{3,2,1,0:T(8,128)(2,1)S(1)} %get-tuple-element.31), channel_id=1, source_target_pairs={{0,2},{1,3},{2,0},{3,1},{4,6},{5,7},{6,4},{7,5},{8,10},{9,11},{10,... | collective-permute-start | bytes 393224 | tf_op jit(solution)/shard_map/ppermute | solution.py:192
  44.8 8.1 %collective-permute-start.10 = (bf16[512,128]{1,0:T(8,128)(2,1)S(1)}, bf16[512,128]{1,0:T(8,128)(2,1)S(1)}, u32[]{:S(2)}, u32[]{:S(2)}) collective-permute-start(bf16[512,128]{1,0:T(8,128)(2,1)S(1)} %get-tuple-element.34), channel_id=1, source_target_pairs={{0,24},{4,28},{8,16},{12,20},{16,8},{20,12},{24,0},{28,4},{1,25},{... | collective-permute-start | bytes 393224 | tf_op jit(solution)/shard_map/ppermute | solution.py:192
  47.3 5.5 %collective-permute-start.9 = (bf16[512,128]{1,0:T(8,128)(2,1)S(1)}, bf16[512,128]{1,0:T(8,128)(2,1)S(1)}, u32[]{:S(2)}, u32[]{:S(2)}) collective-permute-start(bf16[512,128]{1,0:T(8,128)(2,1)S(1)} %get-tuple-element.34), channel_id=1, source_target_pairs={{0,16},{4,20},{8,24},{12,28},{16,0},{20,4},{24,8},{28,12},{1,17},{... | collective-permute-start | bytes 393224 | tf_op jit(solution)/shard_map/ppermute | solution.py:192
  47.9 5.0 %collective-permute-start.8 = (bf16[512,128]{1,0:T(8,128)(2,1)S(1)}, bf16[512,128]{1,0:T(8,128)(2,1)S(1)}, u32[]{:S(2)}, u32[]{:S(2)}) collective-permute-start(bf16[512,128]{1,0:T(8,128)(2,1)S(1)} %get-tuple-element.34), channel_id=1, source_target_pairs={{0,8},{4,12},{8,0},{12,4},{16,24},{20,28},{24,16},{28,20},{1,9},{5... | collective-permute-start | bytes 393224 | tf_op jit(solution)/shard_map/ppermute | solution.py:192
  52.9 2.7 %collective-permute-start.11 = (bf16[8,512,128]{2,1,0:T(8,128)(2,1)S(1)}, bf16[8,512,128]{2,1,0:T(8,128)(2,1)S(1)}, u32[]{:S(2)}, u32[]{:S(2)}) collective-permute-start(bf16[8,512,128]{2,1,0:T(8,128)(2,1)S(1)} %bitcast_dynamic-update-slice_fusion.near_ref), channel_id=1, source_target_pairs={{0,4},{4,0},{8,12},{12,8},{16,20},{20,16},{24,28},{28,24},{1,5},{5... | collective-permute-start | bytes 3145736 | tf_op jit(solution)/shard_map/ppermute | solution.py:192

commit v8 on v7

--- a/solution.py
+++ b/solution.py
@@ -18,7 +18,6 @@
 BLOCKS = NV // LANES
 META = 16
 MIXED = 256
-STEP = 4
 
 VMEM = pl.BlockSpec(memory_space=pltpu.VMEM)
 SMEM = pl.BlockSpec(memory_space=pltpu.SMEM)
@@ -36,7 +35,7 @@
     return jnp.concatenate(rows + [blank], axis=0).astype(jnp.float32).astype(jnp.bfloat16)
 
 
-def grid_kernel(me_ref, values_ref, places_ref, *rest, peers, first, turns, earlier):
+def grid_kernel(me_ref, values_ref, places_ref, *rest, peers, first, subs, step, earlier):
     if first:
         places_from, (kept_ref, sent_ref, out_ref, numbers_ref), rest = rest[:4], rest[4:8], rest[8:]
         values_wide, sums, blank, sem, values, places, in_sem, numbers, numbers_sem = rest
@@ -98,35 +97,35 @@
         return straight + jnp.transpose(crossed)
 
     def some_subs(turn, carry):
-        for pair in range(STEP // 2):
-            sub = turn * STEP + pair * 2
+        for pair in range(step // 2):
+            sub = turn * step + pair * 2
             sums[pair] = jnp.concatenate([one_sub(sub), one_sub(sub + 1)], axis=1).astype(jnp.bfloat16)
-        for pair in range(STEP // 2):
+        for pair in range(step // 2):
             for mask in range(peers):
                 rows = pl.ds(pl.multiple_of((me_ref[0] ^ mask) * rows_each, rows_each), rows_each)
                 target = sent_ref if mask % 2 else kept_ref
-                target[mask // 2, turn * (STEP // 2) + pair] = sums[pair, rows, :]
+                target[mask // 2, turn * (step // 2) + pair] = sums[pair, rows, :]
         return carry
 
-    lax.fori_loop(*turns, some_subs, 0)
+    lax.fori_loop(subs[0] // step, subs[1] // step, some_subs, 0)
     if first:
         for copy in zero_copies:
             copy.wait()
 
 
-def grid_parts(values, places, peers, chunk, turns, order=None, numbers=(), earlier=()):
+def grid_parts(values, places, peers, chunk, subs, step, order=None, numbers=(), earlier=()):
     comp_count, all_subs, row_count = values.shape
     sub_count = all_subs // 2
     rows_each = comp_count // peers * SUB
     first = order is None
     me = lax.axis_index("tm").astype(jnp.int32).reshape(1)
-    parts_shape = (peers // 2, turns[1] * STEP // 2, rows_each, LANES)
+    parts_shape = (peers // 2, subs[1] // 2, rows_each, LANES)
     values_block, places_block = (comp_count, sub_count, row_count), (2, sub_count, row_count)
     out_shape = [jax.ShapeDtypeStruct(parts_shape, jnp.bfloat16)] * 2
     out_specs = [pl.BlockSpec(parts_shape, lambda i: (0, 0, 0, 0))] * 2
     scratch = [
         pltpu.VMEM((comp_count * sub_count, row_count), jnp.float32),
-        pltpu.VMEM((STEP // 2, comp_count * SUB, LANES), jnp.bfloat16),
+        pltpu.VMEM((step // 2, comp_count * SUB, LANES), jnp.bfloat16),
     ]
     if first:
         values, places = (pltpu.with_memory_space_constraint(array, pltpu.HBM) for array in (values, places))
@@ -151,7 +150,7 @@
         in_specs += [pl.BlockSpec(array.shape, lambda i: (0, 0, 0, 0)) for array in earlier]
         more = [order, *earlier]
     return pl.pallas_call(
-        functools.partial(grid_kernel, peers=peers, first=first, turns=turns, earlier=bool(earlier)),
+        functools.partial(grid_kernel, peers=peers, first=first, subs=subs, step=step, earlier=bool(earlier)),
         grid=(1,),
         out_shape=out_shape,
         in_specs=[SMEM] + in_specs,
@@ -159,7 +158,7 @@
         scratch_shapes=scratch,
         compiler_params=pltpu.CompilerParams(vmem_limit_bytes=48 << 20),
         cost_estimate=pl.CostEstimate(
-            flops=8 * (turns[1] - turns[0]) * STEP * row_count * SUB * SUB * comp_count,
+            flops=8 * (subs[1] - subs[0]) * row_count * SUB * SUB * comp_count,
             bytes_accessed=2 << 20,
             transcendentals=0,
         ),
@@ -407,19 +406,22 @@
     tile = lax.axis_index("uv")
     half = sub_count // 2
 
-    split = half // STEP // 2
+    split = half * 3 // 4
     *parts_a, tile_grid, own_numbers = grid_parts(
         visibilities,
         positions,
         peers,
         0,
-        (0, half // STEP),
+        (0, half),
+        half // 2,
         numbers=(owner.T, row_offset[None], w_plane[None], col_offset[None]),
     )
     other_numbers = paired(own_numbers, "uv", 1)
-    parts_b = grid_parts(visibilities, positions, peers, 1, (0, split), order=tile_grid)
+    parts_b = grid_parts(visibilities, positions, peers, 1, (0, split), split, order=tile_grid)
     kept_a, sent_a = halve_all(*parts_a, "tm", [parts_b[0], other_numbers])
-    parts_b = grid_parts(visibilities, positions, peers, 1, (split, half // STEP), order=sent_a, earlier=parts_b)
+    parts_b = grid_parts(
+        visibilities, positions, peers, 1, (split, half), half - split, order=sent_a, earlier=parts_b
+    )
     kept_b, sent_b = halve_all(*parts_b, "tm", [])
     arrived_a, arrived_b = (paired(sent, "tm", peers // 2) for sent in (sent_a, sent_b))
     (sum_a,) = sum_parts(kept_a, arrived_a, 0, own_numbers, [], [other_numbers])

time: 61.4 us -> 62.9 us (1.024)
  the two profiles are of different devices: /device:TPU:0 before, /device:TPU:1 now
where the time goes in v8:
time: 62.9 us; the launch traced here: 62.6 us
  Pallas kernels  27.4 us (44%)
  waiting for transfers between devices  17 us (27%)
  starting transfers between devices  12.2 us (19%)
  local copies, waits for them, and re-layouts  2.86 us (5%)
  other arithmetic  2.82 us (4%)
    pallas_call x3, Pallas kernels, grid_parts(): pl.pallas_call(functools.partial(grid_kernel, peers=peers, first=first, s...  20.7 us
    ppermute x12, waiting for transfers between devices, paired(): lax.ppermute(array, axis, [(i, i ^ mask) for i in range(lax.axis_size(axi...  17 us
    ppermute x12, starting transfers between devices, paired(): lax.ppermute(array, axis, [(i, i ^ mask) for i in range(lax.axis_size(axi...  12.2 us
    pallas_call x1, Pallas kernels, place_all(): pl.pallas_call(place_kernel, out_shape=jax.ShapeDtypeStruct(tile_grid.sha...  5.63 us
  transfers between devices with their start and end apart: 12, of which 6 were waited for; matrix products, arithmetic and copies ran while one was open for 9% of the time, Pallas kernels for 16%

profile of v8, /device:TPU:1, one launch (start us, length us, event | category | flops | bytes accessed | tf_op | source)
XLA Modules:
  0.0 62.6 jit_solution(1033766768182320772)
XLA Ops:
  0.0 10.9 %shard_map.64 = (bf16[2,4,128,128]{3,2,1,0:T(8,128)(2,1)S(1)}, bf16[2,4,128,128]{3,2,1,0:T(8,128)(2,1)S(1)}, f32[2,8,128,2048]{3,2,1,0:T(8,128)}, bf16[16,16]{1,0:T(8,128)(2,1)S(1)}) custom-call(s32[1]{0:T(128)} %bitcast.me_ref, bf16[8,16,4096]{2,1,0:T(8,128)(2,1)} %values_ref.5, f32[2,16,4096]{2,1,0:T(8,128)} %places_ref.5, s32[1,16]{1,0:T(1,128)} %bitcast.50, ...), custom_call_target="tpu_custom_call" | custom-call | flops 8589934592 | bytes 2097152 | tf_op jit(solution)/shard_map/pallas_call | solution.py:152
  11.1 2.8 %collective-permute-start = (bf16[2,4,128,128]{3,2,1,0:T(8,128)(2,1)S(1)}, bf16[2,4,128,128]{3,2,1,0:T(8,128)(2,1)S(1)}, u32[]{:S(2)}, u32[]{:S(2)}) collective-permute-start(bf16[2,4,128,128]{3,2,1,0:T(8,128)(2,1)S(1)} %get-tuple-element.21), channel_id=1, source_target_pairs={{0,1},{1,0},{2,3},{3,2},{4,5},{5,4},{6,7},{7,6},{8,9},{9,8},{10,11... | collective-permute-start | bytes 786440 | tf_op jit(solution)/shard_map/ppermute | solution.py:191
  13.8 7.1 %shard_map.65 = (bf16[2,3,128,128]{3,2,1,0:T(8,128)(2,1)S(1)}, bf16[2,3,128,128]{3,2,1,0:T(8,128)(2,1)S(1)}) custom-call(s32[1]{0:T(128)} %bitcast.me_ref, bf16[8,16,4096]{2,1,0:T(8,128)(2,1)S(1)} %copy-done, f32[2,16,4096]{2,1,0:T(8,128)S(1)} %copy-done.1, f32[2,8,128,2048]{3,2,1,0:T(8,128)} %get-tuple-element.22.rest_0_._), custom_call_target="tpu_custom_call" | custom-call | flops 6442450944 | bytes 2097152 | tf_op jit(solution)/shard_map/pallas_call | solution.py:152
  21.1 2.4 %collective-permute-start.2 = (bf16[1,4,128,128]{3,2,1,0:T(8,128)(2,1)S(1)}, bf16[1,4,128,128]{3,2,1,0:T(8,128)(2,1)S(1)}, u32[]{:S(2)}, u32[]{:S(2)}) collective-permute-start(bf16[1,4,128,128]{3,2,1,0:T(8,128)(2,1)S(1)} %get-tuple-element.26.rest_0_), channel_id=1, source_target_pairs={{0,2},{1,3},{2,0},{3,1},{4,6},{5,7},{6,4},{7,5},{8,10},{9,11},{10,... | collective-permute-start | bytes 393224 | tf_op jit(solution)/shard_map/ppermute | solution.py:191
  23.4 2.6 %shard_map.68 = (bf16[2,4,128,128]{3,2,1,0:T(8,128)(2,1)S(1)}, bf16[2,4,128,128]{3,2,1,0:T(8,128)(2,1)S(1)}) custom-call(s32[1]{0:T(128)} %bitcast.me_ref, bf16[8,16,4096]{2,1,0:T(8,128)(2,1)S(1)} %copy-done, f32[2,16,4096]{2,1,0:T(8,128)S(1)} %copy-done.1, bf16[1,4,128,128]{3,2,1,0:T(8,128)(2,1)S(1)} %get-tuple-element.26.rest_0_, ...), custom_call_target="tpu_custom_call" | custom-call | flops 2147483648 | bytes 2097152 | tf_op jit(solution)/shard_map/pallas_call | solution.py:152
  26.1 0.8 %collective-permute-start.6 = (bf16[2,4,128,128]{3,2,1,0:T(8,128)(2,1)S(1)}, bf16[2,4,128,128]{3,2,1,0:T(8,128)(2,1)S(1)}, u32[]{:S(2)}, u32[]{:S(2)}) collective-permute-start(bf16[2,4,128,128]{3,2,1,0:T(8,128)(2,1)S(1)} %get-tuple-element.29), channel_id=1, source_target_pairs={{0,1},{1,0},{2,3},{3,2},{4,5},{5,4},{6,7},{7,6},{8,9},{9,8},{10,11... | collective-permute-start | bytes 786440 | tf_op jit(solution)/shard_map/ppermute | solution.py:191
  26.8 3.1 %collective-permute-done.2.arrived_ref = bf16[1,4,128,128]{3,2,1,0:T(8,128)(2,1)S(1)} collective-permute-done((bf16[1,4,128,128]{3,2,1,0:T(8,128)(2,1)S(1)}, bf16[1,4,128,128]{3,2,1,0:T(8,128)(2,1)S(1)}, u32[]{:S(2)}, u32[]{:S(2)}) %collective-permute-start.2) | collective-permute-done | bytes 131104 | tf_op jit(solution)/shard_map/ppermute | solution.py:191
  29.9 0.5 shard_map.67.rest_0_
  30.4 2.2 %collective-permute-start.5 = (bf16[528,128]{1,0:T(8,128)(2,1)S(1)}, bf16[528,128]{1,0:T(8,128)(2,1)S(1)}, u32[]{:S(2)}, u32[]{:S(2)}) collective-permute-start(bf16[528,128]{1,0:T(8,128)(2,1)S(1)} %shard_map.67.rest_0_), channel_id=1, source_target_pairs={{0,24},{4,28},{8,16},{12,20},{16,8},{20,12},{24,0},{28,4},{1,25},{... | collective-permute-start | bytes 405512 | tf_op jit(solution)/shard_map/ppermute | solution.py:191
  33.1 2.8 %collective-permute-done.6.arrived_ref = bf16[2,4,128,128]{3,2,1,0:T(8,128)(2,1)S(1)} collective-permute-done((bf16[2,4,128,128]{3,2,1,0:T(8,128)(2,1)S(1)}, bf16[2,4,128,128]{3,2,1,0:T(8,128)(2,1)S(1)}, u32[]{:S(2)}, u32[]{:S(2)}) %collective-permute-start.6) | collective-permute-done | bytes 262176 | tf_op jit(solution)/shard_map/ppermute | solution.py:191
  36.1 3.5 %collective-permute-done.4.rest_2_ = bf16[528,128]{1,0:T(8,128)(2,1)S(1)} collective-permute-done((bf16[528,128]{1,0:T(8,128)(2,1)S(1)}, bf16[528,128]{1,0:T(8,128)(2,1)S(1)}, u32[]{:S(2)}, u32[]{:S(2)}) %collective-permute-start.4) | collective-permute-done | bytes 135200 | tf_op jit(solution)/shard_map/ppermute | solution.py:191
  39.6 4.6 %collective-permute-done.7.arrived_ref = bf16[1,4,128,128]{3,2,1,0:T(8,128)(2,1)S(1)} collective-permute-done((bf16[1,4,128,128]{3,2,1,0:T(8,128)(2,1)S(1)}, bf16[1,4,128,128]{3,2,1,0:T(8,128)(2,1)S(1)}, u32[]{:S(2)}, u32[]{:S(2)}) %collective-permute-start.7) | collective-permute-done | bytes 131104 | tf_op jit(solution)/shard_map/ppermute | solution.py:191
  44.1 0.5 shard_map.70
  44.6 2.2 %collective-permute-start.10 = (bf16[512,128]{1,0:T(8,128)(2,1)S(1)}, bf16[512,128]{1,0:T(8,128)(2,1)S(1)}, u32[]{:S(2)}, u32[]{:S(2)}) collective-permute-start(bf16[512,128]{1,0:T(8,128)(2,1)S(1)} %get-tuple-element.34), channel_id=1, source_target_pairs={{0,24},{4,28},{8,16},{12,20},{16,8},{20,12},{24,0},{28,4},{1,25},{... | collective-permute-start | bytes 393224 | tf_op jit(solution)/shard_map/ppermute | solution.py:191
  47.3 0.6 slice.44
  47.9 0.7 %convert_add_fusion = s32[16,4,32]{2,0,1:T(8,128)S(1)} fusion(bf16[16,1,32]{2,0,1:T(8,128)(2,1)S(1)} %slice_bitcast_fusion, bf16[16,1,32]{2,0,1:T(8,128)(2,1)S(1)} %slice_bitcast_fusion.1, bf16[16,1,32]{2,0,1:T(8,128)(2,1)S(1)} %slice_bitcast_fusion.2, bf16[16,1,32]{2,0,1:T(8,128)(2,1)S(1)} %slice_bitcast_fusion.3, s32[]{:T(128)} %bitcast.9), kind=kLoop, calls=%fused_computation.18 | loop fusion | flops 12288 | bytes 12292 | tf_op jit(solution)/shard_map/add | solution.py:435
  48.6 0.6 broadcast.812
  49.2 0.7 %fusion.23 = (s32[4,32]{1,0:T(4,128)S(1)}, s32[1,4,32]{2,0,1:T(1,128)S(1)}, s32[1,4,32]{2,0,1:T(1,128)S(1)}, s32[1,4,32]{2,0,1:T(1,128)S(1)}, s32[1,4,32]{2,0,1:...) fusion(s32[]{:T(128)} %broadcast.812, ...), kind=kLoop, calls=%fused_computation.93 | loop fusion | flops 640 | bytes 7688 | tf_op jit(solution)/shard_map/add | solution.py:442
  50.7 2.3 %collective-permute-done.8 = bf16[512,128]{1,0:T(8,128)(2,1)S(1)} collective-permute-done((bf16[512,128]{1,0:T(8,128)(2,1)S(1)}, bf16[512,128]{1,0:T(8,128)(2,1)S(1)}, u32[]{:S(2)}, u32[]{:S(2)}) %collective-permute-start.8) | collective-permute-done | bytes 131104 | tf_op jit(solution)/shard_map/ppermute | solution.py:191
  53.1 0.7 %collective-permute-done.9 = bf16[512,128]{1,0:T(8,128)(2,1)S(1)} collective-permute-done((bf16[512,128]{1,0:T(8,128)(2,1)S(1)}, bf16[512,128]{1,0:T(8,128)(2,1)S(1)}, u32[]{:S(2)}, u32[]{:S(2)}) %collective-permute-start.9) | collective-permute-done | bytes 131104 | tf_op jit(solution)/shard_map/ppermute | solution.py:191
  53.9 0.7 %collective-permute-start.11 = (bf16[8,512,128]{2,1,0:T(8,128)(2,1)S(1)}, bf16[8,512,128]{2,1,0:T(8,128)(2,1)S(1)}, u32[]{:S(2)}, u32[]{:S(2)}) collective-permute-start(bf16[8,512,128]{2,1,0:T(8,128)(2,1)S(1)} %bitcast_dynamic-update-slice_fusion.near_ref), channel_id=1, source_target_pairs={{0,4},{4,0},{8,12},{12,8},{16,20},{20,16},{24,28},{28,24},{1,5},{5... | collective-permute-start | bytes 3145736 | tf_op jit(solution)/shard_map/ppermute | solution.py:191
  54.5 0.7 %convert_reduce_fusion = (s32[]{:T(128)}, pred[128]{0:T(512)(128)(4,1)S(1)}) fusion(s32[128]{0:T(128)S(1)} %add.276, s32[128]{0:T(128)S(1)} %sub.64, s32[128]{0:T(128)S(1)} %sub.63), kind=kLoop, calls=%fused_computation.84 | loop fusion | flops 2303 | bytes 1668 | tf_op jit(solution)/shard_map/reduce_sum | solution.py:290
  56.1 0.7 %concatenate.6.table_ref = s32[6,128]{1,0:T(8,128)S(1)} pad(s32[5,128]{1,0:T(8,128)S(1)} %select_reduce_fusion, s32[]{:T(128)} %get-tuple-element.44), padding=0_1x0_0 | pad | bytes 5636 | tf_op jit(solution)/shard_map/concatenate | solution.py:291
  56.8 5.6 %shard_map.71 = f32[2,8,128,2048]{3,2,1,0:T(8,128)} custom-call(s32[6,128]{1,0:T(8,128)S(1)} %concatenate.6.table_ref, bf16[8,512,128]{2,1,0:T(8,128)(2,1)S(1)} %bitcast_dynamic-update-slice_fusion.near_ref, bf16[8,512,128]{2,1,0:T(8,128)(2,1)S(1)} %collective-permute-done.11.other_ref, ...), custom_call_target="tpu_custom_call", output_to_operand_aliasing={{}: (3, {})} | custom-call | bytes 16777216 | tf_op jit(solution)/shard_map/pallas_call | solution.py:386
  (46 shorter events, 2.9 us)
Async XLA Ops:
  0.0 13.8 %copy-start.1 = (f32[2,16,4096]{2,1,0:T(8,128)S(1)}, f32[2,16,4096]{2,1,0:T(8,128)}, u32[]{:S(2)}) copy-start(f32[2,16,4096]{2,1,0:T(8,128)} %places_ref.5) | copy-start | bytes 1572868
  0.0 13.8 %copy-start = (bf16[8,16,4096]{2,1,0:T(8,128)(2,1)S(1)}, bf16[8,16,4096]{2,1,0:T(8,128)(2,1)}, u32[]{:S(2)}) copy-start(bf16[8,16,4096]{2,1,0:T(8,128)(2,1)} %values_ref.5) | copy-start | bytes 3145732
  10.9 10.0 %collective-permute-start.1 = (bf16[16,16]{1,0:T(8,128)(2,1)S(1)}, bf16[16,16]{1,0:T(8,128)(2,1)S(1)}, u32[]{:S(2)}, u32[]{:S(2)}) collective-permute-start(bf16[16,16]{1,0:T(8,128)(2,1)S(1)} %get-tuple-element.24.numbers_ref), channel_id=1, source_target_pairs={{0,4},{4,0},{8,12},{12,8},{16,20},{20,16},{24,28},{28,24},{1,5},{5... | collective-permute-start | bytes 1544 | tf_op jit(solution)/shard_map/ppermute | solution.py:191
  11.1 9.9 %collective-permute-start = (bf16[2,4,128,128]{3,2,1,0:T(8,128)(2,1)S(1)}, bf16[2,4,128,128]{3,2,1,0:T(8,128)(2,1)S(1)}, u32[]{:S(2)}, u32[]{:S(2)}) collective-permute-start(bf16[2,4,128,128]{3,2,1,0:T(8,128)(2,1)S(1)} %get-tuple-element.21), channel_id=1, source_target_pairs={{0,1},{1,0},{2,3},{3,2},{4,5},{5,4},{6,7},{7,6},{8,9},{9,8},{10,11... | collective-permute-start | bytes 786440 | tf_op jit(solution)/shard_map/ppermute | solution.py:191
  21.1 8.8 %collective-permute-start.2 = (bf16[1,4,128,128]{3,2,1,0:T(8,128)(2,1)S(1)}, bf16[1,4,128,128]{3,2,1,0:T(8,128)(2,1)S(1)}, u32[]{:S(2)}, u32[]{:S(2)}) collective-permute-start(bf16[1,4,128,128]{3,2,1,0:T(8,128)(2,1)S(1)} %get-tuple-element.26.rest_0_), channel_id=1, source_target_pairs={{0,2},{1,3},{2,0},{3,1},{4,6},{5,7},{6,4},{7,5},{8,10},{9,11},{10,... | collective-permute-start | bytes 393224 | tf_op jit(solution)/shard_map/ppermute | solution.py:191
  26.1 9.8 %collective-permute-start.6 = (bf16[2,4,128,128]{3,2,1,0:T(8,128)(2,1)S(1)}, bf16[2,4,128,128]{3,2,1,0:T(8,128)(2,1)S(1)}, u32[]{:S(2)}, u32[]{:S(2)}) collective-permute-start(bf16[2,4,128,128]{3,2,1,0:T(8,128)(2,1)S(1)} %get-tuple-element.29), channel_id=1, source_target_pairs={{0,1},{1,0},{2,3},{3,2},{4,5},{5,4},{6,7},{7,6},{8,9},{9,8},{10,11... | collective-permute-start | bytes 786440 | tf_op jit(solution)/shard_map/ppermute | solution.py:191
  30.4 5.7 %collective-permute-start.5 = (bf16[528,128]{1,0:T(8,128)(2,1)S(1)}, bf16[528,128]{1,0:T(8,128)(2,1)S(1)}, u32[]{:S(2)}, u32[]{:S(2)}) collective-permute-start(bf16[528,128]{1,0:T(8,128)(2,1)S(1)} %shard_map.67.rest_0_), channel_id=1, source_target_pairs={{0,24},{4,28},{8,16},{12,20},{16,8},{20,12},{24,0},{28,4},{1,25},{... | collective-permute-start | bytes 405512 | tf_op jit(solution)/shard_map/ppermute | solution.py:191
  32.6 7.0 %collective-permute-start.4 = (bf16[528,128]{1,0:T(8,128)(2,1)S(1)}, bf16[528,128]{1,0:T(8,128)(2,1)S(1)}, u32[]{:S(2)}, u32[]{:S(2)}) collective-permute-start(bf16[528,128]{1,0:T(8,128)(2,1)S(1)} %shard_map.67.rest_0_), channel_id=1, source_target_pairs={{0,16},{4,20},{8,24},{12,28},{16,0},{20,4},{24,8},{28,12},{1,17},{... | collective-permute-start | bytes 405512 | tf_op jit(solution)/shard_map/ppermute | solution.py:191
  32.8 6.8 %collective-permute-start.3 = (bf16[528,128]{1,0:T(8,128)(2,1)S(1)}, bf16[528,128]{1,0:T(8,128)(2,1)S(1)}, u32[]{:S(2)}, u32[]{:S(2)}) collective-permute-start(bf16[528,128]{1,0:T(8,128)(2,1)S(1)} %shard_map.67.rest_0_), channel_id=1, source_target_pairs={{0,8},{4,12},{8,0},{12,4},{16,24},{20,28},{24,16},{28,20},{1,9},{5... | collective-permute-start | bytes 405512 | tf_op jit(solution)/shard_map/ppermute | solution.py:191
  36.0 8.2 %collective-permute-start.7 = (bf16[1,4,128,128]{3,2,1,0:T(8,128)(2,1)S(1)}, bf16[1,4,128,128]{3,2,1,0:T(8,128)(2,1)S(1)}, u32[]{:S(2)}, u32[]{:S(2)}) collective-permute-start(bf16[1,4,128,128]{3,2,1,0:T(8,128)(2,1)S(1)} %get-tuple-element.31), channel_id=1, source_target_pairs={{0,2},{1,3},{2,0},{3,1},{4,6},{5,7},{6,4},{7,5},{8,10},{9,11},{10,... | collective-permute-start | bytes 393224 | tf_op jit(solution)/shard_map/ppermute | solution.py:191
  44.6 9.2 %collective-permute-start.10 = (bf16[512,128]{1,0:T(8,128)(2,1)S(1)}, bf16[512,128]{1,0:T(8,128)(2,1)S(1)}, u32[]{:S(2)}, u32[]{:S(2)}) collective-permute-start(bf16[512,128]{1,0:T(8,128)(2,1)S(1)} %get-tuple-element.34), channel_id=1, source_target_pairs={{0,24},{4,28},{8,16},{12,20},{16,8},{20,12},{24,0},{28,4},{1,25},{... | collective-permute-start | bytes 393224 | tf_op jit(solution)/shard_map/ppermute | solution.py:191
  46.8 7.0 %collective-permute-start.9 = (bf16[512,128]{1,0:T(8,128)(2,1)S(1)}, bf16[512,128]{1,0:T(8,128)(2,1)S(1)}, u32[]{:S(2)}, u32[]{:S(2)}) collective-permute-start(bf16[512,128]{1,0:T(8,128)(2,1)S(1)} %get-tuple-element.34), channel_id=1, source_target_pairs={{0,16},{4,20},{8,24},{12,28},{16,0},{20,4},{24,8},{28,12},{1,17},{... | collective-permute-start | bytes 393224 | tf_op jit(solution)/shard_map/ppermute | solution.py:191
  47.1 6.0 %collective-permute-start.8 = (bf16[512,128]{1,0:T(8,128)(2,1)S(1)}, bf16[512,128]{1,0:T(8,128)(2,1)S(1)}, u32[]{:S(2)}, u32[]{:S(2)}) collective-permute-start(bf16[512,128]{1,0:T(8,128)(2,1)S(1)} %get-tuple-element.34), channel_id=1, source_target_pairs={{0,8},{4,12},{8,0},{12,4},{16,24},{20,28},{24,16},{28,20},{1,9},{5... | collective-permute-start | bytes 393224 | tf_op jit(solution)/shard_map/ppermute | solution.py:191
  53.9 3.0 %collective-permute-start.11 = (bf16[8,512,128]{2,1,0:T(8,128)(2,1)S(1)}, bf16[8,512,128]{2,1,0:T(8,128)(2,1)S(1)}, u32[]{:S(2)}, u32[]{:S(2)}) collective-permute-start(bf16[8,512,128]{2,1,0:T(8,128)(2,1)S(1)} %bitcast_dynamic-update-slice_fusion.near_ref), channel_id=1, source_target_pairs={{0,4},{4,0},{8,12},{12,8},{16,20},{20,16},{24,28},{28,24},{1,5},{5... | collective-permute-start | bytes 3145736 | tf_op jit(solution)/shard_map/ppermute | solution.py:191

commit v9 on v6

--- a/solution.py
+++ b/solution.py
@@ -424,12 +424,12 @@
 
     told = jnp.stack([hop[half * SUB :, : 2 * sub_count] for hop in hops_a], axis=1).astype(jnp.float32).astype(jnp.int32)
     chips = told.shape[1]
-    told = told.reshape(META, -1) + go[0, 0]
+    told = told.reshape(META, -1)
     entry = jnp.arange(told.shape[1], dtype=jnp.int32)
     chip, sub = entry // (2 * sub_count), entry % sub_count
     others = entry // sub_count % 2
     spots = ((sub // half * chips + chip) << 16) + sub % half * SUB
-    ahead = (told[0] - tile) % tiles
+    ahead = (told[0] - tile + go[0, 0]) % tiles
     starts = jnp.where(ahead == 0, told[1] + SUB, jnp.where(ahead == tiles - 1, told[1] + SUB - TU, -1))
     table = touch_plan(starts, told[2], told[3] * LANES + told[4], spots, others)
     return place_all(near, other, table, tile_grid)

time: 59.7 us -> 60.7 us (1.017); the launches traced: 59.2 us -> 61.1 us
  Pallas kernels: 25.2 us -> 27.2 us
    pallas_call x1, Pallas kernels: 3.71 us -> 5.66 us  [place_all(): pl.pallas_call(place_kernel, out_shape=jax.ShapeDtypeStruct(tile_grid.sha...]
    reduce_sum x1, other arithmetic: 0.72 us -> 1.89 us  [touch_plan(): number = jnp.sum(taken.astype(jnp.int32))]
    sub x3 -> x0, local copies, waits for them, and re-layouts: 0.76 us -> none  [body(): ahead = (told[0] - tile) % tiles]
    add x2, other arithmetic: 0.72 us -> 0.04 us  [the longest x1 0.03 us: touch_plan(): edges(left) + jnp.where(right >= 0, 4 * edges(right), 0) + 16 * others]
  transfers between devices with their start and end apart: 12 -> 12, of which waited for: 9 -> 9; matrix products, arithmetic and copies ran while one was open for 10% -> 9% of each run, Pallas kernels for 17% -> 17%
where the time goes in v9:
time: 60.7 us; the launch traced here: 61.1 us
  Pallas kernels  27.2 us (45%)
  starting transfers between devices  15.2 us (25%)
  waiting for transfers between devices  12.6 us (21%)
  other arithmetic  3.14 us (5%)
  local copies, waits for them, and re-layouts  2.65 us (4%)
    pallas_call x3, Pallas kernels, grid_parts(): pl.pallas_call(functools.partial(grid_kernel, peers=peers, first=first, t...  20.4 us
    ppermute x12, starting transfers between devices, paired(): lax.ppermute(array, axis, [(i, i ^ mask) for i in range(lax.axis_size(axi...  15.2 us
    ppermute x12, waiting for transfers between devices, paired(): lax.ppermute(array, axis, [(i, i ^ mask) for i in range(lax.axis_size(axi...  12.6 us
    pallas_call x1, Pallas kernels, place_all(): pl.pallas_call(place_kernel, out_shape=jax.ShapeDtypeStruct(tile_grid.sha...  5.66 us
    reduce_sum x1, other arithmetic, touch_plan(): number = jnp.sum(taken.astype(jnp.int32))  1.89 us
  transfers between devices with their start and end apart: 12, of which 9 were waited for; matrix products, arithmetic and copies ran while one was open for 9% of the time, Pallas kernels for 17%

profile of v9, /device:TPU:0, one launch (start us, length us, event | category | flops | bytes accessed | tf_op | source)
XLA Modules:
  0.0 61.1 jit_solution(6791657722207906724)
XLA Ops:
  0.0 10.7 %shard_map.64 = (bf16[2,4,128,128]{3,2,1,0:T(8,128)(2,1)S(1)}, bf16[2,4,128,128]{3,2,1,0:T(8,128)(2,1)S(1)}, f32[2,8,128,2048]{3,2,1,0:T(8,128)}) custom-call(s32[1]{0:T(128)} %bitcast.me_ref, bf16[8,16,4096]{2,1,0:T(8,128)(2,1)} %values_ref.5, f32[2,16,4096]{2,1,0:T(8,128)} %places_ref.5), custom_call_target="tpu_custom_call" | custom-call | flops 8589934592 | bytes 2097152 | tf_op jit(solution)/shard_map/pallas_call | solution.py:146
  10.8 3.1 %collective-permute-start = (bf16[2,4,128,128]{3,2,1,0:T(8,128)(2,1)S(1)}, bf16[2,4,128,128]{3,2,1,0:T(8,128)(2,1)S(1)}, u32[]{:S(2)}, u32[]{:S(2)}) collective-permute-start(bf16[2,4,128,128]{3,2,1,0:T(8,128)(2,1)S(1)} %get-tuple-element.21), channel_id=1, source_target_pairs={{0,1},{1,0},{2,3},{3,2},{4,5},{5,4},{6,7},{7,6},{8,9},{9,8},{10,11... | collective-permute-start | bytes 786440 | tf_op jit(solution)/shard_map/ppermute | solution.py:185
  13.9 4.9 %shard_map.65 = (bf16[2,2,128,128]{3,2,1,0:T(8,128)(2,1)S(1)}, bf16[2,2,128,128]{3,2,1,0:T(8,128)(2,1)S(1)}, bf16[16,16]{1,0:T(8,128)(2,1)S(1)}) custom-call(s32[1]{0:T(128)} %bitcast.me_ref, bf16[8,16,4096]{2,1,0:T(8,128)(2,1)S(1)} %copy-done, f32[2,16,4096]{2,1,0:T(8,128)S(1)} %copy-done.1, f32[2,8,128,2048]{3,2,1,0:T(8,128)} %get-tuple-element.22.rest_0_._, ...), custom_call_target="tpu_custom_call" | custom-call | flops 4294967296 | bytes 2097152 | tf_op jit(solution)/shard_map/pallas_call | solution.py:146
  18.8 1.2 %collective-permute-done.1.rest_0_ = bf16[16,16]{1,0:T(8,128)(2,1)S(1)} collective-permute-done((bf16[16,16]{1,0:T(8,128)(2,1)S(1)}, bf16[16,16]{1,0:T(8,128)(2,1)S(1)}, u32[]{:S(2)}, u32[]{:S(2)}) %collective-permute-start.1) | collective-permute-done | bytes 544 | tf_op jit(solution)/shard_map/ppermute | solution.py:185
  20.2 2.8 %collective-permute-start.2 = (bf16[1,4,128,128]{3,2,1,0:T(8,128)(2,1)S(1)}, bf16[1,4,128,128]{3,2,1,0:T(8,128)(2,1)S(1)}, u32[]{:S(2)}, u32[]{:S(2)}) collective-permute-start(bf16[1,4,128,128]{3,2,1,0:T(8,128)(2,1)S(1)} %get-tuple-element.25.rest_0_), channel_id=1, source_target_pairs={{0,2},{1,3},{2,0},{3,1},{4,6},{5,7},{6,4},{7,5},{8,10},{9,11},{10,... | collective-permute-start | bytes 393224 | tf_op jit(solution)/shard_map/ppermute | solution.py:185
  23.0 4.8 %shard_map.68 = (bf16[2,4,128,128]{3,2,1,0:T(8,128)(2,1)S(1)}, bf16[2,4,128,128]{3,2,1,0:T(8,128)(2,1)S(1)}) custom-call(s32[1]{0:T(128)} %bitcast.me_ref, bf16[8,16,4096]{2,1,0:T(8,128)(2,1)S(1)} %copy-done, f32[2,16,4096]{2,1,0:T(8,128)S(1)} %copy-done.1, bf16[1,4,128,128]{3,2,1,0:T(8,128)(2,1)S(1)} %get-tuple-element.25.rest_0_, ...), custom_call_target="tpu_custom_call" | custom-call | flops 4294967296 | bytes 2097152 | tf_op jit(solution)/shard_map/pallas_call | solution.py:146
  27.9 1.7 %collective-permute-start.6 = (bf16[2,4,128,128]{3,2,1,0:T(8,128)(2,1)S(1)}, bf16[2,4,128,128]{3,2,1,0:T(8,128)(2,1)S(1)}, u32[]{:S(2)}, u32[]{:S(2)}) collective-permute-start(bf16[2,4,128,128]{3,2,1,0:T(8,128)(2,1)S(1)} %get-tuple-element.29), channel_id=1, source_target_pairs={{0,1},{1,0},{2,3},{3,2},{4,5},{5,4},{6,7},{7,6},{8,9},{9,8},{10,11... | collective-permute-start | bytes 786440 | tf_op jit(solution)/shard_map/ppermute | solution.py:185
  30.0 2.5 %collective-permute-start.5 = (bf16[528,128]{1,0:T(8,128)(2,1)S(1)}, bf16[528,128]{1,0:T(8,128)(2,1)S(1)}, u32[]{:S(2)}, u32[]{:S(2)}) collective-permute-start(bf16[528,128]{1,0:T(8,128)(2,1)S(1)} %shard_map.67.rest_0_), channel_id=1, source_target_pairs={{0,24},{4,28},{8,16},{12,20},{16,8},{20,12},{24,0},{28,4},{1,25},{... | collective-permute-start | bytes 405512 | tf_op jit(solution)/shard_map/ppermute | solution.py:185
  32.5 0.5 collective-permute-start.4
  33.0 0.5 collective-permute-start.3
  33.6 2.1 %collective-permute-done.6.arrived_ref = bf16[2,4,128,128]{3,2,1,0:T(8,128)(2,1)S(1)} collective-permute-done((bf16[2,4,128,128]{3,2,1,0:T(8,128)(2,1)S(1)}, bf16[2,4,128,128]{3,2,1,0:T(8,128)(2,1)S(1)}, u32[]{:S(2)}, u32[]{:S(2)}) %collective-permute-start.6) | collective-permute-done | bytes 262176 | tf_op jit(solution)/shard_map/ppermute | solution.py:185
  36.6 2.5 %collective-permute-done.4.rest_2_ = bf16[528,128]{1,0:T(8,128)(2,1)S(1)} collective-permute-done((bf16[528,128]{1,0:T(8,128)(2,1)S(1)}, bf16[528,128]{1,0:T(8,128)(2,1)S(1)}, u32[]{:S(2)}, u32[]{:S(2)}) %collective-permute-start.4) | collective-permute-done | bytes 135200 | tf_op jit(solution)/shard_map/ppermute | solution.py:185
  39.1 0.5 broadcast.1170
  39.6 0.6 fusion.32
  40.6 3.0 %collective-permute-done.7.arrived_ref = bf16[1,4,128,128]{3,2,1,0:T(8,128)(2,1)S(1)} collective-permute-done((bf16[1,4,128,128]{3,2,1,0:T(8,128)(2,1)S(1)}, bf16[1,4,128,128]{3,2,1,0:T(8,128)(2,1)S(1)}, u32[]{:S(2)}, u32[]{:S(2)}) %collective-permute-start.7) | collective-permute-done | bytes 131104 | tf_op jit(solution)/shard_map/ppermute | solution.py:185
  44.1 2.5 %collective-permute-start.10 = (bf16[512,128]{1,0:T(8,128)(2,1)S(1)}, bf16[512,128]{1,0:T(8,128)(2,1)S(1)}, u32[]{:S(2)}, u32[]{:S(2)}) collective-permute-start(bf16[512,128]{1,0:T(8,128)(2,1)S(1)} %get-tuple-element.34), channel_id=1, source_target_pairs={{0,24},{4,28},{8,16},{12,20},{16,8},{20,12},{24,0},{28,4},{1,25},{... | collective-permute-start | bytes 393224 | tf_op jit(solution)/shard_map/ppermute | solution.py:185
  46.6 0.5 collective-permute-start.9
  47.1 0.5 collective-permute-start.8
  47.6 0.6 slice.41
  48.2 1.9 %fusion.10 = (s32[]{:T(128)}, s32[4,32]{1,0:T(4,128)S(1)}, s32[4,32]{1,0:T(4,128)S(1)}, s32[4,32]{1,0:T(4,128)S(1)}, s32[1,4,32]{2,0,1:T(1,128)S(1)}, /*index=5*/bf16[1,4,32]{2,0,1:T(2,128)(2,1)S(1)}) fusion(s32[]{:T(128)} %broadcast.1170, s32[]{:T(128)} %bitcast.9, s32[]{:T(128)S(6)} %axis_index.33, bf16[16,1,32]{2,0,1:T(8,128)(2,1)S(1)} %slice_bitcast_fusion, ...), kind=kLoop, calls=%fused_computation.70 | loop fusion | flops 5247 | bytes 6416 | tf_op jit(solution)/shard_map/reduce_sum | solution.py:284
  50.5 2.0 %collective-permute-done.8 = bf16[512,128]{1,0:T(8,128)(2,1)S(1)} collective-permute-done((bf16[512,128]{1,0:T(8,128)(2,1)S(1)}, bf16[512,128]{1,0:T(8,128)(2,1)S(1)}, u32[]{:S(2)}, u32[]{:S(2)}) %collective-permute-start.8) | collective-permute-done | bytes 131104 | tf_op jit(solution)/shard_map/ppermute | solution.py:185
  53.6 0.6 concatenate.6.table_ref
  54.2 1.1 %collective-permute-done.11.other_ref = bf16[8,512,128]{2,1,0:T(8,128)(2,1)S(1)} collective-permute-done((bf16[8,512,128]{2,1,0:T(8,128)(2,1)S(1)}, bf16[8,512,128]{2,1,0:T(8,128)(2,1)S(1)}, u32[]{:S(2)}, u32[]{:S(2)}) %collective-permute-start.11) | collective-permute-done | bytes 1048608 | tf_op jit(solution)/shard_map/ppermute | solution.py:185
  55.3 5.7 %shard_map.71 = f32[2,8,128,2048]{3,2,1,0:T(8,128)} custom-call(s32[6,128]{1,0:T(8,128)S(1)} %concatenate.6.table_ref, bf16[8,512,128]{2,1,0:T(8,128)(2,1)S(1)} %bitcast_dynamic-update-slice_fusion.near_ref, bf16[8,512,128]{2,1,0:T(8,128)(2,1)S(1)} %collective-permute-done.11.other_ref, ...), custom_call_target="tpu_custom_call", output_to_operand_aliasing={{}: (3, {})} | custom-call | bytes 16777216 | tf_op jit(solution)/shard_map/pallas_call | solution.py:380
  (53 shorter events, 3.9 us)
Async XLA Ops:
  0.0 13.8 %copy-start.1 = (f32[2,16,4096]{2,1,0:T(8,128)S(1)}, f32[2,16,4096]{2,1,0:T(8,128)}, u32[]{:S(2)}) copy-start(f32[2,16,4096]{2,1,0:T(8,128)} %places_ref.5) | copy-start | bytes 1572868
  0.0 13.8 %copy-start = (bf16[8,16,4096]{2,1,0:T(8,128)(2,1)S(1)}, bf16[8,16,4096]{2,1,0:T(8,128)(2,1)}, u32[]{:S(2)}) copy-start(bf16[8,16,4096]{2,1,0:T(8,128)(2,1)} %values_ref.5) | copy-start | bytes 3145732
  0.0 13.9 %copy-start.5 = (s32[16]{0:T(128)S(1)}, s32[16]{0:T(128)}, u32[]{:S(2)}) copy-start(s32[16]{0:T(128)} %param.11) | copy-start | bytes 196
  0.0 13.9 %copy-start.3 = (s32[16]{0:T(128)S(1)}, s32[16]{0:T(128)}, u32[]{:S(2)}) copy-start(s32[16]{0:T(128)} %param.10) | copy-start | bytes 196
  0.0 13.9 %copy-start.4 = (s32[16]{0:T(128)S(1)}, s32[16]{0:T(128)}, u32[]{:S(2)}) copy-start(s32[16]{0:T(128)} %param.9) | copy-start | bytes 196
  0.0 13.9 %copy-start.2 = (s32[16,1]{0,1:T(1,128)S(1)}, s32[16,1]{0,1:T(1,128)}, u32[]{:S(2)}) copy-start(s32[16,1]{0,1:T(1,128)} %param.8) | copy-start | bytes 196
  10.8 9.4 %collective-permute-start = (bf16[2,4,128,128]{3,2,1,0:T(8,128)(2,1)S(1)}, bf16[2,4,128,128]{3,2,1,0:T(8,128)(2,1)S(1)}, u32[]{:S(2)}, u32[]{:S(2)}) collective-permute-start(bf16[2,4,128,128]{3,2,1,0:T(8,128)(2,1)S(1)} %get-tuple-element.21), channel_id=1, source_target_pairs={{0,1},{1,0},{2,3},{3,2},{4,5},{5,4},{6,7},{7,6},{8,9},{9,8},{10,11... | collective-permute-start | bytes 786440 | tf_op jit(solution)/shard_map/ppermute | solution.py:185
  18.7 1.2 %collective-permute-start.1 = (bf16[16,16]{1,0:T(8,128)(2,1)S(1)}, bf16[16,16]{1,0:T(8,128)(2,1)S(1)}, u32[]{:S(2)}, u32[]{:S(2)}) collective-permute-start(bf16[16,16]{1,0:T(8,128)(2,1)S(1)} %get-tuple-element.23.numbers_ref), channel_id=1, source_target_pairs={{0,4},{4,0},{8,12},{12,8},{16,20},{20,16},{24,28},{28,24},{1,5},{5... | collective-permute-start | bytes 1544 | tf_op jit(solution)/shard_map/ppermute | solution.py:185
  20.2 9.3 %collective-permute-start.2 = (bf16[1,4,128,128]{3,2,1,0:T(8,128)(2,1)S(1)}, bf16[1,4,128,128]{3,2,1,0:T(8,128)(2,1)S(1)}, u32[]{:S(2)}, u32[]{:S(2)}) collective-permute-start(bf16[1,4,128,128]{3,2,1,0:T(8,128)(2,1)S(1)} %get-tuple-element.25.rest_0_), channel_id=1, source_target_pairs={{0,2},{1,3},{2,0},{3,1},{4,6},{5,7},{6,4},{7,5},{8,10},{9,11},{10,... | collective-permute-start | bytes 393224 | tf_op jit(solution)/shard_map/ppermute | solution.py:185
  27.9 7.8 %collective-permute-start.6 = (bf16[2,4,128,128]{3,2,1,0:T(8,128)(2,1)S(1)}, bf16[2,4,128,128]{3,2,1,0:T(8,128)(2,1)S(1)}, u32[]{:S(2)}, u32[]{:S(2)}) collective-permute-start(bf16[2,4,128,128]{3,2,1,0:T(8,128)(2,1)S(1)} %get-tuple-element.29), channel_id=1, source_target_pairs={{0,1},{1,0},{2,3},{3,2},{4,5},{5,4},{6,7},{7,6},{8,9},{9,8},{10,11... | collective-permute-start | bytes 786440 | tf_op jit(solution)/shard_map/ppermute | solution.py:185
  30.0 6.6 %collective-permute-start.5 = (bf16[528,128]{1,0:T(8,128)(2,1)S(1)}, bf16[528,128]{1,0:T(8,128)(2,1)S(1)}, u32[]{:S(2)}, u32[]{:S(2)}) collective-permute-start(bf16[528,128]{1,0:T(8,128)(2,1)S(1)} %shard_map.67.rest_0_), channel_id=1, source_target_pairs={{0,24},{4,28},{8,16},{12,20},{16,8},{20,12},{24,0},{28,4},{1,25},{... | collective-permute-start | bytes 405512 | tf_op jit(solution)/shard_map/ppermute | solution.py:185
  32.5 6.5 %collective-permute-start.4 = (bf16[528,128]{1,0:T(8,128)(2,1)S(1)}, bf16[528,128]{1,0:T(8,128)(2,1)S(1)}, u32[]{:S(2)}, u32[]{:S(2)}) collective-permute-start(bf16[528,128]{1,0:T(8,128)(2,1)S(1)} %shard_map.67.rest_0_), channel_id=1, source_target_pairs={{0,16},{4,20},{8,24},{12,28},{16,0},{20,4},{24,8},{28,12},{1,17},{... | collective-permute-start | bytes 405512 | tf_op jit(solution)/shard_map/ppermute | solution.py:185
  33.0 6.1 %collective-permute-start.3 = (bf16[528,128]{1,0:T(8,128)(2,1)S(1)}, bf16[528,128]{1,0:T(8,128)(2,1)S(1)}, u32[]{:S(2)}, u32[]{:S(2)}) collective-permute-start(bf16[528,128]{1,0:T(8,128)(2,1)S(1)} %shard_map.67.rest_0_), channel_id=1, source_target_pairs={{0,8},{4,12},{8,0},{12,4},{16,24},{20,28},{24,16},{28,20},{1,9},{5... | collective-permute-start | bytes 405512 | tf_op jit(solution)/shard_map/ppermute | solution.py:185
  35.8 7.8 %collective-permute-start.7 = (bf16[1,4,128,128]{3,2,1,0:T(8,128)(2,1)S(1)}, bf16[1,4,128,128]{3,2,1,0:T(8,128)(2,1)S(1)}, u32[]{:S(2)}, u32[]{:S(2)}) collective-permute-start(bf16[1,4,128,128]{3,2,1,0:T(8,128)(2,1)S(1)} %get-tuple-element.31), channel_id=1, source_target_pairs={{0,2},{1,3},{2,0},{3,1},{4,6},{5,7},{6,4},{7,5},{8,10},{9,11},{10,... | collective-permute-start | bytes 393224 | tf_op jit(solution)/shard_map/ppermute | solution.py:185
  44.1 8.4 %collective-permute-start.10 = (bf16[512,128]{1,0:T(8,128)(2,1)S(1)}, bf16[512,128]{1,0:T(8,128)(2,1)S(1)}, u32[]{:S(2)}, u32[]{:S(2)}) collective-permute-start(bf16[512,128]{1,0:T(8,128)(2,1)S(1)} %get-tuple-element.34), channel_id=1, source_target_pairs={{0,24},{4,28},{8,16},{12,20},{16,8},{20,12},{24,0},{28,4},{1,25},{... | collective-permute-start | bytes 393224 | tf_op jit(solution)/shard_map/ppermute | solution.py:185
  46.6 5.9 %collective-permute-start.9 = (bf16[512,128]{1,0:T(8,128)(2,1)S(1)}, bf16[512,128]{1,0:T(8,128)(2,1)S(1)}, u32[]{:S(2)}, u32[]{:S(2)}) collective-permute-start(bf16[512,128]{1,0:T(8,128)(2,1)S(1)} %get-tuple-element.34), channel_id=1, source_target_pairs={{0,16},{4,20},{8,24},{12,28},{16,0},{20,4},{24,8},{28,12},{1,17},{... | collective-permute-start | bytes 393224 | tf_op jit(solution)/shard_map/ppermute | solution.py:185
  47.1 5.4 %collective-permute-start.8 = (bf16[512,128]{1,0:T(8,128)(2,1)S(1)}, bf16[512,128]{1,0:T(8,128)(2,1)S(1)}, u32[]{:S(2)}, u32[]{:S(2)}) collective-permute-start(bf16[512,128]{1,0:T(8,128)(2,1)S(1)} %get-tuple-element.34), channel_id=1, source_target_pairs={{0,8},{4,12},{8,0},{12,4},{16,24},{20,28},{24,16},{28,20},{1,9},{5... | collective-permute-start | bytes 393224 | tf_op jit(solution)/shard_map/ppermute | solution.py:185
  52.6 2.7 %collective-permute-start.11 = (bf16[8,512,128]{2,1,0:T(8,128)(2,1)S(1)}, bf16[8,512,128]{2,1,0:T(8,128)(2,1)S(1)}, u32[]{:S(2)}, u32[]{:S(2)}) collective-permute-start(bf16[8,512,128]{2,1,0:T(8,128)(2,1)S(1)} %bitcast_dynamic-update-slice_fusion.near_ref), channel_id=1, source_target_pairs={{0,4},{4,0},{8,12},{12,8},{16,20},{20,16},{24,28},{28,24},{1,5},{5... | collective-permute-start | bytes 3145736 | tf_op jit(solution)/shard_map/ppermute | solution.py:185
